TPU v7x, 512 devices: a whole 4x4x16 slice. The times are simulated.
512 devices in a mesh: section: 8 (over z_hi, x), expert: 64 (over y, z_lo, core).
Axes of the slice: x: 4, y: 4, z: 16 (z_hi: 2, z_lo: 8; z = z_hi * 8 + z_lo), core: 2. Of those that a mesh axis runs over, the one named last changes fastest.
Arguments:
- hidden: bfloat16 [8, 512, 7168], P('section', 'expert'), may hold values from -6 to 6
- norm_gain: float32 [8, 7168], P('section'), may hold values from 0.25 to 1.75
- w_up: bfloat16 [8, 7168, 8192], P('section', None, 'expert'), may hold values from -0.0625 to 0.0625
- w_down: bfloat16 [8, 8192, 7168], P('section', 'expert'), may hold values from -0.1875 to 0.1875
- expert_ids: int32 [8, 2, 512, 2], P('section', None, 'expert'), may hold values from 0 to 7, all different within a row; in each aligned block of 8 rows (0 to 7, 8 to 15, ..., all dimensions but the last counted through in order) at most 4 rows name the same one
- route_gates: float32 [8, 2, 512, 2], P('section', None, 'expert'), may hold values from 0.25 to 1.5
Outputs:
- advanced: bfloat16 [8, 512, 7168], P('section', 'expert')
Inputs may be any that keep to these rules, and one draw needn't show every extreme that they name: `expert_ids`: the 2 ids of a row differ. In each aligned block of 8 rows (the rows of one device in one pass) no expert is named by more than 4 rows; some expert is named by exactly 4 rows.
All inputs are finite; a program needn't handle non-finite values.
Results may differ from a plain program's by a relative error of at most 0.0085.
Values may be sent and summed in bfloat16 or wider, within the bound.
No kernel may reach another device: no remote copies, remote signals or barrier semaphores. Data moves between devices by JAX's collectives and lax.ppermute only.
A program may use at most 64 MiB of HBM per device.

v0:
```python
import jax
import jax.numpy as jnp
from jax import lax
from jax.sharding import PartitionSpec as P

HID = 1024
HID_DEV = 128


def shifted(value, axis, by):
    count = lax.axis_size(axis)
    return lax.ppermute(value, axis, [(i, (i + by) % count) for i in range(count)])


def rms_scale(current, gain_row):
    values = current.astype(jnp.float32)
    inverse_rms = lax.rsqrt(jnp.mean(values * values, axis=-1, keepdims=True) + 1e-06)
    return (values, (values * inverse_rms * gain_row).astype(jnp.bfloat16))


def route_tables(route_ids, gate_values, expert_count, capacity):
    row_count, top_count = route_ids.shape
    flat_ids = route_ids.reshape(-1)
    onehot = (flat_ids[:, None] == jnp.arange(expert_count, dtype=jnp.int32)[None, :]).astype(
        jnp.int32
    )
    earlier = jnp.cumsum(onehot, axis=0) - onehot
    slot_index = jnp.sum(earlier * onehot, axis=1)
    target = flat_ids * capacity + slot_index
    placed = (
        jnp.arange(expert_count * capacity, dtype=jnp.int32)[:, None] == target[None, :]
    ).astype(jnp.float32)
    owners = (
        (jnp.arange(row_count * top_count, dtype=jnp.int32) // top_count)[:, None]
        == jnp.arange(row_count, dtype=jnp.int32)[None, :]
    ).astype(jnp.float32)
    picker = jnp.dot(placed, owners, precision=lax.Precision.HIGHEST)
    weigher = jnp.dot(
        placed * gate_values.reshape(-1)[None, :], owners, precision=lax.Precision.HIGHEST
    )
    return (picker.astype(jnp.bfloat16), weigher)


def expert_apply(received, up_slice, down_slice):
    flat_rows = received.reshape(-1, received.shape[-1])
    upward = jnp.dot(flat_rows, up_slice, preferred_element_type=jnp.float32)
    active = jax.nn.silu(upward).astype(jnp.bfloat16)
    partial_out = jnp.dot(active, down_slice, preferred_element_type=jnp.float32).astype(
        jnp.bfloat16
    )
    return partial_out.reshape(received.shape)


def body(hidden, norm_gain, w_up, w_down, expert_ids, route_gates):
    model_width = hidden.shape[-1]
    group_size = HID // HID_DEV
    devices = lax.axis_size("expert")
    expert_count = devices // group_size
    row_count = hidden.shape[1]
    top_count = expert_ids.shape[-1]
    capacity = min(row_count, (row_count * top_count + expert_count - 1) // expert_count + 2)
    up_slice = w_up[0]
    down_slice = w_down[0]
    gain_row = norm_gain[0]
    current = hidden[0]
    for pass_index in range(expert_ids.shape[1]):
        values, normed = rms_scale(current, gain_row)
        picker, weigher = route_tables(
            expert_ids[0, pass_index], route_gates[0, pass_index], expert_count, capacity
        )
        packed = jnp.dot(picker, normed, preferred_element_type=jnp.float32).astype(jnp.bfloat16)
        copies = jnp.broadcast_to(
            packed.reshape(expert_count, 1, capacity, model_width),
            (expert_count, group_size, capacity, model_width),
        )
        copies = copies.reshape(devices, capacity, model_width)
        partial_out = expert_apply(
            lax.all_to_all(copies, "expert", split_axis=0, concat_axis=0, tiled=True),
            up_slice,
            down_slice,
        )
        returned = lax.all_to_all(partial_out, "expert", split_axis=0, concat_axis=0, tiled=True)
        outputs = jnp.sum(
            returned.reshape(expert_count, group_size, capacity, model_width).astype(jnp.float32),
            axis=1,
        )
        mixture = jnp.dot(
            weigher.T,
            outputs.reshape(expert_count * capacity, model_width),
            precision=lax.Precision.HIGHEST,
            preferred_element_type=jnp.float32,
        )
        updated = (values + mixture).astype(jnp.bfloat16)
        current = shifted(updated, "section", 1)
    return current[None]


def solution(mesh):
    placed = (
        P("section", "expert", None),
        P("section", None),
        P("section", None, "expert"),
        P("section", "expert", None),
        P("section", None, "expert", None),
        P("section", None, "expert", None),
    )
    return jax.shard_map(
        body, mesh=mesh, in_specs=placed, out_specs=P("section", "expert", None), check_vma=False
    )
```

profile of v0, /device:TPU:7, one launch (start us, length us, event | category | flops | bytes accessed | tf_op | source)
XLA Modules:
  0.0 792.8 jit_solution(1636744962436111728)
XLA Ops:
  1.3 1.1 fusion.11
  2.6 1.2 convolution_convert_fusion.3
  4.0 1.1 broadcast_in_dim.11
  5.1 179.7 %all_to_all.20 = bf16[64,4,7168]{2,1,0:T(4,128)(2,1)} all-to-all(bf16[64,4,7168]{2,1,0:T(4,128)(2,1)S(1)} %bitcast.52), channel_id=1, replica_groups=mesh['section'=8,'expert'=64] {'expert'}, dimensions={0} | all-to-all | bytes 7340032 | tf_op jit(solution)/shard_map/all_to_all | solution.py:78
  184.8 6.7 reshape.86
  191.5 6.6 convolution_convert_fusion.1
  198.1 7.0 reshape.87
  205.1 8.7 %all-to-all-start.1 = ((bf16[64,4,7168]{2,1,0:T(4,128)(2,1)}), bf16[64,4,7168]{2,1,0:T(4,128)(2,1)}, u32[]{:S(2)}, u32[]{:S(2)}) async-start(bf16[64,4,7168]{2,1,0:T(4,128)(2,1)} %reshape.87), calls=%async_computation.1 | async-start | bytes 7340032 | tf_op jit(solution)/shard_map/all_to_all | solution.py:82
  214.7 162.5 %all-to-all-done.1 = bf16[64,4,7168]{2,1,0:T(4,128)(2,1)} async-done(((bf16[64,4,7168]{2,1,0:T(4,128)(2,1)}), bf16[64,4,7168]{2,1,0:T(4,128)(2,1)}, u32[]{:S(2)}, u32[]{:S(2)}) %all-to-all-start.1) | async-done | bytes 3670048 | tf_op jit(solution)/shard_map/all_to_all | solution.py:82
  377.2 4.8 convert_reduce_fusion.1
  382.0 1.5 reshape.88
  384.0 7.9 collective-permute-start
  392.1 5.8 collective-permute-done
  398.6 1.1 broadcast_in_dim.13
  399.7 172.2 %all_to_all.21 = bf16[64,4,7168]{2,1,0:T(4,128)(2,1)} all-to-all(bf16[64,4,7168]{2,1,0:T(4,128)(2,1)S(1)} %bitcast.53), channel_id=1, replica_groups=mesh['section'=8,'expert'=64] {'expert'}, dimensions={0} | all-to-all | bytes 7340032 | tf_op jit(solution)/shard_map/all_to_all | solution.py:78
  572.0 6.7 reshape.90
  578.7 6.6 convolution_convert_fusion
  585.3 7.0 reshape.91
  592.3 8.6 %all-to-all-start.3 = ((bf16[64,4,7168]{2,1,0:T(4,128)(2,1)}), bf16[64,4,7168]{2,1,0:T(4,128)(2,1)}, u32[]{:S(2)}, u32[]{:S(2)}) async-start(bf16[64,4,7168]{2,1,0:T(4,128)(2,1)} %reshape.91), calls=%async_computation.3 | async-start | bytes 7340032 | tf_op jit(solution)/shard_map/all_to_all | solution.py:82
  601.3 163.0 %all-to-all-done.3 = bf16[64,4,7168]{2,1,0:T(4,128)(2,1)} async-done(((bf16[64,4,7168]{2,1,0:T(4,128)(2,1)}), bf16[64,4,7168]{2,1,0:T(4,128)(2,1)}, u32[]{:S(2)}, u32[]{:S(2)}) %all-to-all-start.3) | async-done | bytes 3670048 | tf_op jit(solution)/shard_map/all_to_all | solution.py:82
  764.3 4.8 convert_reduce_fusion
  769.0 1.5 reshape.92
  771.1 14.9 %collective-permute-start.1 = (bf16[8,7168]{1,0:T(8,128)(2,1)S(1)}, bf16[8,7168]{1,0:T(8,128)(2,1)S(1)}, u32[]{:S(2)}, u32[]{:S(2)}) collective-permute-start(bf16[8,7168]{1,0:T(8,128)(2,1)S(1)} %fusion.1), channel_id=1, source_target_pairs={{0,64},{64,128},{128,192},{192,256},{256,320},{320,384},{384,448},... | collective-permute-start | bytes 344072 | tf_op jit(solution)/shard_map/ppermute | solution.py:12
  786.0 6.1 collective-permute-done.1
  (39 shorter events, 5.5 us)
Async XLA Ops:
  0.0 191.5 %copy-start = (bf16[1,128,7168]{2,1,0:T(8,128)(2,1)S(1)}, bf16[1,128,7168]{2,1,0:T(8,128)(2,1)}, u32[]{:S(2)}) copy-start(bf16[1,128,7168]{2,1,0:T(8,128)(2,1)} %param.9) | copy-start | bytes 5505028
  205.1 8.7 %copy-start.3 = (f32[1,2,8,2]{2,3,1,0:T(2,128)S(1)}, f32[1,2,8,2]{2,3,1,0:T(2,128)}, u32[]{:S(2)}) copy-start(f32[1,2,8,2]{2,3,1,0:T(2,128)} %param.11) | copy-start | bytes 388
  205.1 172.1 %all-to-all-start.1 = ((bf16[64,4,7168]{2,1,0:T(4,128)(2,1)}), bf16[64,4,7168]{2,1,0:T(4,128)(2,1)}, u32[]{:S(2)}, u32[]{:S(2)}) async-start(bf16[64,4,7168]{2,1,0:T(4,128)(2,1)} %reshape.87), calls=%async_computation.1 | async-start | bytes 7340032 | tf_op jit(solution)/shard_map/all_to_all | solution.py:82
  213.9 169.6 %copy-start.1 = (bf16[1,8,7168]{2,1,0:T(8,128)(2,1)S(1)}, bf16[1,8,7168]{2,1,0:T(8,128)(2,1)}, u32[]{:S(2)}) copy-start(bf16[1,8,7168]{2,1,0:T(8,128)(2,1)} %param.6) | copy-start | bytes 344068
  214.7 183.4 %copy-start.2 = (f32[1,7168]{1,0:T(1,128)S(1)}, f32[1,7168]{1,0:T(1,128)}, u32[]{:S(2)}) copy-start(f32[1,7168]{1,0:T(1,128)} %param.7) | copy-start | bytes 86020
  384.0 13.9 %collective-permute-start = (bf16[8,7168]{1,0:T(8,128)(2,1)S(1)}, bf16[8,7168]{1,0:T(8,128)(2,1)S(1)}, u32[]{:S(2)}, u32[]{:S(2)}) collective-permute-start(bf16[8,7168]{1,0:T(8,128)(2,1)S(1)} %fusion), channel_id=1, source_target_pairs={{0,64},{64,128},{128,192},{192,256},{256,320},{320,384},{384,448},... | collective-permute-start | bytes 344072 | tf_op jit(solution)/shard_map/ppermute | solution.py:12
  592.3 172.0 %all-to-all-start.3 = ((bf16[64,4,7168]{2,1,0:T(4,128)(2,1)}), bf16[64,4,7168]{2,1,0:T(4,128)(2,1)}, u32[]{:S(2)}, u32[]{:S(2)}) async-start(bf16[64,4,7168]{2,1,0:T(4,128)(2,1)} %reshape.91), calls=%async_computation.3 | async-start | bytes 7340032 | tf_op jit(solution)/shard_map/all_to_all | solution.py:82
  771.1 21.0 %collective-permute-start.1 = (bf16[8,7168]{1,0:T(8,128)(2,1)S(1)}, bf16[8,7168]{1,0:T(8,128)(2,1)S(1)}, u32[]{:S(2)}, u32[]{:S(2)}) collective-permute-start(bf16[8,7168]{1,0:T(8,128)(2,1)S(1)} %fusion.1), channel_id=1, source_target_pairs={{0,64},{64,128},{128,192},{192,256},{256,320},{320,384},{384,448},... | collective-permute-start | bytes 344072 | tf_op jit(solution)/shard_map/ppermute | solution.py:12
where the time goes:
time: 803 us; the launch traced here: 793 us
  blocking collectives  352 us (44%)
  waiting for transfers between devices  337 us (42%)
  starting transfers between devices  40.1 us (5%)
  local copies, waits for them, and re-layouts  35.2 us (4%)
  matrix products  16.6 us (2%)
  other arithmetic  11.4 us (1%)
    all_to_all x2, blocking collectives, body(): lax.all_to_all(copies, 'expert', split_axis=0, concat_axis=0, tiled=True)  352 us
    all_to_all x2, waiting for transfers between devices, body(): lax.all_to_all(partial_out, 'expert', split_axis=0, concat_axis=0, tiled=...  325 us
    ppermute x2, starting transfers between devices, shifted(): lax.ppermute(value, axis, [(i, (i + by) % count) for i in range(count)])  22.8 us
    all_to_all x2, starting transfers between devices, body(): lax.all_to_all(partial_out, 'expert', split_axis=0, concat_axis=0, tiled=...  17.3 us
  transfers between devices with their start and end apart: 4, of which 4 were waited for; matrix products, arithmetic and copies ran while one was open for 0% of the time, Pallas kernels for 0%

commit v1 on v0

--- a/solution.py
+++ b/solution.py
@@ -21,11 +21,9 @@
 def route_tables(route_ids, gate_values, expert_count, capacity):
     row_count, top_count = route_ids.shape
     flat_ids = route_ids.reshape(-1)
-    onehot = (flat_ids[:, None] == jnp.arange(expert_count, dtype=jnp.int32)[None, :]).astype(
-        jnp.int32
-    )
-    earlier = jnp.cumsum(onehot, axis=0) - onehot
-    slot_index = jnp.sum(earlier * onehot, axis=1)
+    order = jnp.arange(row_count * top_count, dtype=jnp.int32)
+    same = (flat_ids[:, None] == flat_ids[None, :]) & (order[None, :] < order[:, None])
+    slot_index = jnp.sum(same.astype(jnp.int32), axis=1)
     target = flat_ids * capacity + slot_index
     placed = (
         jnp.arange(expert_count * capacity, dtype=jnp.int32)[:, None] == target[None, :]

time: 803 us -> 803 us (level)
  no operation moved by 1% of the time
where the time goes in v1:
time: 803 us; the launch traced here: 793 us
  blocking collectives  352 us (44%)
  waiting for transfers between devices  337 us (42%)
  starting transfers between devices  40.1 us (5%)
  local copies, waits for them, and re-layouts  35.2 us (4%)
  matrix products  16.9 us (2%)
  other arithmetic  11.2 us (1%)
    all_to_all x2, blocking collectives, body(): lax.all_to_all(copies, 'expert', split_axis=0, concat_axis=0, tiled=True)  352 us
    all_to_all x2, waiting for transfers between devices, body(): lax.all_to_all(partial_out, 'expert', split_axis=0, concat_axis=0, tiled=...  326 us
    ppermute x2, starting transfers between devices, shifted(): lax.ppermute(value, axis, [(i, (i + by) % count) for i in range(count)])  22.8 us
    all_to_all x2, starting transfers between devices, body(): lax.all_to_all(partial_out, 'expert', split_axis=0, concat_axis=0, tiled=...  17.3 us
  transfers between devices with their start and end apart: 4, of which 4 were waited for; matrix products, arithmetic and copies ran while one was open for 0% of the time, Pallas kernels for 0%

profile of v1, /device:TPU:7, one launch (start us, length us, event | category | flops | bytes accessed | tf_op | source)
XLA Modules:
  0.0 792.7 jit_solution(501124395621847048)
XLA Ops:
  1.2 1.1 fusion.11
  2.5 1.2 convolution_convert_fusion.3
  4.0 1.1 broadcast_in_dim.11
  5.1 179.7 %all_to_all.20 = bf16[64,4,7168]{2,1,0:T(4,128)(2,1)} all-to-all(bf16[64,4,7168]{2,1,0:T(4,128)(2,1)S(1)} %bitcast.52), channel_id=1, replica_groups=mesh['section'=8,'expert'=64] {'expert'}, dimensions={0} | all-to-all | bytes 7340032 | tf_op jit(solution)/shard_map/all_to_all | solution.py:76
  184.7 6.7 reshape.88
  191.5 6.6 convolution_convert_fusion.1
  198.1 7.0 reshape.89
  205.1 8.7 %all-to-all-start.1 = ((bf16[64,4,7168]{2,1,0:T(4,128)(2,1)}), bf16[64,4,7168]{2,1,0:T(4,128)(2,1)}, u32[]{:S(2)}, u32[]{:S(2)}) async-start(bf16[64,4,7168]{2,1,0:T(4,128)(2,1)} %reshape.89), calls=%async_computation.1 | async-start | bytes 7340032 | tf_op jit(solution)/shard_map/all_to_all | solution.py:80
  214.6 162.6 %all-to-all-done.1 = bf16[64,4,7168]{2,1,0:T(4,128)(2,1)} async-done(((bf16[64,4,7168]{2,1,0:T(4,128)(2,1)}), bf16[64,4,7168]{2,1,0:T(4,128)(2,1)}, u32[]{:S(2)}, u32[]{:S(2)}) %all-to-all-start.1) | async-done | bytes 3670048 | tf_op jit(solution)/shard_map/all_to_all | solution.py:80
  377.2 4.8 convert_reduce_fusion.1
  381.9 1.5 reshape.90
  384.0 7.9 collective-permute-start
  392.1 5.7 collective-permute-done
  398.6 1.1 broadcast_in_dim.13
  399.7 172.2 %all_to_all.21 = bf16[64,4,7168]{2,1,0:T(4,128)(2,1)} all-to-all(bf16[64,4,7168]{2,1,0:T(4,128)(2,1)S(1)} %bitcast.53), channel_id=1, replica_groups=mesh['section'=8,'expert'=64] {'expert'}, dimensions={0} | all-to-all | bytes 7340032 | tf_op jit(solution)/shard_map/all_to_all | solution.py:76
  571.9 6.7 reshape.92
  578.7 6.6 convolution_convert_fusion
  585.3 7.0 reshape.93
  592.3 8.6 %all-to-all-start.3 = ((bf16[64,4,7168]{2,1,0:T(4,128)(2,1)}), bf16[64,4,7168]{2,1,0:T(4,128)(2,1)}, u32[]{:S(2)}, u32[]{:S(2)}) async-start(bf16[64,4,7168]{2,1,0:T(4,128)(2,1)} %reshape.93), calls=%async_computation.3 | async-start | bytes 7340032 | tf_op jit(solution)/shard_map/all_to_all | solution.py:80
  601.3 163.0 %all-to-all-done.3 = bf16[64,4,7168]{2,1,0:T(4,128)(2,1)} async-done(((bf16[64,4,7168]{2,1,0:T(4,128)(2,1)}), bf16[64,4,7168]{2,1,0:T(4,128)(2,1)}, u32[]{:S(2)}, u32[]{:S(2)}) %all-to-all-start.3) | async-done | bytes 3670048 | tf_op jit(solution)/shard_map/all_to_all | solution.py:80
  764.2 4.8 convert_reduce_fusion
  769.0 1.5 reshape.94
  771.0 14.9 %collective-permute-start.1 = (bf16[8,7168]{1,0:T(8,128)(2,1)S(1)}, bf16[8,7168]{1,0:T(8,128)(2,1)S(1)}, u32[]{:S(2)}, u32[]{:S(2)}) collective-permute-start(bf16[8,7168]{1,0:T(8,128)(2,1)S(1)} %fusion.1), channel_id=1, source_target_pairs={{0,64},{64,128},{128,192},{192,256},{256,320},{320,384},{384,448},... | collective-permute-start | bytes 344072 | tf_op jit(solution)/shard_map/ppermute | solution.py:12
  786.0 6.1 collective-permute-done.1
  (35 shorter events, 5.5 us)
Async XLA Ops:
  0.0 191.5 %copy-start = (bf16[1,128,7168]{2,1,0:T(8,128)(2,1)S(1)}, bf16[1,128,7168]{2,1,0:T(8,128)(2,1)}, u32[]{:S(2)}) copy-start(bf16[1,128,7168]{2,1,0:T(8,128)(2,1)} %param.9) | copy-start | bytes 5505028
  205.1 8.7 %copy-start.3 = (f32[1,2,8,2]{2,3,1,0:T(2,128)S(1)}, f32[1,2,8,2]{2,3,1,0:T(2,128)}, u32[]{:S(2)}) copy-start(f32[1,2,8,2]{2,3,1,0:T(2,128)} %param.11) | copy-start | bytes 388
  205.1 172.1 %all-to-all-start.1 = ((bf16[64,4,7168]{2,1,0:T(4,128)(2,1)}), bf16[64,4,7168]{2,1,0:T(4,128)(2,1)}, u32[]{:S(2)}, u32[]{:S(2)}) async-start(bf16[64,4,7168]{2,1,0:T(4,128)(2,1)} %reshape.89), calls=%async_computation.1 | async-start | bytes 7340032 | tf_op jit(solution)/shard_map/all_to_all | solution.py:80
  213.8 169.6 %copy-start.1 = (bf16[1,8,7168]{2,1,0:T(8,128)(2,1)S(1)}, bf16[1,8,7168]{2,1,0:T(8,128)(2,1)}, u32[]{:S(2)}) copy-start(bf16[1,8,7168]{2,1,0:T(8,128)(2,1)} %param.6) | copy-start | bytes 344068
  214.6 183.4 %copy-start.2 = (f32[1,7168]{1,0:T(1,128)S(1)}, f32[1,7168]{1,0:T(1,128)}, u32[]{:S(2)}) copy-start(f32[1,7168]{1,0:T(1,128)} %param.7) | copy-start | bytes 86020
  384.0 13.9 %collective-permute-start = (bf16[8,7168]{1,0:T(8,128)(2,1)S(1)}, bf16[8,7168]{1,0:T(8,128)(2,1)S(1)}, u32[]{:S(2)}, u32[]{:S(2)}) collective-permute-start(bf16[8,7168]{1,0:T(8,128)(2,1)S(1)} %fusion), channel_id=1, source_target_pairs={{0,64},{64,128},{128,192},{192,256},{256,320},{320,384},{384,448},... | collective-permute-start | bytes 344072 | tf_op jit(solution)/shard_map/ppermute | solution.py:12
  592.3 172.0 %all-to-all-start.3 = ((bf16[64,4,7168]{2,1,0:T(4,128)(2,1)}), bf16[64,4,7168]{2,1,0:T(4,128)(2,1)}, u32[]{:S(2)}, u32[]{:S(2)}) async-start(bf16[64,4,7168]{2,1,0:T(4,128)(2,1)} %reshape.93), calls=%async_computation.3 | async-start | bytes 7340032 | tf_op jit(solution)/shard_map/all_to_all | solution.py:80
  771.0 21.0 %collective-permute-start.1 = (bf16[8,7168]{1,0:T(8,128)(2,1)S(1)}, bf16[8,7168]{1,0:T(8,128)(2,1)S(1)}, u32[]{:S(2)}, u32[]{:S(2)}) collective-permute-start(bf16[8,7168]{1,0:T(8,128)(2,1)S(1)} %fusion.1), channel_id=1, source_target_pairs={{0,64},{64,128},{128,192},{192,256},{256,320},{320,384},{384,448},... | collective-permute-start | bytes 344072 | tf_op jit(solution)/shard_map/ppermute | solution.py:12

commit v2 on v1

v2 whole, which is shorter than its diff:
```python
import jax
import jax.numpy as jnp
from jax import lax
from jax.sharding import PartitionSpec as P

HID = 1024
HID_DEV = 128
GROUP = HID // HID_DEV
CAP = 4
HALVES = 2
LANES = 128


def groups(count):
    span = GROUP * HALVES
    same_expert = [[first + j for j in range(GROUP)] for first in range(0, count, GROUP)]
    same_row = [[first + k for k in range(span)] for first in range(0, count, span)]
    same_slice = [[first + k for first in range(0, count, span)] for k in range(span)]
    return same_expert, same_row, same_slice


def exchange(value, within):
    return lax.all_to_all(
        value, "expert", split_axis=0, concat_axis=0, axis_index_groups=within, tiled=True
    )


def other_half(value):
    count = lax.axis_size("expert")
    return lax.ppermute(value, "expert", [(i, i ^ GROUP) for i in range(count)])


def next_section(value):
    count = lax.axis_size("section")
    return lax.ppermute(value, "section", [(i, (i + 1) % count) for i in range(count)])


def head(value):
    return lax.reduce_precision(value, exponent_bits=8, mantissa_bits=7)


def in_three(value):
    first = head(value)
    second = head(value - first)
    third = head(value - first - second)
    return [part.astype(jnp.bfloat16) for part in (first, second, third)]


def tables(ids, gates, half, peers, rows_dev):
    rows = ids.shape[0]
    wanted = 2 * jnp.arange(peers, dtype=jnp.int32) + half
    hit = ids.T[None, :, :] == wanted[:, None, None]
    routed = jnp.any(hit, axis=1)
    weight = jnp.sum(jnp.where(hit, gates.T[None, :, :], 0.0), axis=1)
    at = jnp.arange(rows, dtype=jnp.int32)
    before = (at[:, None] < at[None, :]) & (at[:, None] // rows_dev == at[None, :] // rows_dev)
    rank = jnp.dot(
        routed.astype(jnp.bfloat16), before.astype(jnp.bfloat16), preferred_element_type=jnp.float32
    ).astype(jnp.int32)
    slots = rows // rows_dev * CAP
    slot = jnp.arange(slots, dtype=jnp.int32)
    mine = (slot[:, None] // CAP == at[None, :] // rows_dev)[None]
    picked = mine & routed[:, None, :] & (rank[:, None, :] == (slot % CAP)[None, :, None])
    weigher = jnp.where(picked, weight[:, None, :], 0.0)
    shape = (peers * slots, rows)
    return picked.astype(jnp.bfloat16).reshape(shape), weigher.reshape(shape)


def body(hidden, norm_gain, w_up, w_down, expert_ids, route_gates):
    width = hidden.shape[-1]
    rows_dev = hidden.shape[1]
    passes, top = expert_ids.shape[1], expert_ids.shape[-1]
    count = lax.axis_size("expert")
    peers = count // (GROUP * HALVES)
    part = width // GROUP
    block = GROUP * rows_dev
    same_expert, same_row, same_slice = groups(count)
    place = lax.axis_index("expert")
    half = place // GROUP % HALVES

    facts = [expert_ids[0].astype(jnp.bfloat16)] + in_three(route_gates[0])
    facts = jnp.stack(facts).transpose(2, 0, 1, 3).reshape(rows_dev, -1)
    facts = jnp.pad(facts, ((0, 0), (0, LANES - facts.shape[1])))
    sliced = hidden[0].reshape(rows_dev, GROUP, part).transpose(1, 0, 2)
    sliced = jnp.concatenate(
        [sliced, jnp.broadcast_to(facts[None], (GROUP, rows_dev, LANES))], axis=2
    )
    arrived = exchange(jnp.concatenate([sliced, sliced]), same_row)
    arrived = arrived.reshape(HALVES, block, part + LANES)
    arrived = lax.dynamic_slice_in_dim(jnp.concatenate([arrived, arrived]), half, HALVES, 0)
    arrived = arrived.reshape(HALVES * block, part + LANES)
    rows = arrived[:, :part]
    facts = arrived[:, part:].astype(jnp.float32)
    routes = facts[:, : 4 * passes * top].reshape(HALVES * block, 4, passes, top)

    up = exchange(w_up[0].reshape(GROUP, part, HID_DEV), same_expert)
    up = up.transpose(1, 0, 2).reshape(part, HID)
    down = exchange(w_down[0].reshape(HID_DEV, GROUP, part).transpose(1, 0, 2), same_expert)
    down = down.reshape(HID, part)
    gain = lax.dynamic_slice_in_dim(norm_gain[0], place % GROUP * part, part, 0)

    for t in range(passes):
        ids = routes[:, 0, t].astype(jnp.int32)
        gates = jnp.sum(routes[:, 1:, t], axis=1)
        picker, weigher = tables(ids, gates, half, peers, rows_dev)
        slots = jnp.dot(picker, rows, preferred_element_type=jnp.float32).astype(jnp.bfloat16)
        slots = exchange(slots, same_slice)
        values = slots.astype(jnp.float32)
        squares = jnp.sum(values * values, axis=1)
        partial = jnp.dot(
            (values * gain).astype(jnp.bfloat16), up, preferred_element_type=jnp.float32
        ).astype(jnp.bfloat16)
        held = slots.shape[0]
        partial = partial.reshape(held, GROUP, HID_DEV).transpose(1, 0, 2)
        big = head(squares)
        beside = jnp.stack([big, squares - big]).astype(jnp.bfloat16).reshape(-1, LANES)
        beside = jnp.pad(beside, ((0, 16 - beside.shape[0]), (0, 0)))
        beside = jnp.broadcast_to(beside[None], (GROUP, 16, LANES))
        sums = jnp.sum(
            exchange(jnp.concatenate([partial, beside], axis=1), same_expert).astype(jnp.float32),
            axis=0,
        )
        squares = jnp.sum(sums[held:].reshape(-1)[: 2 * held].reshape(2, held), axis=0)
        scale = lax.rsqrt(squares / width + 1e-06)
        active = jax.nn.silu(sums[:held] * scale[:, None]).astype(jnp.bfloat16)
        active = lax.all_gather(active, "expert", axis_index_groups=same_expert)
        active = active.transpose(1, 0, 2).reshape(held, HID)
        outputs = jnp.dot(active, down, preferred_element_type=jnp.float32).astype(jnp.bfloat16)
        outputs = exchange(outputs, same_slice)
        mixture = jnp.dot(
            weigher.T,
            outputs.astype(jnp.float32),
            precision=lax.Precision.HIGHEST,
            preferred_element_type=jnp.float32,
        )
        own = rows[:block].astype(jnp.float32) + mixture[:block]
        other = mixture[block:].astype(jnp.bfloat16)
        if t + 1 < passes:
            own = (own + other_half(other).astype(jnp.float32)).astype(jnp.bfloat16)
            own = next_section(own)
            rows = jnp.concatenate([own, other_half(own)])
        else:
            own = own.astype(jnp.bfloat16)
            both = lax.dynamic_slice_in_dim(jnp.stack([own, other, own]), half, HALVES, 0)
            both = exchange(both.reshape(HALVES * GROUP, rows_dev, part), same_row)
            both = both.reshape(HALVES, GROUP, rows_dev, part).astype(jnp.float32)
            done = jnp.sum(both, axis=0).astype(jnp.bfloat16)
            done = next_section(done.transpose(1, 0, 2).reshape(rows_dev, width))
    return done[None]


def solution(mesh):
    placed = (
        P("section", "expert", None),
        P("section", None),
        P("section", None, "expert"),
        P("section", "expert", None),
        P("section", None, "expert", None),
        P("section", None, "expert", None),
    )
    return jax.shard_map(
        body, mesh=mesh, in_specs=placed, out_specs=P("section", "expert", None), check_vma=False
    )
```

time: 803 us -> 350 us (0.44)
  the two profiles are of different devices: /device:TPU:7 before, /device:TPU:65 now
where the time goes in v2:
time: 350 us; the launch traced here: 349 us
  blocking collectives  147 us (42%)
  waiting for transfers between devices  124 us (35%)
  starting transfers between devices  54.6 us (16%)
  local copies, waits for them, and re-layouts  10 us (3%)
  matrix products  7.88 us (2%)
  other arithmetic  5.71 us (2%)
    all_to_all x4, blocking collectives, exchange(): lax.all_to_all(value, 'expert', split_axis=0, concat_axis=0, axis_index_g...  81.8 us
    all_to_all x6, waiting for transfers between devices, exchange(): lax.all_to_all(value, 'expert', split_axis=0, concat_axis=0, axis_index_g...  78.3 us
    all_gather x2, blocking collectives, body(): active = lax.all_gather(active, 'expert', axis_index_groups=same_expert)  65 us
    all_to_all x6, starting transfers between devices, exchange(): lax.all_to_all(value, 'expert', split_axis=0, concat_axis=0, axis_index_g...  39 us
    ppermute x2, waiting for transfers between devices, next_section(): lax.ppermute(value, 'section', [(i, (i + 1) % count) for i in range(count)])  36.6 us
    ppermute x2, starting transfers between devices, other_half(): return lax.ppermute(value, 'expert', [(i, i ^ GROUP) for i in range(count)])  10.6 us
    ppermute x2, waiting for transfers between devices, other_half(): return lax.ppermute(value, 'expert', [(i, i ^ GROUP) for i in range(count)])  8.63 us
  transfers between devices with their start and end apart: 10, of which 9 were waited for; matrix products, arithmetic and copies ran while one was open for 2% of the time, Pallas kernels for 0%

profile of v2, /device:TPU:65, one launch (start us, length us, event | category | flops | bytes accessed | tf_op | source)
XLA Modules:
  0.0 349.0 jit_solution(2310379854559019846)
XLA Ops:
  3.2 12.5 %all-to-all-start = ((bf16[16,8,1024]{2,1,0:T(8,128)(2,1)}), bf16[16,8,1024]{2,1,0:T(8,128)(2,1)S(1)}, u32[]{:S(2)}, u32[]{:S(2)}) async-start(bf16[16,8,1024]{2,1,0:T(8,128)(2,1)} %maximum_maximum_fusion), calls=%async_computation | async-start | bytes 524288 | tf_op jit(solution)/shard_map/all_to_all | solution.py:23
  15.9 15.4 %all-to-all-done = bf16[16,8,1024]{2,1,0:T(8,128)(2,1)S(1)} async-done(((bf16[16,8,1024]{2,1,0:T(8,128)(2,1)}), bf16[16,8,1024]{2,1,0:T(8,128)(2,1)S(1)}, u32[]{:S(2)}, u32[]{:S(2)}) %all-to-all-start) | async-done | bytes 262176 | tf_op jit(solution)/shard_map/all_to_all | solution.py:23
  32.4 12.7 %all_to_all.66 = bf16[4,64,896]{2,1,0:T(8,128)(2,1)S(1)} all-to-all(bf16[4,64,896]{2,1,0:T(8,128)(2,1)S(1)} %bitcast.109), channel_id=1, replica_groups={{0,16,32,48},{1,17,33,49},{2,18,34,50},{3,19,35,51},{4,20,36,52},{5,21,..., dimensions={0} | all-to-all | bytes 917504 | tf_op jit(solution)/shard_map/all_to_all | solution.py:23
  45.1 5.0 %all-to-all-start.2 = ((bf16[8,896,128]{2,1,0:T(8,128)(2,1)}), bf16[8,896,128]{2,1,0:T(8,128)(2,1)S(1)}, u32[]{:S(2)}, u32[]{:S(2)}) async-start(bf16[8,896,128]{2,1,0:T(8,128)(2,1)} %bitcast.105), calls=%async_computation.2 | async-start | bytes 3670016 | tf_op jit(solution)/shard_map/all_to_all | solution.py:23
  50.5 39.3 %all-to-all-done.2 = bf16[8,896,128]{2,1,0:T(8,128)(2,1)S(1)} async-done(((bf16[8,896,128]{2,1,0:T(8,128)(2,1)}), bf16[8,896,128]{2,1,0:T(8,128)(2,1)S(1)}, u32[]{:S(2)}, u32[]{:S(2)}) %all-to-all-start.2) | async-done | bytes 1835040 | tf_op jit(solution)/shard_map/all_to_all | solution.py:23
  95.7 7.2 %all-to-all-start.3 = ((bf16[8,272,128]{2,1,0:T(8,128)(2,1)}), bf16[8,272,128]{2,1,0:T(8,128)(2,1)S(1)}, u32[]{:S(2)}, u32[]{:S(2)}) async-start(bf16[8,272,128]{2,1,0:T(8,128)(2,1)} %pad_maximum_fusion), calls=%async_computation.3 | async-start | bytes 1114112 | tf_op jit(solution)/shard_map/all_to_all | solution.py:23
  102.9 3.3 copy.48
  108.9 6.3 %all-to-all-done.3 = bf16[8,272,128]{2,1,0:T(8,128)(2,1)S(1)} async-done(((bf16[8,272,128]{2,1,0:T(8,128)(2,1)}), bf16[8,272,128]{2,1,0:T(8,128)(2,1)S(1)}, u32[]{:S(2)}, u32[]{:S(2)}) %all-to-all-start.3) | async-done | bytes 557088 | tf_op jit(solution)/shard_map/all_to_all | solution.py:23
  115.2 7.3 %all-to-all-start.4 = ((bf16[8,128,896]{2,1,0:T(8,128)(2,1)}), bf16[8,128,896]{2,1,0:T(8,128)(2,1)S(1)}, u32[]{:S(2)}, u32[]{:S(2)}) async-start(bf16[8,128,896]{2,1,0:T(8,128)(2,1)} %bitcast.22), calls=%async_computation.4 | async-start | bytes 3670016 | tf_op jit(solution)/shard_map/all_to_all | solution.py:23
  122.8 49.2 %all-gather = bf16[2048,128]{1,0:T(8,128)(2,1)S(1)} all-gather(bf16[256,128]{1,0:T(8,128)(2,1)S(1)} %multiply_convert_fusion.1), channel_id=2, replica_groups={{0,1,2,3,4,5,6,7},{8,9,10,11,12,13,14,15},{16,17,18,19,20,21,22,23},{24..., dimensions={0}, use_global_device_ids=true | all-gather | bytes 589824 | tf_op jit(solution)/shard_map/all_gather | solution.py:126
  173.5 3.5 all-to-all-start.5
  177.0 8.6 %all-to-all-done.5 = bf16[4,64,896]{2,1,0:T(8,128)(2,1)S(1)} async-done(((bf16[4,64,896]{2,1,0:T(8,128)(2,1)}), bf16[4,64,896]{2,1,0:T(8,128)(2,1)S(1)}, u32[]{:S(2)}, u32[]{:S(2)}) %all-to-all-start.5) | async-done | bytes 458784 | tf_op jit(solution)/shard_map/all_to_all | solution.py:23
  186.2 4.8 %collective-permute-start = (bf16[64,896]{1,0:T(8,128)(2,1)S(1)}, bf16[64,896]{1,0:T(8,128)(2,1)S(1)}, u32[]{:S(2)}, u32[]{:S(2)}) collective-permute-start(bf16[64,896]{1,0:T(8,128)(2,1)S(1)} %slice.118), channel_id=1, source_target_pairs={{0,8},{1,9},{2,10},{3,11},{4,12},{5,13},{6,14},{7,15},{8,0},{9,1},... | collective-permute-start | bytes 344072 | tf_op jit(solution)/shard_map/ppermute | solution.py:30
  191.0 5.0 %collective-permute-done = bf16[64,896]{1,0:T(8,128)(2,1)S(1)} collective-permute-done((bf16[64,896]{1,0:T(8,128)(2,1)S(1)}, bf16[64,896]{1,0:T(8,128)(2,1)S(1)}, u32[]{:S(2)}, u32[]{:S(2)}) %collective-permute-start) | collective-permute-done | bytes 114720 | tf_op jit(solution)/shard_map/ppermute | solution.py:30
  199.1 13.3 %collective-permute-done.1 = bf16[64,896]{1,0:T(8,128)(2,1)S(1)} collective-permute-done((bf16[64,896]{1,0:T(8,128)(2,1)S(1)}, bf16[64,896]{1,0:T(8,128)(2,1)S(1)}, u32[]{:S(2)}, u32[]{:S(2)}) %collective-permute-start.1) | collective-permute-done | bytes 114720 | tf_op jit(solution)/shard_map/ppermute | solution.py:35
  212.4 5.8 %collective-permute-start.2 = (bf16[64,896]{1,0:T(8,128)(2,1)S(1)}, bf16[64,896]{1,0:T(8,128)(2,1)S(1)}, u32[]{:S(2)}, u32[]{:S(2)}) collective-permute-start(bf16[64,896]{1,0:T(8,128)(2,1)S(1)} %collective-permute-done.1), channel_id=1, source_target_pairs={{0,8},{1,9},{2,10},{3,11},{4,12},{5,13},{6,14},{7,15},{8,0},{9,1},... | collective-permute-start | bytes 344072 | tf_op jit(solution)/shard_map/ppermute | solution.py:30
  218.2 3.7 %collective-permute-done.2 = bf16[64,896]{1,0:T(8,128)(2,1)S(1)} collective-permute-done((bf16[64,896]{1,0:T(8,128)(2,1)S(1)}, bf16[64,896]{1,0:T(8,128)(2,1)S(1)}, u32[]{:S(2)}, u32[]{:S(2)}) %collective-permute-start.2) | collective-permute-done | bytes 114720 | tf_op jit(solution)/shard_map/ppermute | solution.py:30
  222.2 9.0 %all_to_all.67 = bf16[4,64,896]{2,1,0:T(8,128)(2,1)S(1)} all-to-all(bf16[4,64,896]{2,1,0:T(8,128)(2,1)S(1)} %bitcast.108), channel_id=1, replica_groups={{0,16,32,48},{1,17,33,49},{2,18,34,50},{3,19,35,51},{4,20,36,52},{5,21,..., dimensions={0} | all-to-all | bytes 917504 | tf_op jit(solution)/shard_map/all_to_all | solution.py:23
  232.4 38.5 %all_to_all.68 = bf16[8,272,128]{2,1,0:T(8,128)(2,1)S(1)} all-to-all(bf16[8,272,128]{2,1,0:T(8,128)(2,1)S(1)} %pad_maximum_fusion.1), channel_id=1, replica_groups={{0,1,2,3,4,5,6,7},{8,9,10,11,12,13,14,15},{16,17,18,19,20,21,22,23},{24..., dimensions={0} | all-to-all | bytes 1114112 | tf_op jit(solution)/shard_map/all_to_all | solution.py:23
  271.1 15.9 %all-gather.1 = bf16[2048,128]{1,0:T(8,128)(2,1)S(1)} all-gather(bf16[256,128]{1,0:T(8,128)(2,1)S(1)} %multiply_convert_fusion), channel_id=3, replica_groups={{0,1,2,3,4,5,6,7},{8,9,10,11,12,13,14,15},{16,17,18,19,20,21,22,23},{24..., dimensions={0}, use_global_device_ids=true | all-gather | bytes 589824 | tf_op jit(solution)/shard_map/all_gather | solution.py:126
  288.5 3.5 all-to-all-start.8
  292.0 8.7 %all-to-all-done.8 = bf16[4,64,896]{2,1,0:T(8,128)(2,1)S(1)} async-done(((bf16[4,64,896]{2,1,0:T(8,128)(2,1)}), bf16[4,64,896]{2,1,0:T(8,128)(2,1)S(1)}, u32[]{:S(2)}, u32[]{:S(2)}) %all-to-all-start.8) | async-done | bytes 458784 | tf_op jit(solution)/shard_map/all_to_all | solution.py:23
  301.4 21.6 %all_to_all.69 = bf16[16,8,896]{2,1,0:T(8,128)(2,1)S(1)} all-to-all(bf16[16,8,896]{2,1,0:T(8,128)(2,1)S(1)} %bitcast.114), channel_id=1, replica_groups={{0,1,2,3,4,5,6,7,8,9,10,11,12,13,14,15},{16,17,18,19,20,21,22,23,24,25,..., dimensions={0} | all-to-all | bytes 458752 | tf_op jit(solution)/shard_map/all_to_all | solution.py:23
  325.0 23.3 %collective-permute-done.3 = bf16[8,7168]{1,0:T(8,128)(2,1)S(1)} collective-permute-done((bf16[8,7168]{1,0:T(8,128)(2,1)S(1)}, bf16[8,7168]{1,0:T(8,128)(2,1)S(1)}, u32[]{:S(2)}, u32[]{:S(2)}) %collective-permute-start.3) | collective-permute-done | bytes 114720 | tf_op jit(solution)/shard_map/ppermute | solution.py:35
  (81 shorter events, 25.4 us)
Async XLA Ops:
  0.0 50.2 %copy-start = (f32[1,7168]{1,0:T(1,128)S(1)}, f32[1,7168]{1,0:T(1,128)}, u32[]{:S(2)}) copy-start(f32[1,7168]{1,0:T(1,128)} %param.7) | copy-start | bytes 86020
  3.2 28.1 %all-to-all-start = ((bf16[16,8,1024]{2,1,0:T(8,128)(2,1)}), bf16[16,8,1024]{2,1,0:T(8,128)(2,1)S(1)}, u32[]{:S(2)}, u32[]{:S(2)}) async-start(bf16[16,8,1024]{2,1,0:T(8,128)(2,1)} %maximum_maximum_fusion), calls=%async_computation | async-start | bytes 524288 | tf_op jit(solution)/shard_map/all_to_all | solution.py:23
  45.1 44.7 %all-to-all-start.2 = ((bf16[8,896,128]{2,1,0:T(8,128)(2,1)}), bf16[8,896,128]{2,1,0:T(8,128)(2,1)S(1)}, u32[]{:S(2)}, u32[]{:S(2)}) async-start(bf16[8,896,128]{2,1,0:T(8,128)(2,1)} %bitcast.105), calls=%async_computation.2 | async-start | bytes 3670016 | tf_op jit(solution)/shard_map/all_to_all | solution.py:23
  95.7 19.5 %all-to-all-start.3 = ((bf16[8,272,128]{2,1,0:T(8,128)(2,1)}), bf16[8,272,128]{2,1,0:T(8,128)(2,1)S(1)}, u32[]{:S(2)}, u32[]{:S(2)}) async-start(bf16[8,272,128]{2,1,0:T(8,128)(2,1)} %pad_maximum_fusion), calls=%async_computation.3 | async-start | bytes 1114112 | tf_op jit(solution)/shard_map/all_to_all | solution.py:23
  115.2 56.7 %all-to-all-start.4 = ((bf16[8,128,896]{2,1,0:T(8,128)(2,1)}), bf16[8,128,896]{2,1,0:T(8,128)(2,1)S(1)}, u32[]{:S(2)}, u32[]{:S(2)}) async-start(bf16[8,128,896]{2,1,0:T(8,128)(2,1)} %bitcast.22), calls=%async_computation.4 | async-start | bytes 3670016 | tf_op jit(solution)/shard_map/all_to_all | solution.py:23
  173.5 12.2 %all-to-all-start.5 = ((bf16[4,64,896]{2,1,0:T(8,128)(2,1)}), bf16[4,64,896]{2,1,0:T(8,128)(2,1)S(1)}, u32[]{:S(2)}, u32[]{:S(2)}) async-start(bf16[4,64,896]{2,1,0:T(8,128)(2,1)} %bitcast.24), calls=%async_computation.5 | async-start | bytes 917504 | tf_op jit(solution)/shard_map/all_to_all | solution.py:23
  186.1 45.2 %copy-start.1 = (bf16[896,8,128]{0,2,1:T(8,128)(2,1)S(1)}, bf16[896,8,128]{0,2,1:T(8,128)(2,1)}, u32[]{:S(2)}) copy-start(bf16[896,8,128]{0,2,1:T(8,128)(2,1)} %copy.46) | copy-start | bytes 5505028
  186.2 9.8 %collective-permute-start = (bf16[64,896]{1,0:T(8,128)(2,1)S(1)}, bf16[64,896]{1,0:T(8,128)(2,1)S(1)}, u32[]{:S(2)}, u32[]{:S(2)}) collective-permute-start(bf16[64,896]{1,0:T(8,128)(2,1)S(1)} %slice.118), channel_id=1, source_target_pairs={{0,8},{1,9},{2,10},{3,11},{4,12},{5,13},{6,14},{7,15},{8,0},{9,1},... | collective-permute-start | bytes 344072 | tf_op jit(solution)/shard_map/ppermute | solution.py:30
  196.0 16.4 %collective-permute-start.1 = (bf16[64,896]{1,0:T(8,128)(2,1)S(1)}, bf16[64,896]{1,0:T(8,128)(2,1)S(1)}, u32[]{:S(2)}, u32[]{:S(2)}) collective-permute-start(bf16[64,896]{1,0:T(8,128)(2,1)S(1)} %fusion.13), channel_id=1, source_target_pairs={{0,64},{64,128},{128,192},{192,256},{256,320},{320,384},{384,448},... | collective-permute-start | bytes 344072 | tf_op jit(solution)/shard_map/ppermute | solution.py:35
  212.4 9.4 %collective-permute-start.2 = (bf16[64,896]{1,0:T(8,128)(2,1)S(1)}, bf16[64,896]{1,0:T(8,128)(2,1)S(1)}, u32[]{:S(2)}, u32[]{:S(2)}) collective-permute-start(bf16[64,896]{1,0:T(8,128)(2,1)S(1)} %collective-permute-done.1), channel_id=1, source_target_pairs={{0,8},{1,9},{2,10},{3,11},{4,12},{5,13},{6,14},{7,15},{8,0},{9,1},... | collective-permute-start | bytes 344072 | tf_op jit(solution)/shard_map/ppermute | solution.py:30
  288.5 12.2 %all-to-all-start.8 = ((bf16[4,64,896]{2,1,0:T(8,128)(2,1)}), bf16[4,64,896]{2,1,0:T(8,128)(2,1)S(1)}, u32[]{:S(2)}, u32[]{:S(2)}) async-start(bf16[4,64,896]{2,1,0:T(8,128)(2,1)} %bitcast.37), calls=%async_computation.8 | async-start | bytes 917504 | tf_op jit(solution)/shard_map/all_to_all | solution.py:23
  323.1 25.3 %collective-permute-start.3 = (bf16[8,7168]{1,0:T(8,128)(2,1)S(1)}, bf16[8,7168]{1,0:T(8,128)(2,1)S(1)}, u32[]{:S(2)}, u32[]{:S(2)}) collective-permute-start(bf16[8,7168]{1,0:T(8,128)(2,1)S(1)} %bitcast.122), channel_id=1, source_target_pairs={{0,64},{64,128},{128,192},{192,256},{256,320},{320,384},{384,448},... | collective-permute-start | bytes 344072 | tf_op jit(solution)/shard_map/ppermute | solution.py:35

commit v3 on v2

--- a/solution.py
+++ b/solution.py
@@ -31,8 +31,33 @@
 
 
 def next_section(value):
-    count = lax.axis_size("section")
-    return lax.ppermute(value, "section", [(i, (i + 1) % count) for i in range(count)])
+    sections, count = lax.axis_size("section"), lax.axis_size("expert")
+    route = [
+        (s * count + i, (s + 1) % sections * count + (i ^ GROUP))
+        for s in range(sections)
+        for i in range(count)
+    ]
+    return lax.ppermute(value, ("section", "expert"), route)
+
+
+def spread(slices, place):
+    count = lax.axis_size("expert")
+    return [
+        lax.ppermute(
+            lax.dynamic_index_in_dim(slices, place % GROUP ^ step, 0),
+            "expert",
+            [(i, i ^ step) for i in range(count)],
+        )
+        for step in range(1, GROUP)
+    ]
+
+
+def gathered(slices, came, place):
+    for step in range(1, GROUP):
+        slices = lax.dynamic_update_slice_in_dim(
+            slices, came[step - 1], place % GROUP ^ step, 0
+        )
+    return slices
 
 
 def head(value):
@@ -93,10 +118,10 @@
     facts = arrived[:, part:].astype(jnp.float32)
     routes = facts[:, : 4 * passes * top].reshape(HALVES * block, 4, passes, top)
 
-    up = exchange(w_up[0].reshape(GROUP, part, HID_DEV), same_expert)
+    up_slices = w_up[0].reshape(GROUP, part, HID_DEV)
+    up = gathered(up_slices, spread(up_slices, place), place)
     up = up.transpose(1, 0, 2).reshape(part, HID)
-    down = exchange(w_down[0].reshape(HID_DEV, GROUP, part).transpose(1, 0, 2), same_expert)
-    down = down.reshape(HID, part)
+    down_slices = w_down[0].reshape(HID_DEV, GROUP, part).transpose(1, 0, 2)
     gain = lax.dynamic_slice_in_dim(norm_gain[0], place % GROUP * part, part, 0)
 
     for t in range(passes):
@@ -105,6 +130,9 @@
         picker, weigher = tables(ids, gates, half, peers, rows_dev)
         slots = jnp.dot(picker, rows, preferred_element_type=jnp.float32).astype(jnp.bfloat16)
         slots = exchange(slots, same_slice)
+        if t == 0:
+            slots, down_slices = lax.optimization_barrier((slots, down_slices))
+            came = spread(down_slices, place)
         values = slots.astype(jnp.float32)
         squares = jnp.sum(values * values, axis=1)
         partial = jnp.dot(
@@ -124,6 +152,9 @@
         scale = lax.rsqrt(squares / width + 1e-06)
         active = jax.nn.silu(sums[:held] * scale[:, None]).astype(jnp.bfloat16)
         active = lax.all_gather(active, "expert", axis_index_groups=same_expert)
+        if t == 0:
+            active, came = lax.optimization_barrier((active, came))
+            down = gathered(down_slices, came, place).reshape(HID, part)
         active = active.transpose(1, 0, 2).reshape(held, HID)
         outputs = jnp.dot(active, down, preferred_element_type=jnp.float32).astype(jnp.bfloat16)
         outputs = exchange(outputs, same_slice)
@@ -133,15 +164,15 @@
             precision=lax.Precision.HIGHEST,
             preferred_element_type=jnp.float32,
         )
-        own = rows[:block].astype(jnp.float32) + mixture[:block]
-        other = mixture[block:].astype(jnp.bfloat16)
+        own = mixture[:block].astype(jnp.bfloat16)
+        other = rows[block:].astype(jnp.float32) + mixture[block:]
         if t + 1 < passes:
-            own = (own + other_half(other).astype(jnp.float32)).astype(jnp.bfloat16)
-            own = next_section(own)
+            other = (other + other_half(own).astype(jnp.float32)).astype(jnp.bfloat16)
+            own = next_section(other)
             rows = jnp.concatenate([own, other_half(own)])
         else:
-            own = own.astype(jnp.bfloat16)
-            both = lax.dynamic_slice_in_dim(jnp.stack([own, other, own]), half, HALVES, 0)
+            other = other.astype(jnp.bfloat16)
+            both = lax.dynamic_slice_in_dim(jnp.stack([other, own, other]), half, HALVES, 0)
             both = exchange(both.reshape(HALVES * GROUP, rows_dev, part), same_row)
             both = both.reshape(HALVES, GROUP, rows_dev, part).astype(jnp.float32)
             done = jnp.sum(both, axis=0).astype(jnp.bfloat16)

time: 350 us -> 335 us (0.957)
  the two profiles are of different devices: /device:TPU:65 before, /device:TPU:7 now
where the time goes in v3:
time: 335 us; the launch traced here: 333 us
  waiting for transfers between devices  118 us (35%)
  blocking collectives  92.4 us (28%)
  starting transfers between devices  92 us (27%)
  local copies, waits for them, and re-layouts  18.5 us (6%)
  matrix products  8.62 us (3%)
    all_to_all x3, blocking collectives, exchange(): lax.all_to_all(value, 'expert', split_axis=0, concat_axis=0, axis_index_g...  53.1 us
    ppermute x14, starting transfers between devices, spread(): lax.ppermute(lax.dynamic_index_in_dim(slices, place % GROUP ^ step, 0), '...  48.3 us
    all_gather x2, blocking collectives, body(): active = lax.all_gather(active, 'expert', axis_index_groups=same_expert)  39.2 us
    all_to_all x5, waiting for transfers between devices, exchange(): lax.all_to_all(value, 'expert', split_axis=0, concat_axis=0, axis_index_g...  35.7 us
    ppermute x14, waiting for transfers between devices, spread(): lax.ppermute(lax.dynamic_index_in_dim(slices, place % GROUP ^ step, 0), '...  30.6 us
    all_to_all x5, starting transfers between devices, exchange(): lax.all_to_all(value, 'expert', split_axis=0, concat_axis=0, axis_index_g...  30.3 us
    ppermute x2, waiting for transfers between devices, next_section(): return lax.ppermute(value, ('section', 'expert'), route)  30.3 us
    ppermute x2, waiting for transfers between devices, other_half(): return lax.ppermute(value, 'expert', [(i, i ^ GROUP) for i in range(count)])  21 us
  transfers between devices with their start and end apart: 23, of which 9 were waited for; matrix products, arithmetic and copies ran while one was open for 4% of the time, Pallas kernels for 0%

profile of v3, /device:TPU:7, one launch (start us, length us, event | category | flops | bytes accessed | tf_op | source)
XLA Modules:
  0.0 333.2 jit_solution(6011930941961293980)
XLA Ops:
  2.4 13.2 %all-to-all-start = ((bf16[16,8,1024]{2,1,0:T(8,128)(2,1)}), bf16[16,8,1024]{2,1,0:T(8,128)(2,1)S(1)}, u32[]{:S(2)}, u32[]{:S(2)}) async-start(bf16[16,8,1024]{2,1,0:T(8,128)(2,1)} %maximum_maximum_fusion), calls=%async_computation | async-start | bytes 524288 | tf_op jit(solution)/shard_map/all_to_all | solution.py:23
  21.6 3.5 %collective-permute-start.1 = (bf16[1,896,128]{2,1,0:T(8,128)(2,1)S(1)}, bf16[1,896,128]{2,1,0:T(8,128)(2,1)S(1)}, u32[]{:S(2)}, u32[]{:S(2)}) collective-permute-start(bf16[1,896,128]{2,1,0:T(8,128)(2,1)S(1)} %get-tuple-element.43), channel_id=1, source_target_pairs={{0,2},{1,3},{2,0},{3,1},{4,6},{5,7},{6,4},{7,5},{8,10},{9,11},{10,... | collective-permute-start | bytes 688136 | tf_op jit(solution)/shard_map/ppermute | solution.py:46
  27.5 5.1 %collective-permute-start.6 = (bf16[1,896,128]{2,1,0:T(8,128)(2,1)S(1)}, bf16[1,896,128]{2,1,0:T(8,128)(2,1)}, u32[]{:S(2)}, u32[]{:S(2)}) collective-permute-start(bf16[1,896,128]{2,1,0:T(8,128)(2,1)S(1)} %get-tuple-element.38), channel_id=1, source_target_pairs={{0,7},{1,6},{2,5},{3,4},{4,3},{5,2},{6,1},{7,0},{8,15},{9,14},{10,... | collective-permute-start | bytes 688136 | tf_op jit(solution)/shard_map/ppermute | solution.py:46
  37.6 3.8 %collective-permute-start.3 = (bf16[1,896,128]{2,1,0:T(8,128)(2,1)S(1)}, bf16[1,896,128]{2,1,0:T(8,128)(2,1)S(1)}, u32[]{:S(2)}, u32[]{:S(2)}) collective-permute-start(bf16[1,896,128]{2,1,0:T(8,128)(2,1)S(1)} %get-tuple-element.41), channel_id=1, source_target_pairs={{0,4},{1,5},{2,6},{3,7},{4,0},{5,1},{6,2},{7,3},{8,12},{9,13},{10,... | collective-permute-start | bytes 688136 | tf_op jit(solution)/shard_map/ppermute | solution.py:46
  41.5 30.5 %collective-permute-done.3 = bf16[1,896,128]{2,1,0:T(8,128)(2,1)S(1)} collective-permute-done((bf16[1,896,128]{2,1,0:T(8,128)(2,1)S(1)}, bf16[1,896,128]{2,1,0:T(8,128)(2,1)S(1)}, u32[]{:S(2)}, u32[]{:S(2)}) %collective-permute-start.3) | collective-permute-done | bytes 229408 | tf_op jit(solution)/shard_map/ppermute | solution.py:46
  74.3 4.2 %all-to-all-start.1 = ((bf16[4,64,896]{2,1,0:T(8,128)(2,1)}), bf16[4,64,896]{2,1,0:T(8,128)(2,1)S(1)}, u32[]{:S(2)}, u32[]{:S(2)}) async-start(bf16[4,64,896]{2,1,0:T(8,128)(2,1)} %bitcast.13), calls=%async_computation.1 | async-start | bytes 917504 | tf_op jit(solution)/shard_map/all_to_all | solution.py:23
  89.3 6.0 %all-to-all-start.2 = ((bf16[8,272,128]{2,1,0:T(8,128)(2,1)}), bf16[8,272,128]{2,1,0:T(8,128)(2,1)S(1)}, u32[]{:S(2)}, u32[]{:S(2)}) async-start(bf16[8,272,128]{2,1,0:T(8,128)(2,1)} %pad_maximum_fusion), calls=%async_computation.2 | async-start | bytes 1114112 | tf_op jit(solution)/shard_map/all_to_all | solution.py:23
  96.3 5.3 %collective-permute-start.13 = (bf16[1,128,896]{2,1,0:T(8,128)(2,1)}, bf16[1,128,896]{2,1,0:T(8,128)(2,1)}, u32[]{:S(2)}, u32[]{:S(2)}) collective-permute-start(bf16[1,128,896]{2,1,0:T(8,128)(2,1)} %get-tuple-element.31), channel_id=1, source_target_pairs={{0,7},{1,6},{2,5},{3,4},{4,3},{5,2},{6,1},{7,0},{8,15},{9,14},{10,... | collective-permute-start | bytes 688136 | tf_op jit(solution)/shard_map/ppermute | solution.py:46
  106.3 3.8 %collective-permute-start.10 = (bf16[1,128,896]{2,1,0:T(8,128)(2,1)}, bf16[1,128,896]{2,1,0:T(8,128)(2,1)}, u32[]{:S(2)}, u32[]{:S(2)}) collective-permute-start(bf16[1,128,896]{2,1,0:T(8,128)(2,1)} %get-tuple-element.34), channel_id=1, source_target_pairs={{0,4},{1,5},{2,6},{3,7},{4,0},{5,1},{6,2},{7,3},{8,12},{9,13},{10,... | collective-permute-start | bytes 688136 | tf_op jit(solution)/shard_map/ppermute | solution.py:46
  113.4 16.7 %all-to-all-done.2 = bf16[8,272,128]{2,1,0:T(8,128)(2,1)S(1)} async-done(((bf16[8,272,128]{2,1,0:T(8,128)(2,1)}), bf16[8,272,128]{2,1,0:T(8,128)(2,1)S(1)}, u32[]{:S(2)}, u32[]{:S(2)}) %all-to-all-start.2) | async-done | bytes 557088 | tf_op jit(solution)/shard_map/all_to_all | solution.py:23
  130.4 7.6 %collective-permute-start.8 = (bf16[1,128,896]{2,1,0:T(8,128)(2,1)S(1)}, bf16[1,128,896]{2,1,0:T(8,128)(2,1)S(1)}, u32[]{:S(2)}, u32[]{:S(2)}) collective-permute-start(bf16[1,128,896]{2,1,0:T(8,128)(2,1)S(1)} %get-tuple-element.36), channel_id=1, source_target_pairs={{0,2},{1,3},{2,0},{3,1},{4,6},{5,7},{6,4},{7,5},{8,10},{9,11},{10,... | collective-permute-start | bytes 688136 | tf_op jit(solution)/shard_map/ppermute | solution.py:46
  140.0 24.0 %all-gather = bf16[2048,128]{1,0:T(8,128)(2,1)S(1)} all-gather(bf16[256,128]{1,0:T(8,128)(2,1)S(1)} %multiply_convert_fusion.1), channel_id=2, replica_groups={{0,1,2,3,4,5,6,7},{8,9,10,11,12,13,14,15},{16,17,18,19,20,21,22,23},{24..., dimensions={0}, use_global_device_ids=true | all-gather | bytes 589824 | tf_op jit(solution)/shard_map/all_gather | solution.py:154
  174.1 8.6 %all-to-all-done.3 = bf16[4,64,896]{2,1,0:T(8,128)(2,1)S(1)} async-done(((bf16[4,64,896]{2,1,0:T(8,128)(2,1)}), bf16[4,64,896]{2,1,0:T(8,128)(2,1)S(1)}, u32[]{:S(2)}, u32[]{:S(2)}) %all-to-all-start.3) | async-done | bytes 458784 | tf_op jit(solution)/shard_map/all_to_all | solution.py:23
  183.2 7.1 %collective-permute-start.14 = (bf16[64,896]{1,0:T(8,128)(2,1)S(1)}, bf16[64,896]{1,0:T(8,128)(2,1)S(1)}, u32[]{:S(2)}, u32[]{:S(2)}) collective-permute-start(bf16[64,896]{1,0:T(8,128)(2,1)S(1)} %slice.118), channel_id=1, source_target_pairs={{0,8},{1,9},{2,10},{3,11},{4,12},{5,13},{6,14},{7,15},{8,0},{9,1},... | collective-permute-start | bytes 344072 | tf_op jit(solution)/shard_map/ppermute | solution.py:30
  190.4 10.0 %collective-permute-done.14 = bf16[64,896]{1,0:T(8,128)(2,1)S(1)} collective-permute-done((bf16[64,896]{1,0:T(8,128)(2,1)S(1)}, bf16[64,896]{1,0:T(8,128)(2,1)S(1)}, u32[]{:S(2)}, u32[]{:S(2)}) %collective-permute-start.14) | collective-permute-done | bytes 114720 | tf_op jit(solution)/shard_map/ppermute | solution.py:30
  202.5 14.6 %collective-permute-done.15 = bf16[64,896]{1,0:T(8,128)(2,1)S(1)} collective-permute-done((bf16[64,896]{1,0:T(8,128)(2,1)S(1)}, bf16[64,896]{1,0:T(8,128)(2,1)S(1)}, u32[]{:S(2)}, u32[]{:S(2)}) %collective-permute-start.15) | collective-permute-done | bytes 114720 | tf_op jit(solution)/shard_map/ppermute | solution.py:40
  219.0 11.0 %collective-permute-done.16 = bf16[64,896]{1,0:T(8,128)(2,1)S(1)} collective-permute-done((bf16[64,896]{1,0:T(8,128)(2,1)S(1)}, bf16[64,896]{1,0:T(8,128)(2,1)S(1)}, u32[]{:S(2)}, u32[]{:S(2)}) %collective-permute-start.16) | collective-permute-done | bytes 114720 | tf_op jit(solution)/shard_map/ppermute | solution.py:30
  230.3 10.5 %all_to_all.59 = bf16[4,64,896]{2,1,0:T(8,128)(2,1)S(1)} all-to-all(bf16[4,64,896]{2,1,0:T(8,128)(2,1)S(1)} %bitcast.118), channel_id=1, replica_groups={{0,16,32,48},{1,17,33,49},{2,18,34,50},{3,19,35,51},{4,20,36,52},{5,21,..., dimensions={0} | all-to-all | bytes 917504 | tf_op jit(solution)/shard_map/all_to_all | solution.py:23
  242.1 19.4 %all_to_all.60 = bf16[8,272,128]{2,1,0:T(8,128)(2,1)S(1)} all-to-all(bf16[8,272,128]{2,1,0:T(8,128)(2,1)S(1)} %pad_maximum_fusion.1), channel_id=1, replica_groups={{0,1,2,3,4,5,6,7},{8,9,10,11,12,13,14,15},{16,17,18,19,20,21,22,23},{24..., dimensions={0} | all-to-all | bytes 1114112 | tf_op jit(solution)/shard_map/all_to_all | solution.py:23
  261.8 15.2 %all-gather.1 = bf16[2048,128]{1,0:T(8,128)(2,1)S(1)} all-gather(bf16[256,128]{1,0:T(8,128)(2,1)S(1)} %multiply_convert_fusion), channel_id=3, replica_groups={{0,1,2,3,4,5,6,7},{8,9,10,11,12,13,14,15},{16,17,18,19,20,21,22,23},{24..., dimensions={0}, use_global_device_ids=true | all-gather | bytes 589824 | tf_op jit(solution)/shard_map/all_gather | solution.py:154
  278.5 3.5 %all-to-all-start.6 = ((bf16[4,64,896]{2,1,0:T(8,128)(2,1)}), bf16[4,64,896]{2,1,0:T(8,128)(2,1)S(1)}, u32[]{:S(2)}, u32[]{:S(2)}) async-start(bf16[4,64,896]{2,1,0:T(8,128)(2,1)} %bitcast.37), calls=%async_computation.6 | async-start | bytes 917504 | tf_op jit(solution)/shard_map/all_to_all | solution.py:23
  282.0 8.7 %all-to-all-done.6 = bf16[4,64,896]{2,1,0:T(8,128)(2,1)S(1)} async-done(((bf16[4,64,896]{2,1,0:T(8,128)(2,1)}), bf16[4,64,896]{2,1,0:T(8,128)(2,1)S(1)}, u32[]{:S(2)}, u32[]{:S(2)}) %all-to-all-start.6) | async-done | bytes 458784 | tf_op jit(solution)/shard_map/all_to_all | solution.py:23
  291.4 23.2 %all_to_all.61 = bf16[16,8,896]{2,1,0:T(8,128)(2,1)S(1)} all-to-all(bf16[16,8,896]{2,1,0:T(8,128)(2,1)S(1)} %bitcast.123), channel_id=1, replica_groups={{0,1,2,3,4,5,6,7,8,9,10,11,12,13,14,15},{16,17,18,19,20,21,22,23,24,25,..., dimensions={0} | all-to-all | bytes 458752 | tf_op jit(solution)/shard_map/all_to_all | solution.py:23
  316.9 15.7 %collective-permute-done.17 = bf16[8,7168]{1,0:T(8,128)(2,1)S(1)} collective-permute-done((bf16[8,7168]{1,0:T(8,128)(2,1)S(1)}, bf16[8,7168]{1,0:T(8,128)(2,1)S(1)}, u32[]{:S(2)}, u32[]{:S(2)}) %collective-permute-start.17) | collective-permute-done | bytes 114720 | tf_op jit(solution)/shard_map/ppermute | solution.py:40
  (166 shorter events, 61.1 us)
Async XLA Ops:
  2.4 69.6 %all-to-all-start = ((bf16[16,8,1024]{2,1,0:T(8,128)(2,1)}), bf16[16,8,1024]{2,1,0:T(8,128)(2,1)S(1)}, u32[]{:S(2)}, u32[]{:S(2)}) async-start(bf16[16,8,1024]{2,1,0:T(8,128)(2,1)} %maximum_maximum_fusion), calls=%async_computation | async-start | bytes 524288 | tf_op jit(solution)/shard_map/all_to_all | solution.py:23
  15.7 5.6 %collective-permute-start = (bf16[1,896,128]{2,1,0:T(8,128)(2,1)S(1)}, bf16[1,896,128]{2,1,0:T(8,128)(2,1)S(1)}, u32[]{:S(2)}, u32[]{:S(2)}) collective-permute-start(bf16[1,896,128]{2,1,0:T(8,128)(2,1)S(1)} %constant_dynamic-slice_fusion.13), channel_id=1, source_target_pairs={{0,1},{1,0},{2,3},{3,2},{4,5},{5,4},{6,7},{7,6},{8,9},{9,8},{10,11... | collective-permute-start | bytes 688136 | tf_op jit(solution)/shard_map/ppermute | solution.py:46
  21.6 16.0 %collective-permute-start.1 = (bf16[1,896,128]{2,1,0:T(8,128)(2,1)S(1)}, bf16[1,896,128]{2,1,0:T(8,128)(2,1)S(1)}, u32[]{:S(2)}, u32[]{:S(2)}) collective-permute-start(bf16[1,896,128]{2,1,0:T(8,128)(2,1)S(1)} %get-tuple-element.43), channel_id=1, source_target_pairs={{0,2},{1,3},{2,0},{3,1},{4,6},{5,7},{6,4},{7,5},{8,10},{9,11},{10,... | collective-permute-start | bytes 688136 | tf_op jit(solution)/shard_map/ppermute | solution.py:46
  25.2 16.2 %collective-permute-start.2 = (bf16[1,896,128]{2,1,0:T(8,128)(2,1)S(1)}, bf16[1,896,128]{2,1,0:T(8,128)(2,1)S(1)}, u32[]{:S(2)}, u32[]{:S(2)}) collective-permute-start(bf16[1,896,128]{2,1,0:T(8,128)(2,1)S(1)} %get-tuple-element.42), channel_id=1, source_target_pairs={{0,3},{1,2},{2,1},{3,0},{4,7},{5,6},{6,5},{7,4},{8,11},{9,10},{10,... | collective-permute-start | bytes 688136 | tf_op jit(solution)/shard_map/ppermute | solution.py:46
  27.5 53.0 %collective-permute-start.6 = (bf16[1,896,128]{2,1,0:T(8,128)(2,1)S(1)}, bf16[1,896,128]{2,1,0:T(8,128)(2,1)}, u32[]{:S(2)}, u32[]{:S(2)}) collective-permute-start(bf16[1,896,128]{2,1,0:T(8,128)(2,1)S(1)} %get-tuple-element.38), channel_id=1, source_target_pairs={{0,7},{1,6},{2,5},{3,4},{4,3},{5,2},{6,1},{7,0},{8,15},{9,14},{10,... | collective-permute-start | bytes 688136 | tf_op jit(solution)/shard_map/ppermute | solution.py:46
  32.6 46.9 %collective-permute-start.5 = (bf16[1,896,128]{2,1,0:T(8,128)(2,1)S(1)}, bf16[1,896,128]{2,1,0:T(8,128)(2,1)}, u32[]{:S(2)}, u32[]{:S(2)}) collective-permute-start(bf16[1,896,128]{2,1,0:T(8,128)(2,1)S(1)} %get-tuple-element.39), channel_id=1, source_target_pairs={{0,6},{1,7},{2,4},{3,5},{4,2},{5,3},{6,0},{7,1},{8,14},{9,15},{10,... | collective-permute-start | bytes 688136 | tf_op jit(solution)/shard_map/ppermute | solution.py:46
  34.6 44.0 %collective-permute-start.4 = (bf16[1,896,128]{2,1,0:T(8,128)(2,1)S(1)}, bf16[1,896,128]{2,1,0:T(8,128)(2,1)}, u32[]{:S(2)}, u32[]{:S(2)}) collective-permute-start(bf16[1,896,128]{2,1,0:T(8,128)(2,1)S(1)} %get-tuple-element.40), channel_id=1, source_target_pairs={{0,5},{1,4},{2,7},{3,6},{4,1},{5,0},{6,3},{7,2},{8,13},{9,12},{10,... | collective-permute-start | bytes 688136 | tf_op jit(solution)/shard_map/ppermute | solution.py:46
  37.6 34.4 %collective-permute-start.3 = (bf16[1,896,128]{2,1,0:T(8,128)(2,1)S(1)}, bf16[1,896,128]{2,1,0:T(8,128)(2,1)S(1)}, u32[]{:S(2)}, u32[]{:S(2)}) collective-permute-start(bf16[1,896,128]{2,1,0:T(8,128)(2,1)S(1)} %get-tuple-element.41), channel_id=1, source_target_pairs={{0,4},{1,5},{2,6},{3,7},{4,0},{5,1},{6,2},{7,3},{8,12},{9,13},{10,... | collective-permute-start | bytes 688136 | tf_op jit(solution)/shard_map/ppermute | solution.py:46
  74.3 11.5 %all-to-all-start.1 = ((bf16[4,64,896]{2,1,0:T(8,128)(2,1)}), bf16[4,64,896]{2,1,0:T(8,128)(2,1)S(1)}, u32[]{:S(2)}, u32[]{:S(2)}) async-start(bf16[4,64,896]{2,1,0:T(8,128)(2,1)} %bitcast.13), calls=%async_computation.1 | async-start | bytes 917504 | tf_op jit(solution)/shard_map/all_to_all | solution.py:23
  89.3 40.9 %all-to-all-start.2 = ((bf16[8,272,128]{2,1,0:T(8,128)(2,1)}), bf16[8,272,128]{2,1,0:T(8,128)(2,1)S(1)}, u32[]{:S(2)}, u32[]{:S(2)}) async-start(bf16[8,272,128]{2,1,0:T(8,128)(2,1)} %pad_maximum_fusion), calls=%async_computation.2 | async-start | bytes 1114112 | tf_op jit(solution)/shard_map/all_to_all | solution.py:23
  96.3 34.2 %collective-permute-start.13 = (bf16[1,128,896]{2,1,0:T(8,128)(2,1)}, bf16[1,128,896]{2,1,0:T(8,128)(2,1)}, u32[]{:S(2)}, u32[]{:S(2)}) collective-permute-start(bf16[1,128,896]{2,1,0:T(8,128)(2,1)} %get-tuple-element.31), channel_id=1, source_target_pairs={{0,7},{1,6},{2,5},{3,4},{4,3},{5,2},{6,1},{7,0},{8,15},{9,14},{10,... | collective-permute-start | bytes 688136 | tf_op jit(solution)/shard_map/ppermute | solution.py:46
  101.6 36.4 %collective-permute-start.12 = (bf16[1,128,896]{2,1,0:T(8,128)(2,1)}, bf16[1,128,896]{2,1,0:T(8,128)(2,1)}, u32[]{:S(2)}, u32[]{:S(2)}) collective-permute-start(bf16[1,128,896]{2,1,0:T(8,128)(2,1)} %get-tuple-element.32), channel_id=1, source_target_pairs={{0,6},{1,7},{2,4},{3,5},{4,2},{5,3},{6,0},{7,1},{8,14},{9,15},{10,... | collective-permute-start | bytes 688136 | tf_op jit(solution)/shard_map/ppermute | solution.py:46
  103.5 60.4 %collective-permute-start.11 = (bf16[1,128,896]{2,1,0:T(8,128)(2,1)}, bf16[1,128,896]{2,1,0:T(8,128)(2,1)}, u32[]{:S(2)}, u32[]{:S(2)}) collective-permute-start(bf16[1,128,896]{2,1,0:T(8,128)(2,1)} %get-tuple-element.33), channel_id=1, source_target_pairs={{0,5},{1,4},{2,7},{3,6},{4,1},{5,0},{6,3},{7,2},{8,13},{9,12},{10,... | collective-permute-start | bytes 688136 | tf_op jit(solution)/shard_map/ppermute | solution.py:46
  106.3 57.7 %collective-permute-start.10 = (bf16[1,128,896]{2,1,0:T(8,128)(2,1)}, bf16[1,128,896]{2,1,0:T(8,128)(2,1)}, u32[]{:S(2)}, u32[]{:S(2)}) collective-permute-start(bf16[1,128,896]{2,1,0:T(8,128)(2,1)} %get-tuple-element.34), channel_id=1, source_target_pairs={{0,4},{1,5},{2,6},{3,7},{4,0},{5,1},{6,2},{7,3},{8,12},{9,13},{10,... | collective-permute-start | bytes 688136 | tf_op jit(solution)/shard_map/ppermute | solution.py:46
  110.1 53.9 %collective-permute-start.9 = (bf16[1,128,896]{2,1,0:T(8,128)(2,1)S(1)}, bf16[1,128,896]{2,1,0:T(8,128)(2,1)}, u32[]{:S(2)}, u32[]{:S(2)}) collective-permute-start(bf16[1,128,896]{2,1,0:T(8,128)(2,1)S(1)} %get-tuple-element.35), channel_id=1, source_target_pairs={{0,3},{1,2},{2,1},{3,0},{4,7},{5,6},{6,5},{7,4},{8,11},{9,10},{10,... | collective-permute-start | bytes 688136 | tf_op jit(solution)/shard_map/ppermute | solution.py:46
  130.4 33.5 %collective-permute-start.8 = (bf16[1,128,896]{2,1,0:T(8,128)(2,1)S(1)}, bf16[1,128,896]{2,1,0:T(8,128)(2,1)S(1)}, u32[]{:S(2)}, u32[]{:S(2)}) collective-permute-start(bf16[1,128,896]{2,1,0:T(8,128)(2,1)S(1)} %get-tuple-element.36), channel_id=1, source_target_pairs={{0,2},{1,3},{2,0},{3,1},{4,6},{5,7},{6,4},{7,5},{8,10},{9,11},{10,... | collective-permute-start | bytes 688136 | tf_op jit(solution)/shard_map/ppermute | solution.py:46
  138.1 26.0 %collective-permute-start.7 = (bf16[1,128,896]{2,1,0:T(8,128)(2,1)S(1)}, bf16[1,128,896]{2,1,0:T(8,128)(2,1)S(1)}, u32[]{:S(2)}, u32[]{:S(2)}) collective-permute-start(bf16[1,128,896]{2,1,0:T(8,128)(2,1)S(1)} %get-tuple-element.37), channel_id=1, source_target_pairs={{0,1},{1,0},{2,3},{3,2},{4,5},{5,4},{6,7},{7,6},{8,9},{9,8},{10,11... | collective-permute-start | bytes 688136 | tf_op jit(solution)/shard_map/ppermute | solution.py:46
  170.5 12.2 %all-to-all-start.3 = ((bf16[4,64,896]{2,1,0:T(8,128)(2,1)}), bf16[4,64,896]{2,1,0:T(8,128)(2,1)S(1)}, u32[]{:S(2)}, u32[]{:S(2)}) async-start(bf16[4,64,896]{2,1,0:T(8,128)(2,1)} %bitcast.24), calls=%async_computation.3 | async-start | bytes 917504 | tf_op jit(solution)/shard_map/all_to_all | solution.py:23
  183.2 57.9 %copy-start.2 = (bf16[896,8,128]{0,2,1:T(8,128)(2,1)S(1)}, bf16[896,8,128]{0,2,1:T(8,128)(2,1)}, u32[]{:S(2)}) copy-start(bf16[896,8,128]{0,2,1:T(8,128)(2,1)} %copy.43) | copy-start | bytes 5505028
  183.2 17.2 %collective-permute-start.14 = (bf16[64,896]{1,0:T(8,128)(2,1)S(1)}, bf16[64,896]{1,0:T(8,128)(2,1)S(1)}, u32[]{:S(2)}, u32[]{:S(2)}) collective-permute-start(bf16[64,896]{1,0:T(8,128)(2,1)S(1)} %slice.118), channel_id=1, source_target_pairs={{0,8},{1,9},{2,10},{3,11},{4,12},{5,13},{6,14},{7,15},{8,0},{9,1},... | collective-permute-start | bytes 344072 | tf_op jit(solution)/shard_map/ppermute | solution.py:30
  200.5 16.6 %collective-permute-start.15 = (bf16[64,896]{1,0:T(8,128)(2,1)S(1)}, bf16[64,896]{1,0:T(8,128)(2,1)S(1)}, u32[]{:S(2)}, u32[]{:S(2)}) collective-permute-start(bf16[64,896]{1,0:T(8,128)(2,1)S(1)} %fusion.16), channel_id=1, source_target_pairs={{0,72},{1,73},{2,74},{3,75},{4,76},{5,77},{6,78},{7,79},{8,64},{9,... | collective-permute-start | bytes 344072 | tf_op jit(solution)/shard_map/ppermute | solution.py:40
  217.1 12.9 %collective-permute-start.16 = (bf16[64,896]{1,0:T(8,128)(2,1)S(1)}, bf16[64,896]{1,0:T(8,128)(2,1)S(1)}, u32[]{:S(2)}, u32[]{:S(2)}) collective-permute-start(bf16[64,896]{1,0:T(8,128)(2,1)S(1)} %collective-permute-done.15), channel_id=1, source_target_pairs={{0,8},{1,9},{2,10},{3,11},{4,12},{5,13},{6,14},{7,15},{8,0},{9,1},... | collective-permute-start | bytes 344072 | tf_op jit(solution)/shard_map/ppermute | solution.py:30
  278.5 12.2 %all-to-all-start.6 = ((bf16[4,64,896]{2,1,0:T(8,128)(2,1)}), bf16[4,64,896]{2,1,0:T(8,128)(2,1)S(1)}, u32[]{:S(2)}, u32[]{:S(2)}) async-start(bf16[4,64,896]{2,1,0:T(8,128)(2,1)} %bitcast.37), calls=%async_computation.6 | async-start | bytes 917504 | tf_op jit(solution)/shard_map/all_to_all | solution.py:23
  314.6 17.9 %collective-permute-start.17 = (bf16[8,7168]{1,0:T(8,128)(2,1)S(1)}, bf16[8,7168]{1,0:T(8,128)(2,1)S(1)}, u32[]{:S(2)}, u32[]{:S(2)}) collective-permute-start(bf16[8,7168]{1,0:T(8,128)(2,1)S(1)} %bitcast.130), channel_id=1, source_target_pairs={{0,72},{1,73},{2,74},{3,75},{4,76},{5,77},{6,78},{7,79},{8,64},{9,... | collective-permute-start | bytes 344072 | tf_op jit(solution)/shard_map/ppermute | solution.py:40
  (23 other events, 195.8 us)

commit v4 on v3

--- a/solution.py
+++ b/solution.py
@@ -58,6 +58,36 @@
             slices, came[step - 1], place % GROUP ^ step, 0
         )
     return slices
+
+
+def paired(slices, place):
+    count = lax.axis_size("expert")
+    core = place % 2
+    slices = slices.reshape((GROUP // 2, 2) + slices.shape[1:])
+    keep = lax.dynamic_index_in_dim(slices, core, 1, keepdims=False)
+    give = lax.dynamic_index_in_dim(slices, 1 - core, 1, keepdims=False)
+    got = lax.ppermute(give, "expert", [(i, i ^ 1) for i in range(count)])
+    return lax.dynamic_slice_in_dim(jnp.stack([keep, got, keep], axis=1), core, 2, 1)
+
+
+def chips_spread(pair, place):
+    count = lax.axis_size("expert")
+    chip = place // 2 % (GROUP // 2)
+    return [
+        lax.ppermute(
+            lax.dynamic_index_in_dim(pair, chip ^ step, 0),
+            "expert",
+            [(i, i ^ 2 * step) for i in range(count)],
+        )
+        for step in range(1, GROUP // 2)
+    ]
+
+
+def chips_gathered(pair, came, place):
+    chip = place // 2 % (GROUP // 2)
+    for step in range(1, GROUP // 2):
+        pair = lax.dynamic_update_slice_in_dim(pair, came[step - 1], chip ^ step, 0)
+    return pair
 
 
 def head(value):
@@ -111,6 +141,7 @@
         [sliced, jnp.broadcast_to(facts[None], (GROUP, rows_dev, LANES))], axis=2
     )
     arrived = exchange(jnp.concatenate([sliced, sliced]), same_row)
+    arrived, down_rows = lax.optimization_barrier((arrived, w_down[0]))
     arrived = arrived.reshape(HALVES, block, part + LANES)
     arrived = lax.dynamic_slice_in_dim(jnp.concatenate([arrived, arrived]), half, HALVES, 0)
     arrived = arrived.reshape(HALVES * block, part + LANES)
@@ -119,9 +150,8 @@
     routes = facts[:, : 4 * passes * top].reshape(HALVES * block, 4, passes, top)
 
     up_slices = w_up[0].reshape(GROUP, part, HID_DEV)
-    up = gathered(up_slices, spread(up_slices, place), place)
-    up = up.transpose(1, 0, 2).reshape(part, HID)
-    down_slices = w_down[0].reshape(HID_DEV, GROUP, part).transpose(1, 0, 2)
+    up_came = spread(up_slices, place)
+    down_pair = paired(down_rows.reshape(HID_DEV, GROUP, part).transpose(1, 0, 2), place)
     gain = lax.dynamic_slice_in_dim(norm_gain[0], place % GROUP * part, part, 0)
 
     for t in range(passes):
@@ -131,8 +161,10 @@
         slots = jnp.dot(picker, rows, preferred_element_type=jnp.float32).astype(jnp.bfloat16)
         slots = exchange(slots, same_slice)
         if t == 0:
-            slots, down_slices = lax.optimization_barrier((slots, down_slices))
-            came = spread(down_slices, place)
+            slots, up_came, down_pair = lax.optimization_barrier((slots, up_came, down_pair))
+            down_came = chips_spread(down_pair, place)
+            up = gathered(up_slices, up_came, place)
+            up = up.transpose(1, 0, 2).reshape(part, HID)
         values = slots.astype(jnp.float32)
         squares = jnp.sum(values * values, axis=1)
         partial = jnp.dot(
@@ -153,8 +185,8 @@
         active = jax.nn.silu(sums[:held] * scale[:, None]).astype(jnp.bfloat16)
         active = lax.all_gather(active, "expert", axis_index_groups=same_expert)
         if t == 0:
-            active, came = lax.optimization_barrier((active, came))
-            down = gathered(down_slices, came, place).reshape(HID, part)
+            active, down_came = lax.optimization_barrier((active, down_came))
+            down = chips_gathered(down_pair, down_came, place).reshape(HID, part)
         active = active.transpose(1, 0, 2).reshape(held, HID)
         outputs = jnp.dot(active, down, preferred_element_type=jnp.float32).astype(jnp.bfloat16)
         outputs = exchange(outputs, same_slice)

time: 335 us -> 341 us (1.018)
  starting transfers between devices: 92 us -> 72.5 us
  local copies, waits for them, and re-layouts: 18.5 us -> 32.6 us
  waiting for transfers between devices: 118 us -> 124 us
    ppermute x14 -> x7, starting transfers between devices: 48.3 us -> 22 us  [spread(): lax.ppermute(lax.dynamic_index_in_dim(slices, place % GROUP ^ step, 0), '...]
    all_to_all x5, waiting for transfers between devices: 35.7 us -> 55.7 us  [exchange(): lax.all_to_all(value, 'expert', split_axis=0, concat_axis=0, axis_index_g...]
    ppermute x14 -> x7, waiting for transfers between devices: 30.6 us -> 13.2 us  [spread(): lax.ppermute(lax.dynamic_index_in_dim(slices, place % GROUP ^ step, 0), '...]
    ppermute x0 -> x4, starting transfers between devices: none -> 11.2 us  [the longest x3 9.26 us: chips_spread(): lax.ppermute(lax.dynamic_index_in_dim(pair, chip ^ step, 0), 'expert', [(...]
    ppermute x2, waiting for transfers between devices: 21 us -> 25.3 us  [other_half(): return lax.ppermute(value, 'expert', [(i, i ^ GROUP) for i in range(count)])]
    all_gather x2, blocking collectives: 39.2 us -> 43.5 us  [body(): active = lax.all_gather(active, 'expert', axis_index_groups=same_expert)]
    dynamic_update_slice x13 -> x7, local copies, waits for them, and re-layouts: 7.94 us -> 11.5 us  [gathered(): lax.dynamic_update_slice_in_dim(slices, came[step - 1], place % GROUP ^ s...]
  transfers between devices with their start and end apart: 23 -> 20, of which waited for: 9 -> 12; matrix products, arithmetic and copies ran while one was open for 4% -> 4% of each run, Pallas kernels for 0% -> 0%
where the time goes in v4:
time: 341 us; the launch traced here: 339 us
  waiting for transfers between devices  124 us (36%)
  blocking collectives  95.2 us (28%)
  starting transfers between devices  72.5 us (21%)
  local copies, waits for them, and re-layouts  32.6 us (10%)
  matrix products  8.69 us (3%)
  other arithmetic  5.69 us (2%)
    all_to_all x5, waiting for transfers between devices, exchange(): lax.all_to_all(value, 'expert', split_axis=0, concat_axis=0, axis_index_g...  55.7 us
    all_to_all x3, blocking collectives, exchange(): lax.all_to_all(value, 'expert', split_axis=0, concat_axis=0, axis_index_g...  51.7 us
    all_gather x2, blocking collectives, body(): active = lax.all_gather(active, 'expert', axis_index_groups=same_expert)  43.5 us
    ppermute x2, waiting for transfers between devices, next_section(): return lax.ppermute(value, ('section', 'expert'), route)  29.7 us
    all_to_all x5, starting transfers between devices, exchange(): lax.all_to_all(value, 'expert', split_axis=0, concat_axis=0, axis_index_g...  29.6 us
    ppermute x2, waiting for transfers between devices, other_half(): return lax.ppermute(value, 'expert', [(i, i ^ GROUP) for i in range(count)])  25.3 us
    ppermute x7, starting transfers between devices, spread(): lax.ppermute(lax.dynamic_index_in_dim(slices, place % GROUP ^ step, 0), '...  22 us
    ppermute x7, waiting for transfers between devices, spread(): lax.ppermute(lax.dynamic_index_in_dim(slices, place % GROUP ^ step, 0), '...  13.2 us
  transfers between devices with their start and end apart: 20, of which 12 were waited for; matrix products, arithmetic and copies ran while one was open for 4% of the time, Pallas kernels for 0%

profile of v4, /device:TPU:7, one launch (start us, length us, event | category | flops | bytes accessed | tf_op | source)
XLA Modules:
  0.0 339.5 jit_solution(15147001975278661671)
XLA Ops:
  2.6 13.2 %all-to-all-start = ((bf16[16,8,1024]{2,1,0:T(8,128)(2,1)}), bf16[16,8,1024]{2,1,0:T(8,128)(2,1)S(1)}, u32[]{:S(2)}, u32[]{:S(2)}) async-start(bf16[16,8,1024]{2,1,0:T(8,128)(2,1)} %maximum_maximum_fusion), calls=%async_computation | async-start | bytes 524288 | tf_op jit(solution)/shard_map/all_to_all | solution.py:23
  17.0 5.3 %collective-permute-start.6 = (bf16[1,896,128]{2,1,0:T(8,128)(2,1)}, bf16[1,896,128]{2,1,0:T(8,128)(2,1)}, u32[]{:S(2)}, u32[]{:S(2)}) collective-permute-start(bf16[1,896,128]{2,1,0:T(8,128)(2,1)} %get-tuple-element.46), channel_id=1, source_target_pairs={{0,7},{1,6},{2,5},{3,4},{4,3},{5,2},{6,1},{7,0},{8,15},{9,14},{10,... | collective-permute-start | bytes 688136 | tf_op jit(solution)/shard_map/ppermute | solution.py:46
  28.4 14.2 %all-to-all-done = bf16[16,8,1024]{2,1,0:T(8,128)(2,1)S(1)} async-done(((bf16[16,8,1024]{2,1,0:T(8,128)(2,1)}), bf16[16,8,1024]{2,1,0:T(8,128)(2,1)S(1)}, u32[]{:S(2)}, u32[]{:S(2)}) %all-to-all-start) | async-done | bytes 262176 | tf_op jit(solution)/shard_map/all_to_all | solution.py:23
  50.9 4.2 %all-to-all-start.1 = ((bf16[4,64,896]{2,1,0:T(8,128)(2,1)}), bf16[4,64,896]{2,1,0:T(8,128)(2,1)S(1)}, u32[]{:S(2)}, u32[]{:S(2)}) async-start(bf16[4,64,896]{2,1,0:T(8,128)(2,1)} %bitcast.14), calls=%async_computation.1 | async-start | bytes 917504 | tf_op jit(solution)/shard_map/all_to_all | solution.py:23
  72.2 4.0 %collective-permute-done.4 = bf16[1,896,128]{2,1,0:T(8,128)(2,1)} collective-permute-done((bf16[1,896,128]{2,1,0:T(8,128)(2,1)}, bf16[1,896,128]{2,1,0:T(8,128)(2,1)}, u32[]{:S(2)}, u32[]{:S(2)}) %collective-permute-start.4) | collective-permute-done | bytes 229408 | tf_op jit(solution)/shard_map/ppermute | solution.py:46
  76.2 4.9 %collective-permute-done.3 = bf16[1,896,128]{2,1,0:T(8,128)(2,1)} collective-permute-done((bf16[1,896,128]{2,1,0:T(8,128)(2,1)}, bf16[1,896,128]{2,1,0:T(8,128)(2,1)}, u32[]{:S(2)}, u32[]{:S(2)}) %collective-permute-start.3) | collective-permute-done | bytes 229408 | tf_op jit(solution)/shard_map/ppermute | solution.py:46
  81.4 4.0 %collective-permute-done.1 = bf16[1,896,128]{2,1,0:T(8,128)(2,1)} collective-permute-done((bf16[1,896,128]{2,1,0:T(8,128)(2,1)}, bf16[1,896,128]{2,1,0:T(8,128)(2,1)}, u32[]{:S(2)}, u32[]{:S(2)}) %collective-permute-start.1) | collective-permute-done | bytes 229408 | tf_op jit(solution)/shard_map/ppermute | solution.py:46
  96.9 3.8 %copy.66 = bf16[896,8,128]{0,2,1:T(8,128)(2,1)} copy(bf16[896,8,128]{2,0,1:T(8,128)(2,1)} %bitcast.107) | data formatting | bytes 3670016 | tf_op jit(solution)/shard_map/transpose | solution.py:167
  104.1 4.5 %all-to-all-start.2 = ((bf16[8,272,128]{2,1,0:T(8,128)(2,1)}), bf16[8,272,128]{2,1,0:T(8,128)(2,1)S(1)}, u32[]{:S(2)}, u32[]{:S(2)}) async-start(bf16[8,272,128]{2,1,0:T(8,128)(2,1)} %pad_maximum_fusion), calls=%async_computation.2 | async-start | bytes 1114112 | tf_op jit(solution)/shard_map/all_to_all | solution.py:23
  109.7 5.1 %collective-permute-start.10 = (bf16[1,2,128,896]{3,2,1,0:T(8,128)(2,1)}, bf16[1,2,128,896]{3,2,1,0:T(8,128)(2,1)S(1)}, u32[]{:S(2)}, u32[]{:S(2)}) collective-permute-start(bf16[1,2,128,896]{3,2,1,0:T(8,128)(2,1)} %get-tuple-element.41), channel_id=1, source_target_pairs={{0,6},{1,7},{2,4},{3,5},{4,2},{5,3},{6,0},{7,1},{8,14},{9,15},{10,... | collective-permute-start | bytes 1376264 | tf_op jit(solution)/shard_map/ppermute | solution.py:77
  119.0 24.4 %all-to-all-done.2 = bf16[8,272,128]{2,1,0:T(8,128)(2,1)S(1)} async-done(((bf16[8,272,128]{2,1,0:T(8,128)(2,1)}), bf16[8,272,128]{2,1,0:T(8,128)(2,1)S(1)}, u32[]{:S(2)}, u32[]{:S(2)}) %all-to-all-start.2) | async-done | bytes 557088 | tf_op jit(solution)/shard_map/all_to_all | solution.py:23
  143.7 28.3 %all-gather = bf16[2048,128]{1,0:T(8,128)(2,1)S(1)} all-gather(bf16[256,128]{1,0:T(8,128)(2,1)S(1)} %multiply_convert_fusion.1), channel_id=2, replica_groups={{0,1,2,3,4,5,6,7},{8,9,10,11,12,13,14,15},{16,17,18,19,20,21,22,23},{24..., dimensions={0}, use_global_device_ids=true | all-gather | bytes 589824 | tf_op jit(solution)/shard_map/all_gather | solution.py:186
  177.2 4.2 %all-to-all-start.3 = ((bf16[4,64,896]{2,1,0:T(8,128)(2,1)}), bf16[4,64,896]{2,1,0:T(8,128)(2,1)S(1)}, u32[]{:S(2)}, u32[]{:S(2)}) async-start(bf16[4,64,896]{2,1,0:T(8,128)(2,1)} %bitcast.31), calls=%async_computation.3 | async-start | bytes 917504 | tf_op jit(solution)/shard_map/all_to_all | solution.py:23
  181.6 8.3 %all-to-all-done.3 = bf16[4,64,896]{2,1,0:T(8,128)(2,1)S(1)} async-done(((bf16[4,64,896]{2,1,0:T(8,128)(2,1)}), bf16[4,64,896]{2,1,0:T(8,128)(2,1)S(1)}, u32[]{:S(2)}, u32[]{:S(2)}) %all-to-all-start.3) | async-done | bytes 458784 | tf_op jit(solution)/shard_map/all_to_all | solution.py:23
  190.5 4.0 %collective-permute-start.11 = (bf16[64,896]{1,0:T(8,128)(2,1)S(1)}, bf16[64,896]{1,0:T(8,128)(2,1)S(1)}, u32[]{:S(2)}, u32[]{:S(2)}) collective-permute-start(bf16[64,896]{1,0:T(8,128)(2,1)S(1)} %slice.118), channel_id=1, source_target_pairs={{0,8},{1,9},{2,10},{3,11},{4,12},{5,13},{6,14},{7,15},{8,0},{9,1},... | collective-permute-start | bytes 344072 | tf_op jit(solution)/shard_map/ppermute | solution.py:30
  194.4 14.4 %collective-permute-done.11 = bf16[64,896]{1,0:T(8,128)(2,1)S(1)} collective-permute-done((bf16[64,896]{1,0:T(8,128)(2,1)S(1)}, bf16[64,896]{1,0:T(8,128)(2,1)S(1)}, u32[]{:S(2)}, u32[]{:S(2)}) %collective-permute-start.11) | collective-permute-done | bytes 114720 | tf_op jit(solution)/shard_map/ppermute | solution.py:30
  210.9 13.7 %collective-permute-done.12 = bf16[64,896]{1,0:T(8,128)(2,1)S(1)} collective-permute-done((bf16[64,896]{1,0:T(8,128)(2,1)S(1)}, bf16[64,896]{1,0:T(8,128)(2,1)S(1)}, u32[]{:S(2)}, u32[]{:S(2)}) %collective-permute-start.12) | collective-permute-done | bytes 114720 | tf_op jit(solution)/shard_map/ppermute | solution.py:40
  226.5 10.9 %collective-permute-done.13 = bf16[64,896]{1,0:T(8,128)(2,1)S(1)} collective-permute-done((bf16[64,896]{1,0:T(8,128)(2,1)S(1)}, bf16[64,896]{1,0:T(8,128)(2,1)S(1)}, u32[]{:S(2)}, u32[]{:S(2)}) %collective-permute-start.13) | collective-permute-done | bytes 114720 | tf_op jit(solution)/shard_map/ppermute | solution.py:30
  237.8 10.5 %all_to_all.59 = bf16[4,64,896]{2,1,0:T(8,128)(2,1)S(1)} all-to-all(bf16[4,64,896]{2,1,0:T(8,128)(2,1)S(1)} %bitcast.120), channel_id=1, replica_groups={{0,16,32,48},{1,17,33,49},{2,18,34,50},{3,19,35,51},{4,20,36,52},{5,21,..., dimensions={0} | all-to-all | bytes 917504 | tf_op jit(solution)/shard_map/all_to_all | solution.py:23
  249.5 19.4 %all_to_all.60 = bf16[8,272,128]{2,1,0:T(8,128)(2,1)S(1)} all-to-all(bf16[8,272,128]{2,1,0:T(8,128)(2,1)S(1)} %pad_maximum_fusion.1), channel_id=1, replica_groups={{0,1,2,3,4,5,6,7},{8,9,10,11,12,13,14,15},{16,17,18,19,20,21,22,23},{24..., dimensions={0} | all-to-all | bytes 1114112 | tf_op jit(solution)/shard_map/all_to_all | solution.py:23
  269.2 15.2 %all-gather.1 = bf16[2048,128]{1,0:T(8,128)(2,1)S(1)} all-gather(bf16[256,128]{1,0:T(8,128)(2,1)S(1)} %multiply_convert_fusion), channel_id=3, replica_groups={{0,1,2,3,4,5,6,7},{8,9,10,11,12,13,14,15},{16,17,18,19,20,21,22,23},{24..., dimensions={0}, use_global_device_ids=true | all-gather | bytes 589824 | tf_op jit(solution)/shard_map/all_gather | solution.py:186
  289.7 8.7 %all-to-all-done.6 = bf16[4,64,896]{2,1,0:T(8,128)(2,1)S(1)} async-done(((bf16[4,64,896]{2,1,0:T(8,128)(2,1)}), bf16[4,64,896]{2,1,0:T(8,128)(2,1)S(1)}, u32[]{:S(2)}, u32[]{:S(2)}) %all-to-all-start.6) | async-done | bytes 458784 | tf_op jit(solution)/shard_map/all_to_all | solution.py:23
  299.2 21.7 %all_to_all.61 = bf16[16,8,896]{2,1,0:T(8,128)(2,1)S(1)} all-to-all(bf16[16,8,896]{2,1,0:T(8,128)(2,1)S(1)} %bitcast.125), channel_id=1, replica_groups={{0,1,2,3,4,5,6,7,8,9,10,11,12,13,14,15},{16,17,18,19,20,21,22,23,24,25,..., dimensions={0} | all-to-all | bytes 458752 | tf_op jit(solution)/shard_map/all_to_all | solution.py:23
  322.8 16.0 %collective-permute-done.14 = bf16[8,7168]{1,0:T(8,128)(2,1)S(1)} collective-permute-done((bf16[8,7168]{1,0:T(8,128)(2,1)S(1)}, bf16[8,7168]{1,0:T(8,128)(2,1)S(1)}, u32[]{:S(2)}, u32[]{:S(2)}) %collective-permute-start.14) | collective-permute-done | bytes 114720 | tf_op jit(solution)/shard_map/ppermute | solution.py:40
  (159 shorter events, 75.6 us)
Async XLA Ops:
  0.0 69.9 %copy-start = (f32[1,7168]{1,0:T(1,128)S(1)}, f32[1,7168]{1,0:T(1,128)}, u32[]{:S(2)}) copy-start(f32[1,7168]{1,0:T(1,128)} %param.7) | copy-start | bytes 86020
  1.6 15.5 %copy-start.1 = (bf16[1,7168,128]{2,1,0:T(8,128)(2,1)}, bf16[1,7168,128]{2,1,0:T(8,128)(2,1)S(1)}, u32[]{:S(2)}) copy-start(bf16[1,7168,128]{2,1,0:T(8,128)(2,1)S(1)} %copy.99) | copy-start | bytes 5505028
  2.6 40.0 %all-to-all-start = ((bf16[16,8,1024]{2,1,0:T(8,128)(2,1)}), bf16[16,8,1024]{2,1,0:T(8,128)(2,1)S(1)}, u32[]{:S(2)}, u32[]{:S(2)}) async-start(bf16[16,8,1024]{2,1,0:T(8,128)(2,1)} %maximum_maximum_fusion), calls=%async_computation | async-start | bytes 524288 | tf_op jit(solution)/shard_map/all_to_all | solution.py:23
  17.0 45.0 %collective-permute-start.6 = (bf16[1,896,128]{2,1,0:T(8,128)(2,1)}, bf16[1,896,128]{2,1,0:T(8,128)(2,1)}, u32[]{:S(2)}, u32[]{:S(2)}) collective-permute-start(bf16[1,896,128]{2,1,0:T(8,128)(2,1)} %get-tuple-element.46), channel_id=1, source_target_pairs={{0,7},{1,6},{2,5},{3,4},{4,3},{5,2},{6,1},{7,0},{8,15},{9,14},{10,... | collective-permute-start | bytes 688136 | tf_op jit(solution)/shard_map/ppermute | solution.py:46
  22.4 42.1 %collective-permute-start.5 = (bf16[1,896,128]{2,1,0:T(8,128)(2,1)}, bf16[1,896,128]{2,1,0:T(8,128)(2,1)}, u32[]{:S(2)}, u32[]{:S(2)}) collective-permute-start(bf16[1,896,128]{2,1,0:T(8,128)(2,1)} %get-tuple-element.47), channel_id=1, source_target_pairs={{0,6},{1,7},{2,4},{3,5},{4,2},{5,3},{6,0},{7,1},{8,14},{9,15},{10,... | collective-permute-start | bytes 688136 | tf_op jit(solution)/shard_map/ppermute | solution.py:46
  28.3 20.8 %copy-start.20 = (s32[4]{0:T(128)}, s32[4]{0:T(128)S(1)}, u32[]{:S(2)}) copy-start(s32[4]{0:T(128)S(1)} %multiply_add_fusion) | copy-start | bytes 52
  47.2 20.0 %collective-permute-start.7 = (bf16[4,128,896]{2,1,0:T(8,128)(2,1)S(1)}, bf16[4,128,896]{2,1,0:T(8,128)(2,1)S(1)}, u32[]{:S(2)}, u32[]{:S(2)}) collective-permute-start(bf16[4,128,896]{2,1,0:T(8,128)(2,1)S(1)} %get-tuple-element.44), channel_id=1, source_target_pairs={{0,1},{1,0},{2,3},{3,2},{4,5},{5,4},{6,7},{7,6},{8,9},{9,8},{10,11... | collective-permute-start | bytes 2752520 | tf_op jit(solution)/shard_map/ppermute | solution.py:69
  50.9 34.4 %all-to-all-start.1 = ((bf16[4,64,896]{2,1,0:T(8,128)(2,1)}), bf16[4,64,896]{2,1,0:T(8,128)(2,1)S(1)}, u32[]{:S(2)}, u32[]{:S(2)}) async-start(bf16[4,64,896]{2,1,0:T(8,128)(2,1)} %bitcast.14), calls=%async_computation.1 | async-start | bytes 917504 | tf_op jit(solution)/shard_map/all_to_all | solution.py:23
  55.1 21.1 %collective-permute-start.4 = (bf16[1,896,128]{2,1,0:T(8,128)(2,1)}, bf16[1,896,128]{2,1,0:T(8,128)(2,1)}, u32[]{:S(2)}, u32[]{:S(2)}) collective-permute-start(bf16[1,896,128]{2,1,0:T(8,128)(2,1)} %get-tuple-element.48), channel_id=1, source_target_pairs={{0,5},{1,4},{2,7},{3,6},{4,1},{5,0},{6,3},{7,2},{8,13},{9,12},{10,... | collective-permute-start | bytes 688136 | tf_op jit(solution)/shard_map/ppermute | solution.py:46
  58.6 22.6 %collective-permute-start.3 = (bf16[1,896,128]{2,1,0:T(8,128)(2,1)}, bf16[1,896,128]{2,1,0:T(8,128)(2,1)}, u32[]{:S(2)}, u32[]{:S(2)}) collective-permute-start(bf16[1,896,128]{2,1,0:T(8,128)(2,1)} %get-tuple-element.49), channel_id=1, source_target_pairs={{0,4},{1,5},{2,6},{3,7},{4,0},{5,1},{6,2},{7,3},{8,12},{9,13},{10,... | collective-permute-start | bytes 688136 | tf_op jit(solution)/shard_map/ppermute | solution.py:46
  62.0 19.4 %collective-permute-start.2 = (bf16[1,896,128]{2,1,0:T(8,128)(2,1)}, bf16[1,896,128]{2,1,0:T(8,128)(2,1)}, u32[]{:S(2)}, u32[]{:S(2)}) collective-permute-start(bf16[1,896,128]{2,1,0:T(8,128)(2,1)} %get-tuple-element.50), channel_id=1, source_target_pairs={{0,3},{1,2},{2,1},{3,0},{4,7},{5,6},{6,5},{7,4},{8,11},{9,10},{10,... | collective-permute-start | bytes 688136 | tf_op jit(solution)/shard_map/ppermute | solution.py:46
  64.5 20.9 %collective-permute-start.1 = (bf16[1,896,128]{2,1,0:T(8,128)(2,1)}, bf16[1,896,128]{2,1,0:T(8,128)(2,1)}, u32[]{:S(2)}, u32[]{:S(2)}) collective-permute-start(bf16[1,896,128]{2,1,0:T(8,128)(2,1)} %get-tuple-element.51), channel_id=1, source_target_pairs={{0,2},{1,3},{2,0},{3,1},{4,6},{5,7},{6,4},{7,5},{8,10},{9,11},{10,... | collective-permute-start | bytes 688136 | tf_op jit(solution)/shard_map/ppermute | solution.py:46
  67.2 18.2 %collective-permute-start = (bf16[1,896,128]{2,1,0:T(8,128)(2,1)}, bf16[1,896,128]{2,1,0:T(8,128)(2,1)}, u32[]{:S(2)}, u32[]{:S(2)}) collective-permute-start(bf16[1,896,128]{2,1,0:T(8,128)(2,1)} %get-tuple-element.52), channel_id=1, source_target_pairs={{0,1},{1,0},{2,3},{3,2},{4,5},{5,4},{6,7},{7,6},{8,9},{9,8},{10,11... | collective-permute-start | bytes 688136 | tf_op jit(solution)/shard_map/ppermute | solution.py:46
  104.1 39.4 %all-to-all-start.2 = ((bf16[8,272,128]{2,1,0:T(8,128)(2,1)}), bf16[8,272,128]{2,1,0:T(8,128)(2,1)S(1)}, u32[]{:S(2)}, u32[]{:S(2)}) async-start(bf16[8,272,128]{2,1,0:T(8,128)(2,1)} %pad_maximum_fusion), calls=%async_computation.2 | async-start | bytes 1114112 | tf_op jit(solution)/shard_map/all_to_all | solution.py:23
  109.7 62.3 %collective-permute-start.10 = (bf16[1,2,128,896]{3,2,1,0:T(8,128)(2,1)}, bf16[1,2,128,896]{3,2,1,0:T(8,128)(2,1)S(1)}, u32[]{:S(2)}, u32[]{:S(2)}) collective-permute-start(bf16[1,2,128,896]{3,2,1,0:T(8,128)(2,1)} %get-tuple-element.41), channel_id=1, source_target_pairs={{0,6},{1,7},{2,4},{3,5},{4,2},{5,3},{6,0},{7,1},{8,14},{9,15},{10,... | collective-permute-start | bytes 1376264 | tf_op jit(solution)/shard_map/ppermute | solution.py:77
  114.9 57.1 %collective-permute-start.9 = (bf16[1,2,128,896]{3,2,1,0:T(8,128)(2,1)}, bf16[1,2,128,896]{3,2,1,0:T(8,128)(2,1)}, u32[]{:S(2)}, u32[]{:S(2)}) collective-permute-start(bf16[1,2,128,896]{3,2,1,0:T(8,128)(2,1)} %get-tuple-element.42), channel_id=1, source_target_pairs={{0,4},{1,5},{2,6},{3,7},{4,0},{5,1},{6,2},{7,3},{8,12},{9,13},{10,... | collective-permute-start | bytes 1376264 | tf_op jit(solution)/shard_map/ppermute | solution.py:77
  116.8 55.2 %collective-permute-start.8 = (bf16[1,2,128,896]{3,2,1,0:T(8,128)(2,1)}, bf16[1,2,128,896]{3,2,1,0:T(8,128)(2,1)}, u32[]{:S(2)}, u32[]{:S(2)}) collective-permute-start(bf16[1,2,128,896]{3,2,1,0:T(8,128)(2,1)} %get-tuple-element.43), channel_id=1, source_target_pairs={{0,2},{1,3},{2,0},{3,1},{4,6},{5,7},{6,4},{7,5},{8,10},{9,11},{10,... | collective-permute-start | bytes 1376264 | tf_op jit(solution)/shard_map/ppermute | solution.py:77
  177.2 12.7 %all-to-all-start.3 = ((bf16[4,64,896]{2,1,0:T(8,128)(2,1)}), bf16[4,64,896]{2,1,0:T(8,128)(2,1)S(1)}, u32[]{:S(2)}, u32[]{:S(2)}) async-start(bf16[4,64,896]{2,1,0:T(8,128)(2,1)} %bitcast.31), calls=%async_computation.3 | async-start | bytes 917504 | tf_op jit(solution)/shard_map/all_to_all | solution.py:23
  190.4 58.1 %copy-start.2 = (bf16[896,8,128]{0,2,1:T(8,128)(2,1)S(1)}, bf16[896,8,128]{0,2,1:T(8,128)(2,1)}, u32[]{:S(2)}) copy-start(bf16[896,8,128]{0,2,1:T(8,128)(2,1)} %copy.66) | copy-start | bytes 5505028
  190.5 18.4 %collective-permute-start.11 = (bf16[64,896]{1,0:T(8,128)(2,1)S(1)}, bf16[64,896]{1,0:T(8,128)(2,1)S(1)}, u32[]{:S(2)}, u32[]{:S(2)}) collective-permute-start(bf16[64,896]{1,0:T(8,128)(2,1)S(1)} %slice.118), channel_id=1, source_target_pairs={{0,8},{1,9},{2,10},{3,11},{4,12},{5,13},{6,14},{7,15},{8,0},{9,1},... | collective-permute-start | bytes 344072 | tf_op jit(solution)/shard_map/ppermute | solution.py:30
  208.9 15.8 %collective-permute-start.12 = (bf16[64,896]{1,0:T(8,128)(2,1)S(1)}, bf16[64,896]{1,0:T(8,128)(2,1)S(1)}, u32[]{:S(2)}, u32[]{:S(2)}) collective-permute-start(bf16[64,896]{1,0:T(8,128)(2,1)S(1)} %fusion.15), channel_id=1, source_target_pairs={{0,72},{1,73},{2,74},{3,75},{4,76},{5,77},{6,78},{7,79},{8,64},{9,... | collective-permute-start | bytes 344072 | tf_op jit(solution)/shard_map/ppermute | solution.py:40
  224.6 12.9 %collective-permute-start.13 = (bf16[64,896]{1,0:T(8,128)(2,1)S(1)}, bf16[64,896]{1,0:T(8,128)(2,1)S(1)}, u32[]{:S(2)}, u32[]{:S(2)}) collective-permute-start(bf16[64,896]{1,0:T(8,128)(2,1)S(1)} %collective-permute-done.12), channel_id=1, source_target_pairs={{0,8},{1,9},{2,10},{3,11},{4,12},{5,13},{6,14},{7,15},{8,0},{9,1},... | collective-permute-start | bytes 344072 | tf_op jit(solution)/shard_map/ppermute | solution.py:30
  286.3 12.2 %all-to-all-start.6 = ((bf16[4,64,896]{2,1,0:T(8,128)(2,1)}), bf16[4,64,896]{2,1,0:T(8,128)(2,1)S(1)}, u32[]{:S(2)}, u32[]{:S(2)}) async-start(bf16[4,64,896]{2,1,0:T(8,128)(2,1)} %bitcast.44), calls=%async_computation.6 | async-start | bytes 917504 | tf_op jit(solution)/shard_map/all_to_all | solution.py:23
  320.9 17.9 %collective-permute-start.14 = (bf16[8,7168]{1,0:T(8,128)(2,1)S(1)}, bf16[8,7168]{1,0:T(8,128)(2,1)S(1)}, u32[]{:S(2)}, u32[]{:S(2)}) collective-permute-start(bf16[8,7168]{1,0:T(8,128)(2,1)S(1)} %bitcast.131), channel_id=1, source_target_pairs={{0,72},{1,73},{2,74},{3,75},{4,76},{5,77},{6,78},{7,79},{8,64},{9,... | collective-permute-start | bytes 344072 | tf_op jit(solution)/shard_map/ppermute | solution.py:40
  (20 other events, 108.2 us)

commit v5 on v2

v5 whole, which is shorter than its diff:
```python
import jax
import jax.numpy as jnp
from jax import lax
from jax.sharding import PartitionSpec as P

HID = 1024
HID_DEV = 128
GROUP = HID // HID_DEV
PAIR = 4
CAP = 4
HALVES = 2
LANES = 128


def groups(count):
    span = GROUP * HALVES
    same_row = [[first + k for k in range(span)] for first in range(0, count, span)]
    same_place = [[first + k for first in range(0, count, span)] for k in range(span)]
    return same_row, same_place


def exchange(value, within):
    return lax.all_to_all(
        value, "expert", split_axis=0, concat_axis=0, axis_index_groups=within, tiled=True
    )


def swap(value, bit):
    count = lax.axis_size("expert")
    return lax.ppermute(value, "expert", [(i, i ^ bit) for i in range(count)])


def next_section(value):
    sections, count = lax.axis_size("section"), lax.axis_size("expert")
    route = [
        (s * count + i, (s + 1) % sections * count + (i ^ GROUP))
        for s in range(sections)
        for i in range(count)
    ]
    return lax.ppermute(value, ("section", "expert"), route)


def head(value):
    return lax.reduce_precision(value, exponent_bits=8, mantissa_bits=7)


def in_three(value):
    first = head(value)
    second = head(value - first)
    third = head(value - first - second)
    return [part.astype(jnp.bfloat16) for part in (first, second, third)]


def take(value, index, axis):
    return lax.dynamic_index_in_dim(value, index, axis, keepdims=False)


def recut(quarters, chip, core):
    near = swap(take(quarters, 1 - core, 1), 1)
    both = jnp.stack([take(quarters, core, 1), near], axis=1)
    far = swap(take(both, 1 - chip, 0), 2)
    return take(both, chip, 0), far


def tables(ids, gates, half, peers, rows_dev):
    rows = ids.shape[0]
    wanted = 2 * jnp.arange(peers, dtype=jnp.int32) + half
    hit = ids.T[None, :, :] == wanted[:, None, None]
    routed = jnp.any(hit, axis=1)
    weight = jnp.sum(jnp.where(hit, gates.T[None, :, :], 0.0), axis=1)
    at = jnp.arange(rows, dtype=jnp.int32)
    before = (at[:, None] < at[None, :]) & (at[:, None] // rows_dev == at[None, :] // rows_dev)
    rank = jnp.dot(
        routed.astype(jnp.bfloat16), before.astype(jnp.bfloat16), preferred_element_type=jnp.float32
    ).astype(jnp.int32)
    slots = rows // rows_dev * CAP
    slot = jnp.arange(slots, dtype=jnp.int32)
    mine = (slot[:, None] // CAP == at[None, :] // rows_dev)[None]
    picked = mine & routed[:, None, :] & (rank[:, None, :] == (slot % CAP)[None, :, None])
    weigher = jnp.where(picked, weight[:, None, :], 0.0)
    shape = (peers * slots, rows)
    return picked.astype(jnp.bfloat16).reshape(shape), weigher.reshape(shape)


def body(hidden, norm_gain, w_up, w_down, expert_ids, route_gates):
    width = hidden.shape[-1]
    rows_dev = hidden.shape[1]
    passes, top = expert_ids.shape[1], expert_ids.shape[-1]
    count = lax.axis_size("expert")
    peers = count // (GROUP * HALVES)
    part = width // PAIR
    piece = part // 2
    block = GROUP * rows_dev
    same_row, same_place = groups(count)
    place = lax.axis_index("expert")
    core, chip, pair, half = place % 2, place // 2 % 2, place // 4 % 2, place // 8 % 2

    facts = [expert_ids[0].astype(jnp.bfloat16)] + in_three(route_gates[0])
    facts = jnp.stack(facts).transpose(2, 0, 1, 3).reshape(rows_dev, -1)
    facts = jnp.pad(facts, ((0, 0), (0, LANES - facts.shape[1])))
    quarters = hidden[0].reshape(rows_dev, PAIR, part).transpose(1, 0, 2)
    quarters = jnp.concatenate(
        [quarters, jnp.broadcast_to(facts[None], (PAIR, rows_dev, LANES))], axis=2
    )
    sent, w_up, w_down = lax.optimization_barrier(
        (jnp.concatenate([quarters] * (2 * HALVES)), w_up, w_down)
    )
    arrived = exchange(sent, same_row)
    up, up_far = recut(w_up[0].reshape(2, 2, part, HID_DEV), chip, core)
    down, down_far = recut(w_down[0].reshape(HID_DEV, 2, 2, part).transpose(1, 2, 0, 3), chip, core)
    arrived, up, up_far, down = lax.optimization_barrier((arrived, up, up_far, down))
    arrived = arrived.reshape(HALVES, block, part + LANES)
    arrived = lax.dynamic_slice_in_dim(jnp.concatenate([arrived, arrived]), half, HALVES, 0)
    arrived = arrived.reshape(HALVES * block, part + LANES)
    rows = arrived[:, :part]
    facts = arrived[:, part:].astype(jnp.float32)
    routes = facts[:, : 4 * passes * top].reshape(HALVES * block, 4, passes, top)

    up = [up[0], up[1], up_far[0], up_far[1]]
    gain = lax.dynamic_slice_in_dim(norm_gain[0], place % PAIR * part, part, 0)

    for t in range(passes):
        ids = routes[:, 0, t].astype(jnp.int32)
        gates = jnp.sum(routes[:, 1:, t], axis=1)
        picker, weigher = tables(ids, gates, half, peers, rows_dev)
        slots = jnp.dot(picker, rows, preferred_element_type=jnp.float32).astype(jnp.bfloat16)
        slots = exchange(slots, same_place)
        if t == 0:
            slots, down_far = lax.optimization_barrier((slots, down_far))
            down = jnp.concatenate([down, down_far]).reshape(PAIR * HID_DEV, part)
        values = slots.astype(jnp.float32)
        squares = jnp.broadcast_to(
            jnp.sum(values * values, axis=1, keepdims=True), (slots.shape[0], LANES)
        )
        scaled = (values * gain).astype(jnp.bfloat16)
        sums = [
            jnp.dot(scaled, up[k], preferred_element_type=jnp.float32) for k in range(PAIR)
        ]
        came = swap(jnp.stack([sums[1], sums[3], squares]), 1)
        sums = [sums[0] + came[0], sums[2] + came[1]]
        squares = squares + came[2]
        came = swap(jnp.stack([sums[1], squares]), 2)
        scale = lax.rsqrt((squares + came[1]) / width + 1e-06)
        active = jax.nn.silu((sums[0] + came[0]) * scale).astype(jnp.bfloat16)
        active = jnp.stack([active, swap(active, 1)])
        active = jnp.concatenate([active, swap(active, 2)])
        active = jnp.concatenate([active[k] for k in range(PAIR)], axis=1)
        outputs = jnp.dot(active, down, preferred_element_type=jnp.float32).astype(jnp.bfloat16)
        outputs = exchange(outputs, same_place)
        mixture = jnp.dot(
            weigher.T,
            outputs.astype(jnp.float32),
            precision=lax.Precision.HIGHEST,
            preferred_element_type=jnp.float32,
        )
        if t + 1 < passes:
            mixture = mixture.reshape(2 * block, 2, piece)
            mine = take(mixture, pair, 1)
            mine = mine + swap(take(mixture, 1 - pair, 1).astype(jnp.bfloat16), 4).astype(
                jnp.float32
            )
            kept = take(rows[block:].reshape(block, 2, piece), pair, 1).astype(jnp.float32)
            other = swap(mine[:block].astype(jnp.bfloat16), 8).astype(jnp.float32)
            own = next_section((kept + mine[block:] + other).astype(jnp.bfloat16))
            rows = jnp.concatenate([own, swap(own, 8)])
            pieces = jnp.stack([rows, swap(rows, 4), rows], axis=1)
            rows = lax.dynamic_slice_in_dim(pieces, pair, 2, 1).reshape(2 * block, part)
        else:
            own = mixture[:block].astype(jnp.bfloat16)
            kept = jnp.where(pair == 0, rows[block:].astype(jnp.float32), 0.0)
            other = (kept + mixture[block:]).astype(jnp.bfloat16)
            both = lax.dynamic_slice_in_dim(jnp.stack([other, own, other]), half, HALVES, 0)
            both = exchange(both.reshape(HALVES * GROUP, rows_dev, part), same_row)
            both = both.reshape(2 * HALVES, PAIR, rows_dev, part).astype(jnp.float32)
            done = jnp.sum(both, axis=0).astype(jnp.bfloat16)
            done = next_section(done.transpose(1, 0, 2).reshape(rows_dev, width))
    return done[None]


def solution(mesh):
    placed = (
        P("section", "expert", None),
        P("section", None),
        P("section", None, "expert"),
        P("section", "expert", None),
        P("section", None, "expert", None),
        P("section", None, "expert", None),
    )
    return jax.shard_map(
        body, mesh=mesh, in_specs=placed, out_specs=P("section", "expert", None), check_vma=False
    )
```

time: 350 us -> 328 us (0.937)
  the two profiles are of different devices: /device:TPU:65 before, /device:TPU:7 now
where the time goes in v5:
time: 328 us; the launch traced here: 326 us
  waiting for transfers between devices  152 us (46%)
  starting transfers between devices  81.7 us (25%)
  blocking collectives  47.9 us (15%)
  matrix products  16.1 us (5%)
  other arithmetic  13.8 us (4%)
  local copies, waits for them, and re-layouts  13.7 us (4%)
    ppermute x16, waiting for transfers between devices, swap(): return lax.ppermute(value, 'expert', [(i, i ^ bit) for i in range(count)])  99.1 us
    ppermute x16, starting transfers between devices, swap(): return lax.ppermute(value, 'expert', [(i, i ^ bit) for i in range(count)])  52.1 us
    all_to_all x2, blocking collectives, exchange(): lax.all_to_all(value, 'expert', split_axis=0, concat_axis=0, axis_index_g...  47.9 us
    ppermute x2, waiting for transfers between devices, next_section(): return lax.ppermute(value, ('section', 'expert'), route)  28.8 us
    all_to_all x4, waiting for transfers between devices, exchange(): lax.all_to_all(value, 'expert', split_axis=0, concat_axis=0, axis_index_g...  24.3 us
    all_to_all x4, starting transfers between devices, exchange(): lax.all_to_all(value, 'expert', split_axis=0, concat_axis=0, axis_index_g...  24 us
    dot_general x8, matrix products, body(): jnp.dot(scaled, up[k], preferred_element_type=jnp.float32)  7.81 us
  transfers between devices with their start and end apart: 22, of which 19 were waited for; matrix products, arithmetic and copies ran while one was open for 5% of the time, Pallas kernels for 0%

profile of v5, /device:TPU:7, one launch (start us, length us, event | category | flops | bytes accessed | tf_op | source)
XLA Modules:
  0.0 326.0 jit_solution(1706856223519902961)
XLA Ops:
  8.9 12.7 %all-to-all-start = ((bf16[16,8,1920]{2,1,0:T(8,128)(2,1)}), bf16[16,8,1920]{2,1,0:T(8,128)(2,1)}, u32[]{:S(2)}, u32[]{:S(2)}) async-start(bf16[16,8,1920]{2,1,0:T(8,128)(2,1)} %maximum_maximum_fusion), calls=%async_computation | async-start | bytes 983040 | tf_op jit(solution)/shard_map/all_to_all | solution.py:23
  30.9 3.5 %collective-permute-start.1 = (bf16[2,1792,128]{2,1,0:T(8,128)(2,1)}, bf16[2,1792,128]{2,1,0:T(8,128)(2,1)}, u32[]{:S(2)}, u32[]{:S(2)}) collective-permute-start(bf16[2,1792,128]{2,1,0:T(8,128)(2,1)} %get-tuple-element.33), channel_id=1, source_target_pairs={{0,2},{1,3},{2,0},{3,1},{4,6},{5,7},{6,4},{7,5},{8,10},{9,11},{10,... | collective-permute-start | bytes 2752520 | tf_op jit(solution)/shard_map/ppermute | solution.py:30
  40.6 17.5 %collective-permute-done.1 = bf16[2,1792,128]{2,1,0:T(8,128)(2,1)} collective-permute-done((bf16[2,1792,128]{2,1,0:T(8,128)(2,1)}, bf16[2,1792,128]{2,1,0:T(8,128)(2,1)}, u32[]{:S(2)}, u32[]{:S(2)}) %collective-permute-start.1) | collective-permute-done | bytes 917536 | tf_op jit(solution)/shard_map/ppermute | solution.py:30
  61.5 4.2 %all-to-all-start.1 = ((bf16[4,64,1792]{2,1,0:T(8,128)(2,1)}), bf16[4,64,1792]{2,1,0:T(8,128)(2,1)S(1)}, u32[]{:S(2)}, u32[]{:S(2)}) async-start(bf16[4,64,1792]{2,1,0:T(8,128)(2,1)} %bitcast.27), calls=%async_computation.1 | async-start | bytes 1835008 | tf_op jit(solution)/shard_map/all_to_all | solution.py:23
  65.8 12.0 %collective-permute-done.3 = bf16[2,128,1792]{2,1,0:T(8,128)(2,1)} collective-permute-done((bf16[2,128,1792]{2,1,0:T(8,128)(2,1)}, bf16[2,128,1792]{2,1,0:T(8,128)(2,1)}, u32[]{:S(2)}, u32[]{:S(2)}) %collective-permute-start.3) | collective-permute-done | bytes 917536 | tf_op jit(solution)/shard_map/ppermute | solution.py:30
  80.2 4.3 %collective-permute-start.4 = (f32[3,256,128]{1,2,0:T(8,128)S(1)}, f32[3,256,128]{1,2,0:T(8,128)S(1)}, u32[]{:S(2)}, u32[]{:S(2)}) collective-permute-start(f32[3,256,128]{1,2,0:T(8,128)S(1)} %pad_maximum_fusion.1), channel_id=1, source_target_pairs={{0,1},{1,0},{2,3},{3,2},{4,5},{5,4},{6,7},{7,6},{8,9},{9,8},{10,11... | collective-permute-start | bytes 1179656 | tf_op jit(solution)/shard_map/ppermute | solution.py:30
  89.3 7.5 %collective-permute-done.5 = f32[2,256,128]{1,2,0:T(8,128)S(1)} collective-permute-done((f32[2,256,128]{1,2,0:T(8,128)S(1)}, f32[2,256,128]{1,2,0:T(8,128)S(1)}, u32[]{:S(2)}, u32[]{:S(2)}) %collective-permute-start.5) | collective-permute-done | bytes 262176 | tf_op jit(solution)/shard_map/ppermute | solution.py:30
  109.5 3.5 %all-to-all-start.2 = ((bf16[4,64,1792]{2,1,0:T(8,128)(2,1)}), bf16[4,64,1792]{2,1,0:T(8,128)(2,1)S(1)}, u32[]{:S(2)}, u32[]{:S(2)}) async-start(bf16[4,64,1792]{2,1,0:T(8,128)(2,1)} %bitcast.239), calls=%async_computation.2 | async-start | bytes 1835008 | tf_op jit(solution)/shard_map/all_to_all | solution.py:23
  113.8 11.7 %all-to-all-done.2 = bf16[4,64,1792]{2,1,0:T(8,128)(2,1)S(1)} async-done(((bf16[4,64,1792]{2,1,0:T(8,128)(2,1)}), bf16[4,64,1792]{2,1,0:T(8,128)(2,1)S(1)}, u32[]{:S(2)}, u32[]{:S(2)}) %all-to-all-start.2) | async-done | bytes 917536 | tf_op jit(solution)/shard_map/all_to_all | solution.py:23
  129.9 9.5 %collective-permute-start.8 = (bf16[128,896]{1,0:T(8,128)(2,1)}, bf16[128,896]{1,0:T(8,128)(2,1)}, u32[]{:S(2)}, u32[]{:S(2)}) collective-permute-start(bf16[128,896]{1,0:T(8,128)(2,1)} %fusion.85), channel_id=1, source_target_pairs={{0,4},{1,5},{2,6},{3,7},{4,0},{5,1},{6,2},{7,3},{8,12},{9,13},{10,... | collective-permute-start | bytes 688136 | tf_op jit(solution)/shard_map/ppermute | solution.py:30
  139.5 11.2 %collective-permute-done.8 = bf16[128,896]{1,0:T(8,128)(2,1)} collective-permute-done((bf16[128,896]{1,0:T(8,128)(2,1)}, bf16[128,896]{1,0:T(8,128)(2,1)}, u32[]{:S(2)}, u32[]{:S(2)}) %collective-permute-start.8) | collective-permute-done | bytes 229408 | tf_op jit(solution)/shard_map/ppermute | solution.py:30
  151.7 7.2 %collective-permute-start.9 = (bf16[64,896]{1,0:T(8,128)(2,1)S(1)}, bf16[64,896]{1,0:T(8,128)(2,1)S(1)}, u32[]{:S(2)}, u32[]{:S(2)}) collective-permute-start(bf16[64,896]{1,0:T(8,128)(2,1)S(1)} %slice.274), channel_id=1, source_target_pairs={{0,8},{1,9},{2,10},{3,11},{4,12},{5,13},{6,14},{7,15},{8,0},{9,1},... | collective-permute-start | bytes 344072 | tf_op jit(solution)/shard_map/ppermute | solution.py:30
  159.1 9.1 %collective-permute-done.9 = bf16[64,896]{1,0:T(8,128)(2,1)S(1)} collective-permute-done((bf16[64,896]{1,0:T(8,128)(2,1)S(1)}, bf16[64,896]{1,0:T(8,128)(2,1)S(1)}, u32[]{:S(2)}, u32[]{:S(2)}) %collective-permute-start.9) | collective-permute-done | bytes 114720 | tf_op jit(solution)/shard_map/ppermute | solution.py:30
  170.2 13.3 %collective-permute-done.10 = bf16[64,896]{1,0:T(8,128)(2,1)S(1)} collective-permute-done((bf16[64,896]{1,0:T(8,128)(2,1)S(1)}, bf16[64,896]{1,0:T(8,128)(2,1)S(1)}, u32[]{:S(2)}, u32[]{:S(2)}) %collective-permute-start.10) | collective-permute-done | bytes 114720 | tf_op jit(solution)/shard_map/ppermute | solution.py:40
  185.5 11.4 %collective-permute-done.11 = bf16[64,896]{1,0:T(8,128)(2,1)S(1)} collective-permute-done((bf16[64,896]{1,0:T(8,128)(2,1)S(1)}, bf16[64,896]{1,0:T(8,128)(2,1)S(1)}, u32[]{:S(2)}, u32[]{:S(2)}) %collective-permute-start.11) | collective-permute-done | bytes 114720 | tf_op jit(solution)/shard_map/ppermute | solution.py:30
  198.9 10.4 %collective-permute-done.12 = bf16[128,896]{1,0:T(8,128)(2,1)S(1)} collective-permute-done((bf16[128,896]{1,0:T(8,128)(2,1)S(1)}, bf16[128,896]{1,0:T(8,128)(2,1)S(1)}, u32[]{:S(2)}, u32[]{:S(2)}) %collective-permute-start.12) | collective-permute-done | bytes 229408 | tf_op jit(solution)/shard_map/ppermute | solution.py:30
  210.3 15.9 %all_to_all.52 = bf16[4,64,1792]{2,1,0:T(8,128)(2,1)S(1)} all-to-all(bf16[4,64,1792]{2,1,0:T(8,128)(2,1)S(1)} %bitcast.246), channel_id=1, replica_groups={{0,16,32,48},{1,17,33,49},{2,18,34,50},{3,19,35,51},{4,20,36,52},{5,21,..., dimensions={0} | all-to-all | bytes 1835008 | tf_op jit(solution)/shard_map/all_to_all | solution.py:23
  236.7 7.5 %collective-permute-done.14 = f32[2,256,128]{1,2,0:T(8,128)S(1)} collective-permute-done((f32[2,256,128]{1,2,0:T(8,128)S(1)}, f32[2,256,128]{1,2,0:T(8,128)S(1)}, u32[]{:S(2)}, u32[]{:S(2)}) %collective-permute-start.14) | collective-permute-done | bytes 262176 | tf_op jit(solution)/shard_map/ppermute | solution.py:30
  250.7 4.7 %collective-permute-done.16 = bf16[2,256,128]{1,2,0:T(8,128)(2,1)S(1)} collective-permute-done((bf16[2,256,128]{1,2,0:T(8,128)(2,1)S(1)}, bf16[2,256,128]{1,2,0:T(8,128)(2,1)S(1)}, u32[]{:S(2)}, u32[]{:S(2)}) %collective-permute-start.16) | collective-permute-done | bytes 131104 | tf_op jit(solution)/shard_map/ppermute | solution.py:30
  257.0 3.6 %all-to-all-start.4 = ((bf16[4,64,1792]{2,1,0:T(8,128)(2,1)}), bf16[4,64,1792]{2,1,0:T(8,128)(2,1)S(1)}, u32[]{:S(2)}, u32[]{:S(2)}) async-start(bf16[4,64,1792]{2,1,0:T(8,128)(2,1)} %bitcast.74), calls=%async_computation.4 | async-start | bytes 1835008 | tf_op jit(solution)/shard_map/all_to_all | solution.py:23
  260.7 12.4 %all-to-all-done.4 = bf16[4,64,1792]{2,1,0:T(8,128)(2,1)S(1)} async-done(((bf16[4,64,1792]{2,1,0:T(8,128)(2,1)}), bf16[4,64,1792]{2,1,0:T(8,128)(2,1)S(1)}, u32[]{:S(2)}, u32[]{:S(2)}) %all-to-all-start.4) | async-done | bytes 917536 | tf_op jit(solution)/shard_map/all_to_all | solution.py:23
  274.2 32.0 %all_to_all.53 = bf16[16,8,1792]{2,1,0:T(8,128)(2,1)S(1)} all-to-all(bf16[16,8,1792]{2,1,0:T(8,128)(2,1)S(1)} %bitcast.251), channel_id=1, replica_groups={{0,1,2,3,4,5,6,7,8,9,10,11,12,13,14,15},{16,17,18,19,20,21,22,23,24,25,..., dimensions={0} | all-to-all | bytes 917504 | tf_op jit(solution)/shard_map/all_to_all | solution.py:23
  306.3 3.5 %collective-permute-start.17 = (bf16[8,7168]{1,0:T(8,128)(2,1)S(1)}, bf16[8,7168]{1,0:T(8,128)(2,1)S(1)}, u32[]{:S(2)}, u32[]{:S(2)}) collective-permute-start(bf16[8,7168]{1,0:T(8,128)(2,1)S(1)} %bitcast.266), channel_id=1, source_target_pairs={{0,72},{1,73},{2,74},{3,75},{4,76},{5,77},{6,78},{7,79},{8,64},{9,... | collective-permute-start | bytes 344072 | tf_op jit(solution)/shard_map/ppermute | solution.py:40
  309.8 15.5 %collective-permute-done.17 = bf16[8,7168]{1,0:T(8,128)(2,1)S(1)} collective-permute-done((bf16[8,7168]{1,0:T(8,128)(2,1)S(1)}, bf16[8,7168]{1,0:T(8,128)(2,1)S(1)}, u32[]{:S(2)}, u32[]{:S(2)}) %collective-permute-start.17) | collective-permute-done | bytes 114720 | tf_op jit(solution)/shard_map/ppermute | solution.py:40
  (125 shorter events, 81.2 us)
Async XLA Ops:
  0.0 65.7 %copy-start = (f32[1,7168]{1,0:T(1,128)S(1)}, f32[1,7168]{1,0:T(1,128)}, u32[]{:S(2)}) copy-start(f32[1,7168]{1,0:T(1,128)} %param.7) | copy-start | bytes 86020
  6.3 21.7 %collective-permute-start = (bf16[2,1792,128]{2,1,0:T(8,128)(2,1)}, bf16[2,1792,128]{2,1,0:T(8,128)(2,1)}, u32[]{:S(2)}, u32[]{:S(2)}) collective-permute-start(bf16[2,1792,128]{2,1,0:T(8,128)(2,1)} %get-tuple-element.35), channel_id=1, source_target_pairs={{0,1},{1,0},{2,3},{3,2},{4,5},{5,4},{6,7},{7,6},{8,9},{9,8},{10,11... | collective-permute-start | bytes 2752520 | tf_op jit(solution)/shard_map/ppermute | solution.py:30
  8.9 49.2 %all-to-all-start = ((bf16[16,8,1920]{2,1,0:T(8,128)(2,1)}), bf16[16,8,1920]{2,1,0:T(8,128)(2,1)}, u32[]{:S(2)}, u32[]{:S(2)}) async-start(bf16[16,8,1920]{2,1,0:T(8,128)(2,1)} %maximum_maximum_fusion), calls=%async_computation | async-start | bytes 983040 | tf_op jit(solution)/shard_map/all_to_all | solution.py:23
  26.0 8.7 %collective-permute-start.2 = (bf16[2,128,1792]{1,2,0:T(8,128)(2,1)}, bf16[2,128,1792]{1,2,0:T(8,128)(2,1)S(1)}, u32[]{:S(2)}, u32[]{:S(2)}) collective-permute-start(bf16[2,128,1792]{1,2,0:T(8,128)(2,1)} %get-tuple-element.31), channel_id=1, source_target_pairs={{0,1},{1,0},{2,3},{3,2},{4,5},{5,4},{6,7},{7,6},{8,9},{9,8},{10,11... | collective-permute-start | bytes 2752520 | tf_op jit(solution)/shard_map/ppermute | solution.py:30
  30.9 27.2 %collective-permute-start.1 = (bf16[2,1792,128]{2,1,0:T(8,128)(2,1)}, bf16[2,1792,128]{2,1,0:T(8,128)(2,1)}, u32[]{:S(2)}, u32[]{:S(2)}) collective-permute-start(bf16[2,1792,128]{2,1,0:T(8,128)(2,1)} %get-tuple-element.33), channel_id=1, source_target_pairs={{0,2},{1,3},{2,0},{3,1},{4,6},{5,7},{6,4},{7,5},{8,10},{9,11},{10,... | collective-permute-start | bytes 2752520 | tf_op jit(solution)/shard_map/ppermute | solution.py:30
  38.7 39.1 %collective-permute-start.3 = (bf16[2,128,1792]{2,1,0:T(8,128)(2,1)}, bf16[2,128,1792]{2,1,0:T(8,128)(2,1)}, u32[]{:S(2)}, u32[]{:S(2)}) collective-permute-start(bf16[2,128,1792]{2,1,0:T(8,128)(2,1)} %bitcast.29), channel_id=1, source_target_pairs={{0,2},{1,3},{2,0},{3,1},{4,6},{5,7},{6,4},{7,5},{8,10},{9,11},{10,... | collective-permute-start | bytes 2752520 | tf_op jit(solution)/shard_map/ppermute | solution.py:30
  59.6 18.4 %copy-start.8 = (pred[4,128]{1,0:T(4,128)(4,1)}, pred[4,128]{1,0:T(4,128)(4,1)S(1)}, u32[]{:S(2)}) copy-start(pred[4,128]{1,0:T(4,128)(4,1)S(1)} %get-tuple-element.27) | copy-start | bytes 1540
  61.5 16.4 %all-to-all-start.1 = ((bf16[4,64,1792]{2,1,0:T(8,128)(2,1)}), bf16[4,64,1792]{2,1,0:T(8,128)(2,1)S(1)}, u32[]{:S(2)}, u32[]{:S(2)}) async-start(bf16[4,64,1792]{2,1,0:T(8,128)(2,1)} %bitcast.27), calls=%async_computation.1 | async-start | bytes 1835008 | tf_op jit(solution)/shard_map/all_to_all | solution.py:23
  80.2 5.7 %collective-permute-start.4 = (f32[3,256,128]{1,2,0:T(8,128)S(1)}, f32[3,256,128]{1,2,0:T(8,128)S(1)}, u32[]{:S(2)}, u32[]{:S(2)}) collective-permute-start(f32[3,256,128]{1,2,0:T(8,128)S(1)} %pad_maximum_fusion.1), channel_id=1, source_target_pairs={{0,1},{1,0},{2,3},{3,2},{4,5},{5,4},{6,7},{7,6},{8,9},{9,8},{10,11... | collective-permute-start | bytes 1179656 | tf_op jit(solution)/shard_map/ppermute | solution.py:30
  87.4 9.4 %collective-permute-start.5 = (f32[2,256,128]{1,2,0:T(8,128)S(1)}, f32[2,256,128]{1,2,0:T(8,128)S(1)}, u32[]{:S(2)}, u32[]{:S(2)}) collective-permute-start(f32[2,256,128]{1,2,0:T(8,128)S(1)} %pad_maximum_fusion.3), channel_id=1, source_target_pairs={{0,2},{1,3},{2,0},{3,1},{4,6},{5,7},{6,4},{7,5},{8,10},{9,11},{10,... | collective-permute-start | bytes 786440 | tf_op jit(solution)/shard_map/ppermute | solution.py:30
  97.3 4.0 %collective-permute-start.6 = (bf16[256,128]{0,1:T(8,128)(2,1)S(1)}, bf16[256,128]{0,1:T(8,128)(2,1)S(1)}, u32[]{:S(2)}, u32[]{:S(2)}) collective-permute-start(bf16[256,128]{0,1:T(8,128)(2,1)S(1)} %multiply_convert_fusion.1), channel_id=1, source_target_pairs={{0,1},{1,0},{2,3},{3,2},{4,5},{5,4},{6,7},{7,6},{8,9},{9,8},{10,11... | collective-permute-start | bytes 196616 | tf_op jit(solution)/shard_map/ppermute | solution.py:30
  101.3 6.6 %collective-permute-start.7 = (bf16[2,256,128]{1,2,0:T(8,128)(2,1)S(1)}, bf16[2,256,128]{1,2,0:T(8,128)(2,1)S(1)}, u32[]{:S(2)}, u32[]{:S(2)}) collective-permute-start(bf16[2,256,128]{1,2,0:T(8,128)(2,1)S(1)} %pad_maximum_fusion.5), channel_id=1, source_target_pairs={{0,2},{1,3},{2,0},{3,1},{4,6},{5,7},{6,4},{7,5},{8,10},{9,11},{10,... | collective-permute-start | bytes 393224 | tf_op jit(solution)/shard_map/ppermute | solution.py:30
  109.5 16.0 %all-to-all-start.2 = ((bf16[4,64,1792]{2,1,0:T(8,128)(2,1)}), bf16[4,64,1792]{2,1,0:T(8,128)(2,1)S(1)}, u32[]{:S(2)}, u32[]{:S(2)}) async-start(bf16[4,64,1792]{2,1,0:T(8,128)(2,1)} %bitcast.239), calls=%async_computation.2 | async-start | bytes 1835008 | tf_op jit(solution)/shard_map/all_to_all | solution.py:23
  129.9 20.7 %collective-permute-start.8 = (bf16[128,896]{1,0:T(8,128)(2,1)}, bf16[128,896]{1,0:T(8,128)(2,1)}, u32[]{:S(2)}, u32[]{:S(2)}) collective-permute-start(bf16[128,896]{1,0:T(8,128)(2,1)} %fusion.85), channel_id=1, source_target_pairs={{0,4},{1,5},{2,6},{3,7},{4,0},{5,1},{6,2},{7,3},{8,12},{9,13},{10,... | collective-permute-start | bytes 688136 | tf_op jit(solution)/shard_map/ppermute | solution.py:30
  151.7 16.5 %collective-permute-start.9 = (bf16[64,896]{1,0:T(8,128)(2,1)S(1)}, bf16[64,896]{1,0:T(8,128)(2,1)S(1)}, u32[]{:S(2)}, u32[]{:S(2)}) collective-permute-start(bf16[64,896]{1,0:T(8,128)(2,1)S(1)} %slice.274), channel_id=1, source_target_pairs={{0,8},{1,9},{2,10},{3,11},{4,12},{5,13},{6,14},{7,15},{8,0},{9,1},... | collective-permute-start | bytes 344072 | tf_op jit(solution)/shard_map/ppermute | solution.py:30
  168.2 15.4 %collective-permute-start.10 = (bf16[64,896]{1,0:T(8,128)(2,1)S(1)}, bf16[64,896]{1,0:T(8,128)(2,1)S(1)}, u32[]{:S(2)}, u32[]{:S(2)}) collective-permute-start(bf16[64,896]{1,0:T(8,128)(2,1)S(1)} %fusion.89), channel_id=1, source_target_pairs={{0,72},{1,73},{2,74},{3,75},{4,76},{5,77},{6,78},{7,79},{8,64},{9,... | collective-permute-start | bytes 344072 | tf_op jit(solution)/shard_map/ppermute | solution.py:40
  183.6 13.4 %collective-permute-start.11 = (bf16[64,896]{1,0:T(8,128)(2,1)S(1)}, bf16[64,896]{1,0:T(8,128)(2,1)S(1)}, u32[]{:S(2)}, u32[]{:S(2)}) collective-permute-start(bf16[64,896]{1,0:T(8,128)(2,1)S(1)} %collective-permute-done.10), channel_id=1, source_target_pairs={{0,8},{1,9},{2,10},{3,11},{4,12},{5,13},{6,14},{7,15},{8,0},{9,1},... | collective-permute-start | bytes 344072 | tf_op jit(solution)/shard_map/ppermute | solution.py:30
  196.9 12.4 %collective-permute-start.12 = (bf16[128,896]{1,0:T(8,128)(2,1)S(1)}, bf16[128,896]{1,0:T(8,128)(2,1)S(1)}, u32[]{:S(2)}, u32[]{:S(2)}) collective-permute-start(bf16[128,896]{1,0:T(8,128)(2,1)S(1)} %constant_dynamic-update-slice_fusion), channel_id=1, source_target_pairs={{0,4},{1,5},{2,6},{3,7},{4,0},{5,1},{6,2},{7,3},{8,12},{9,13},{10,... | collective-permute-start | bytes 688136 | tf_op jit(solution)/shard_map/ppermute | solution.py:30
  228.6 4.7 %collective-permute-start.13 = (f32[3,256,128]{1,2,0:T(8,128)S(1)}, f32[3,256,128]{1,2,0:T(8,128)S(1)}, u32[]{:S(2)}, u32[]{:S(2)}) collective-permute-start(f32[3,256,128]{1,2,0:T(8,128)S(1)} %pad_maximum_fusion.2), channel_id=1, source_target_pairs={{0,1},{1,0},{2,3},{3,2},{4,5},{5,4},{6,7},{7,6},{8,9},{9,8},{10,11... | collective-permute-start | bytes 1179656 | tf_op jit(solution)/shard_map/ppermute | solution.py:30
  234.8 9.4 %collective-permute-start.14 = (f32[2,256,128]{1,2,0:T(8,128)S(1)}, f32[2,256,128]{1,2,0:T(8,128)S(1)}, u32[]{:S(2)}, u32[]{:S(2)}) collective-permute-start(f32[2,256,128]{1,2,0:T(8,128)S(1)} %pad_maximum_fusion.4), channel_id=1, source_target_pairs={{0,2},{1,3},{2,0},{3,1},{4,6},{5,7},{6,4},{7,5},{8,10},{9,11},{10,... | collective-permute-start | bytes 786440 | tf_op jit(solution)/shard_map/ppermute | solution.py:30
  244.7 4.0 %collective-permute-start.15 = (bf16[256,128]{0,1:T(8,128)(2,1)S(1)}, bf16[256,128]{0,1:T(8,128)(2,1)S(1)}, u32[]{:S(2)}, u32[]{:S(2)}) collective-permute-start(bf16[256,128]{0,1:T(8,128)(2,1)S(1)} %multiply_convert_fusion), channel_id=1, source_target_pairs={{0,1},{1,0},{2,3},{3,2},{4,5},{5,4},{6,7},{7,6},{8,9},{9,8},{10,11... | collective-permute-start | bytes 196616 | tf_op jit(solution)/shard_map/ppermute | solution.py:30
  248.8 6.6 %collective-permute-start.16 = (bf16[2,256,128]{1,2,0:T(8,128)(2,1)S(1)}, bf16[2,256,128]{1,2,0:T(8,128)(2,1)S(1)}, u32[]{:S(2)}, u32[]{:S(2)}) collective-permute-start(bf16[2,256,128]{1,2,0:T(8,128)(2,1)S(1)} %pad_maximum_fusion.6), channel_id=1, source_target_pairs={{0,2},{1,3},{2,0},{3,1},{4,6},{5,7},{6,4},{7,5},{8,10},{9,11},{10,... | collective-permute-start | bytes 393224 | tf_op jit(solution)/shard_map/ppermute | solution.py:30
  257.0 16.1 %all-to-all-start.4 = ((bf16[4,64,1792]{2,1,0:T(8,128)(2,1)}), bf16[4,64,1792]{2,1,0:T(8,128)(2,1)S(1)}, u32[]{:S(2)}, u32[]{:S(2)}) async-start(bf16[4,64,1792]{2,1,0:T(8,128)(2,1)} %bitcast.74), calls=%async_computation.4 | async-start | bytes 1835008 | tf_op jit(solution)/shard_map/all_to_all | solution.py:23
  306.3 19.0 %collective-permute-start.17 = (bf16[8,7168]{1,0:T(8,128)(2,1)S(1)}, bf16[8,7168]{1,0:T(8,128)(2,1)S(1)}, u32[]{:S(2)}, u32[]{:S(2)}) collective-permute-start(bf16[8,7168]{1,0:T(8,128)(2,1)S(1)} %bitcast.266), channel_id=1, source_target_pairs={{0,72},{1,73},{2,74},{3,75},{4,76},{5,77},{6,78},{7,79},{8,64},{9,... | collective-permute-start | bytes 344072 | tf_op jit(solution)/shard_map/ppermute | solution.py:40
  (8 other events, 105.3 us)

commit v6 on v5

--- a/solution.py
+++ b/solution.py
@@ -10,13 +10,19 @@
 CAP = 4
 HALVES = 2
 LANES = 128
+SIDE = 4
 
 
 def groups(count):
     span = GROUP * HALVES
     same_row = [[first + k for k in range(span)] for first in range(0, count, span)]
     same_place = [[first + k for first in range(0, count, span)] for k in range(span)]
-    return same_row, same_place
+    same_quarter = [
+        [first + k for k in range(q, span, PAIR)]
+        for first in range(0, count, span)
+        for q in range(PAIR)
+    ]
+    return same_row, same_place, same_quarter
 
 
 def exchange(value, within):
@@ -33,7 +39,7 @@
 def next_section(value):
     sections, count = lax.axis_size("section"), lax.axis_size("expert")
     route = [
-        (s * count + i, (s + 1) % sections * count + (i ^ GROUP))
+        (s * count + i, (s + 1) % sections * count + (i ^ GROUP if s % SIDE == SIDE - 1 else i))
         for s in range(sections)
         for i in range(count)
     ]
@@ -91,9 +97,10 @@
     part = width // PAIR
     piece = part // 2
     block = GROUP * rows_dev
-    same_row, same_place = groups(count)
+    same_row, same_place, same_quarter = groups(count)
     place = lax.axis_index("expert")
     core, chip, pair, half = place % 2, place // 2 % 2, place // 4 % 2, place // 8 % 2
+    crosses = (lax.axis_index("section") % SIDE == SIDE - 1).astype(jnp.int32)
 
     facts = [expert_ids[0].astype(jnp.bfloat16)] + in_three(route_gates[0])
     facts = jnp.stack(facts).transpose(2, 0, 1, 3).reshape(rows_dev, -1)
@@ -153,23 +160,25 @@
             precision=lax.Precision.HIGHEST,
             preferred_element_type=jnp.float32,
         )
+        mixture = mixture.reshape(HALVES, block, part)
         if t + 1 < passes:
-            mixture = mixture.reshape(2 * block, 2, piece)
-            mine = take(mixture, pair, 1)
-            mine = mine + swap(take(mixture, 1 - pair, 1).astype(jnp.bfloat16), 4).astype(
-                jnp.float32
-            )
-            kept = take(rows[block:].reshape(block, 2, piece), pair, 1).astype(jnp.float32)
-            other = swap(mine[:block].astype(jnp.bfloat16), 8).astype(jnp.float32)
-            own = next_section((kept + mine[block:] + other).astype(jnp.bfloat16))
+            sent = mixture.astype(jnp.bfloat16).reshape(HALVES, block, 2, piece)
+            sent = jnp.concatenate([sent, sent[:1]])
+            sent = lax.dynamic_slice_in_dim(sent, half ^ crosses, HALVES, 0)
+            sent = sent.transpose(0, 2, 1, 3).reshape(2 * HALVES, block, piece)
+            came = exchange(sent, same_quarter).astype(jnp.float32)
+            kept = take(rows.reshape(HALVES, block, 2, piece), crosses, 0)
+            kept = take(kept, pair, 1).astype(jnp.float32)
+            own = next_section((kept + jnp.sum(came, axis=0)).astype(jnp.bfloat16))
             rows = jnp.concatenate([own, swap(own, 8)])
             pieces = jnp.stack([rows, swap(rows, 4), rows], axis=1)
             rows = lax.dynamic_slice_in_dim(pieces, pair, 2, 1).reshape(2 * block, part)
         else:
-            own = mixture[:block].astype(jnp.bfloat16)
             kept = jnp.where(pair == 0, rows[block:].astype(jnp.float32), 0.0)
-            other = (kept + mixture[block:]).astype(jnp.bfloat16)
-            both = lax.dynamic_slice_in_dim(jnp.stack([other, own, other]), half, HALVES, 0)
+            own = mixture[0].astype(jnp.bfloat16)
+            other = (kept + mixture[1]).astype(jnp.bfloat16)
+            both = jnp.stack([own, other, own])
+            both = lax.dynamic_slice_in_dim(both, half ^ crosses, HALVES, 0)
             both = exchange(both.reshape(HALVES * GROUP, rows_dev, part), same_row)
             both = both.reshape(2 * HALVES, PAIR, rows_dev, part).astype(jnp.float32)
             done = jnp.sum(both, axis=0).astype(jnp.bfloat16)

time: 328 us -> 319 us (0.973); the launches traced: 326 us -> 313 us
  waiting for transfers between devices: 152 us -> 146 us
  blocking collectives: 47.9 us -> 44.3 us
    all_to_all x4 -> x5, waiting for transfers between devices: 24.3 us -> 52.2 us  [exchange(): lax.all_to_all(value, 'expert', split_axis=0, concat_axis=0, axis_index_g...]
    ppermute x16 -> x14, waiting for transfers between devices: 99.1 us -> 76.8 us  [swap(): return lax.ppermute(value, 'expert', [(i, i ^ bit) for i in range(count)])]
    ppermute x16 -> x14, starting transfers between devices: 52.1 us -> 35.8 us  [swap(): return lax.ppermute(value, 'expert', [(i, i ^ bit) for i in range(count)])]
    ppermute x2, waiting for transfers between devices: 28.8 us -> 16.6 us  [next_section(): return lax.ppermute(value, ('section', 'expert'), route)]
    all_to_all x4 -> x5, starting transfers between devices: 24 us -> 35.8 us  [exchange(): lax.all_to_all(value, 'expert', split_axis=0, concat_axis=0, axis_index_g...]
    ppermute x2, starting transfers between devices: 5.57 us -> 10.9 us  [next_section(): return lax.ppermute(value, ('section', 'expert'), route)]
    all_to_all x2, blocking collectives: 47.9 us -> 44.3 us  [exchange(): lax.all_to_all(value, 'expert', split_axis=0, concat_axis=0, axis_index_g...]
  transfers between devices with their start and end apart: 22 -> 21, of which waited for: 19 -> 18; matrix products, arithmetic and copies ran while one was open for 5% -> 5% of each run, Pallas kernels for 0% -> 0%
where the time goes in v6:
time: 319 us; the launch traced here: 313 us
  waiting for transfers between devices  146 us (46%)
  starting transfers between devices  82.6 us (26%)
  blocking collectives  44.3 us (14%)
  other arithmetic  14.5 us (5%)
  matrix products  14.3 us (4%)
  local copies, waits for them, and re-layouts  10.7 us (3%)
    ppermute x14, waiting for transfers between devices, swap(): return lax.ppermute(value, 'expert', [(i, i ^ bit) for i in range(count)])  76.8 us
    all_to_all x5, waiting for transfers between devices, exchange(): lax.all_to_all(value, 'expert', split_axis=0, concat_axis=0, axis_index_g...  52.2 us
    all_to_all x2, blocking collectives, exchange(): lax.all_to_all(value, 'expert', split_axis=0, concat_axis=0, axis_index_g...  44.3 us
    ppermute x14, starting transfers between devices, swap(): return lax.ppermute(value, 'expert', [(i, i ^ bit) for i in range(count)])  35.8 us
    all_to_all x5, starting transfers between devices, exchange(): lax.all_to_all(value, 'expert', split_axis=0, concat_axis=0, axis_index_g...  35.8 us
    ppermute x2, waiting for transfers between devices, next_section(): return lax.ppermute(value, ('section', 'expert'), route)  16.6 us
    ppermute x2, starting transfers between devices, next_section(): return lax.ppermute(value, ('section', 'expert'), route)  10.9 us
    dot_general x8, matrix products, body(): jnp.dot(scaled, up[k], preferred_element_type=jnp.float32)  7.82 us
  transfers between devices with their start and end apart: 21, of which 18 were waited for; matrix products, arithmetic and copies ran while one was open for 5% of the time, Pallas kernels for 0%

profile of v6, /device:TPU:7, one launch (start us, length us, event | category | flops | bytes accessed | tf_op | source)
XLA Modules:
  0.0 312.8 jit_solution(17714945642132995862)
XLA Ops:
  8.9 12.7 %all-to-all-start = ((bf16[16,8,1920]{2,1,0:T(8,128)(2,1)}), bf16[16,8,1920]{2,1,0:T(8,128)(2,1)}, u32[]{:S(2)}, u32[]{:S(2)}) async-start(bf16[16,8,1920]{2,1,0:T(8,128)(2,1)} %maximum_maximum_fusion), calls=%async_computation | async-start | bytes 983040 | tf_op jit(solution)/shard_map/all_to_all | solution.py:29
  30.9 3.5 %collective-permute-start.1 = (bf16[2,1792,128]{2,1,0:T(8,128)(2,1)}, bf16[2,1792,128]{2,1,0:T(8,128)(2,1)}, u32[]{:S(2)}, u32[]{:S(2)}) collective-permute-start(bf16[2,1792,128]{2,1,0:T(8,128)(2,1)} %get-tuple-element.35), channel_id=1, source_target_pairs={{0,2},{1,3},{2,0},{3,1},{4,6},{5,7},{6,4},{7,5},{8,10},{9,11},{10,... | collective-permute-start | bytes 2752520 | tf_op jit(solution)/shard_map/ppermute | solution.py:36
  39.7 18.4 %collective-permute-done.1 = bf16[2,1792,128]{2,1,0:T(8,128)(2,1)} collective-permute-done((bf16[2,1792,128]{2,1,0:T(8,128)(2,1)}, bf16[2,1792,128]{2,1,0:T(8,128)(2,1)}, u32[]{:S(2)}, u32[]{:S(2)}) %collective-permute-start.1) | collective-permute-done | bytes 917536 | tf_op jit(solution)/shard_map/ppermute | solution.py:36
  62.8 4.2 %all-to-all-start.1 = ((bf16[4,64,1792]{2,1,0:T(8,128)(2,1)}), bf16[4,64,1792]{2,1,0:T(8,128)(2,1)S(1)}, u32[]{:S(2)}, u32[]{:S(2)}) async-start(bf16[4,64,1792]{2,1,0:T(8,128)(2,1)} %bitcast.31), calls=%async_computation.1 | async-start | bytes 1835008 | tf_op jit(solution)/shard_map/all_to_all | solution.py:29
  67.0 10.8 %collective-permute-done.3 = bf16[2,128,1792]{2,1,0:T(8,128)(2,1)} collective-permute-done((bf16[2,128,1792]{2,1,0:T(8,128)(2,1)}, bf16[2,128,1792]{2,1,0:T(8,128)(2,1)}, u32[]{:S(2)}, u32[]{:S(2)}) %collective-permute-start.3) | collective-permute-done | bytes 917536 | tf_op jit(solution)/shard_map/ppermute | solution.py:36
  81.5 4.3 %collective-permute-start.4 = (f32[3,256,128]{1,2,0:T(8,128)S(1)}, f32[3,256,128]{1,2,0:T(8,128)S(1)}, u32[]{:S(2)}, u32[]{:S(2)}) collective-permute-start(f32[3,256,128]{1,2,0:T(8,128)S(1)} %pad_maximum_fusion.1), channel_id=1, source_target_pairs={{0,1},{1,0},{2,3},{3,2},{4,5},{5,4},{6,7},{7,6},{8,9},{9,8},{10,11... | collective-permute-start | bytes 1179656 | tf_op jit(solution)/shard_map/ppermute | solution.py:36
  90.6 7.5 %collective-permute-done.5 = f32[2,256,128]{1,2,0:T(8,128)S(1)} collective-permute-done((f32[2,256,128]{1,2,0:T(8,128)S(1)}, f32[2,256,128]{1,2,0:T(8,128)S(1)}, u32[]{:S(2)}, u32[]{:S(2)}) %collective-permute-start.5) | collective-permute-done | bytes 262176 | tf_op jit(solution)/shard_map/ppermute | solution.py:36
  105.9 3.3 %collective-permute-done.7 = bf16[2,256,128]{1,2,0:T(8,128)(2,1)S(1)} collective-permute-done((bf16[2,256,128]{1,2,0:T(8,128)(2,1)S(1)}, bf16[2,256,128]{1,2,0:T(8,128)(2,1)S(1)}, u32[]{:S(2)}, u32[]{:S(2)}) %collective-permute-start.7) | collective-permute-done | bytes 131104 | tf_op jit(solution)/shard_map/ppermute | solution.py:36
  110.8 3.5 %all-to-all-start.2 = ((bf16[4,64,1792]{2,1,0:T(8,128)(2,1)}), bf16[4,64,1792]{2,1,0:T(8,128)(2,1)S(1)}, u32[]{:S(2)}, u32[]{:S(2)}) async-start(bf16[4,64,1792]{2,1,0:T(8,128)(2,1)} %bitcast.255), calls=%async_computation.2 | async-start | bytes 1835008 | tf_op jit(solution)/shard_map/all_to_all | solution.py:29
  114.5 12.4 %all-to-all-done.2 = bf16[4,64,1792]{2,1,0:T(8,128)(2,1)S(1)} async-done(((bf16[4,64,1792]{2,1,0:T(8,128)(2,1)}), bf16[4,64,1792]{2,1,0:T(8,128)(2,1)S(1)}, u32[]{:S(2)}, u32[]{:S(2)}) %all-to-all-start.2) | async-done | bytes 917536 | tf_op jit(solution)/shard_map/all_to_all | solution.py:29
  128.4 11.8 %all-to-all-start.3 = ((bf16[4,64,896]{2,1,0:T(8,128)(2,1)}), bf16[4,64,896]{2,1,0:T(8,128)(2,1)S(1)}, u32[]{:S(2)}, u32[]{:S(2)}) async-start(bf16[4,64,896]{2,1,0:T(8,128)(2,1)} %bitcast.55), calls=%async_computation.3 | async-start | bytes 917504 | tf_op jit(solution)/shard_map/all_to_all | solution.py:29
  140.6 25.9 %all-to-all-done.3 = bf16[4,64,896]{2,1,0:T(8,128)(2,1)S(1)} async-done(((bf16[4,64,896]{2,1,0:T(8,128)(2,1)}), bf16[4,64,896]{2,1,0:T(8,128)(2,1)S(1)}, u32[]{:S(2)}, u32[]{:S(2)}) %all-to-all-start.3) | async-done | bytes 458784 | tf_op jit(solution)/shard_map/all_to_all | solution.py:29
  168.8 7.4 %collective-permute-done.8 = bf16[64,896]{1,0:T(8,128)(2,1)S(1)} collective-permute-done((bf16[64,896]{1,0:T(8,128)(2,1)S(1)}, bf16[64,896]{1,0:T(8,128)(2,1)S(1)}, u32[]{:S(2)}, u32[]{:S(2)}) %collective-permute-start.8) | collective-permute-done | bytes 114720 | tf_op jit(solution)/shard_map/ppermute | solution.py:46
  178.5 10.7 %collective-permute-done.9 = bf16[64,896]{1,0:T(8,128)(2,1)S(1)} collective-permute-done((bf16[64,896]{1,0:T(8,128)(2,1)S(1)}, bf16[64,896]{1,0:T(8,128)(2,1)S(1)}, u32[]{:S(2)}, u32[]{:S(2)}) %collective-permute-start.9) | collective-permute-done | bytes 114720 | tf_op jit(solution)/shard_map/ppermute | solution.py:36
  191.2 9.5 %collective-permute-done.10 = bf16[128,896]{1,0:T(8,128)(2,1)S(1)} collective-permute-done((bf16[128,896]{1,0:T(8,128)(2,1)S(1)}, bf16[128,896]{1,0:T(8,128)(2,1)S(1)}, u32[]{:S(2)}, u32[]{:S(2)}) %collective-permute-start.10) | collective-permute-done | bytes 229408 | tf_op jit(solution)/shard_map/ppermute | solution.py:36
  201.6 15.9 %all_to_all.57 = bf16[4,64,1792]{2,1,0:T(8,128)(2,1)S(1)} all-to-all(bf16[4,64,1792]{2,1,0:T(8,128)(2,1)S(1)} %bitcast.256), channel_id=1, replica_groups={{0,16,32,48},{1,17,33,49},{2,18,34,50},{3,19,35,51},{4,20,36,52},{5,21,..., dimensions={0} | all-to-all | bytes 1835008 | tf_op jit(solution)/shard_map/all_to_all | solution.py:29
  219.9 3.4 %collective-permute-start.11 = (f32[3,256,128]{1,2,0:T(8,128)S(1)}, f32[3,256,128]{1,2,0:T(8,128)S(1)}, u32[]{:S(2)}, u32[]{:S(2)}) collective-permute-start(f32[3,256,128]{1,2,0:T(8,128)S(1)} %pad_maximum_fusion.2), channel_id=1, source_target_pairs={{0,1},{1,0},{2,3},{3,2},{4,5},{5,4},{6,7},{7,6},{8,9},{9,8},{10,11... | collective-permute-start | bytes 1179656 | tf_op jit(solution)/shard_map/ppermute | solution.py:36
  228.1 7.5 %collective-permute-done.12 = f32[2,256,128]{1,2,0:T(8,128)S(1)} collective-permute-done((f32[2,256,128]{1,2,0:T(8,128)S(1)}, f32[2,256,128]{1,2,0:T(8,128)S(1)}, u32[]{:S(2)}, u32[]{:S(2)}) %collective-permute-start.12) | collective-permute-done | bytes 262176 | tf_op jit(solution)/shard_map/ppermute | solution.py:36
  242.0 4.7 %collective-permute-done.14 = bf16[2,256,128]{1,2,0:T(8,128)(2,1)S(1)} collective-permute-done((bf16[2,256,128]{1,2,0:T(8,128)(2,1)S(1)}, bf16[2,256,128]{1,2,0:T(8,128)(2,1)S(1)}, u32[]{:S(2)}, u32[]{:S(2)}) %collective-permute-start.14) | collective-permute-done | bytes 131104 | tf_op jit(solution)/shard_map/ppermute | solution.py:36
  248.4 3.6 %all-to-all-start.5 = ((bf16[4,64,1792]{2,1,0:T(8,128)(2,1)}), bf16[4,64,1792]{2,1,0:T(8,128)(2,1)S(1)}, u32[]{:S(2)}, u32[]{:S(2)}) async-start(bf16[4,64,1792]{2,1,0:T(8,128)(2,1)} %bitcast.73), calls=%async_computation.5 | async-start | bytes 1835008 | tf_op jit(solution)/shard_map/all_to_all | solution.py:29
  252.1 12.4 %all-to-all-done.5 = bf16[4,64,1792]{2,1,0:T(8,128)(2,1)S(1)} async-done(((bf16[4,64,1792]{2,1,0:T(8,128)(2,1)}), bf16[4,64,1792]{2,1,0:T(8,128)(2,1)S(1)}, u32[]{:S(2)}, u32[]{:S(2)}) %all-to-all-start.5) | async-done | bytes 917536 | tf_op jit(solution)/shard_map/all_to_all | solution.py:29
  265.5 28.5 %all_to_all.58 = bf16[16,8,1792]{2,1,0:T(8,128)(2,1)S(1)} all-to-all(bf16[16,8,1792]{2,1,0:T(8,128)(2,1)S(1)} %bitcast.259), channel_id=1, replica_groups={{0,1,2,3,4,5,6,7,8,9,10,11,12,13,14,15},{16,17,18,19,20,21,22,23,24,25,..., dimensions={0} | all-to-all | bytes 917504 | tf_op jit(solution)/shard_map/all_to_all | solution.py:29
  294.1 8.8 %collective-permute-start.15 = (bf16[8,7168]{1,0:T(8,128)(2,1)S(1)}, bf16[8,7168]{1,0:T(8,128)(2,1)S(1)}, u32[]{:S(2)}, u32[]{:S(2)}) collective-permute-start(bf16[8,7168]{1,0:T(8,128)(2,1)S(1)} %bitcast.277), channel_id=1, source_target_pairs={{0,64},{1,65},{2,66},{3,67},{4,68},{5,69},{6,70},{7,71},{8,72},{9,... | collective-permute-start | bytes 344072 | tf_op jit(solution)/shard_map/ppermute | solution.py:46
  302.9 9.3 %collective-permute-done.15 = bf16[8,7168]{1,0:T(8,128)(2,1)S(1)} collective-permute-done((bf16[8,7168]{1,0:T(8,128)(2,1)S(1)}, bf16[8,7168]{1,0:T(8,128)(2,1)S(1)}, u32[]{:S(2)}, u32[]{:S(2)}) %collective-permute-start.15) | collective-permute-done | bytes 114720 | tf_op jit(solution)/shard_map/ppermute | solution.py:46
  (128 shorter events, 72.3 us)
Async XLA Ops:
  0.0 67.0 %copy-start = (f32[1,7168]{1,0:T(1,128)S(1)}, f32[1,7168]{1,0:T(1,128)}, u32[]{:S(2)}) copy-start(f32[1,7168]{1,0:T(1,128)} %param.7) | copy-start | bytes 86020
  6.3 21.7 %collective-permute-start = (bf16[2,1792,128]{2,1,0:T(8,128)(2,1)}, bf16[2,1792,128]{2,1,0:T(8,128)(2,1)}, u32[]{:S(2)}, u32[]{:S(2)}) collective-permute-start(bf16[2,1792,128]{2,1,0:T(8,128)(2,1)} %get-tuple-element.37), channel_id=1, source_target_pairs={{0,1},{1,0},{2,3},{3,2},{4,5},{5,4},{6,7},{7,6},{8,9},{9,8},{10,11... | collective-permute-start | bytes 2752520 | tf_op jit(solution)/shard_map/ppermute | solution.py:36
  8.9 49.2 %all-to-all-start = ((bf16[16,8,1920]{2,1,0:T(8,128)(2,1)}), bf16[16,8,1920]{2,1,0:T(8,128)(2,1)}, u32[]{:S(2)}, u32[]{:S(2)}) async-start(bf16[16,8,1920]{2,1,0:T(8,128)(2,1)} %maximum_maximum_fusion), calls=%async_computation | async-start | bytes 983040 | tf_op jit(solution)/shard_map/all_to_all | solution.py:29
  26.0 8.7 %collective-permute-start.2 = (bf16[2,128,1792]{1,2,0:T(8,128)(2,1)}, bf16[2,128,1792]{1,2,0:T(8,128)(2,1)}, u32[]{:S(2)}, u32[]{:S(2)}) collective-permute-start(bf16[2,128,1792]{1,2,0:T(8,128)(2,1)} %get-tuple-element.33), channel_id=1, source_target_pairs={{0,1},{1,0},{2,3},{3,2},{4,5},{5,4},{6,7},{7,6},{8,9},{9,8},{10,11... | collective-permute-start | bytes 2752520 | tf_op jit(solution)/shard_map/ppermute | solution.py:36
  30.9 27.2 %collective-permute-start.1 = (bf16[2,1792,128]{2,1,0:T(8,128)(2,1)}, bf16[2,1792,128]{2,1,0:T(8,128)(2,1)}, u32[]{:S(2)}, u32[]{:S(2)}) collective-permute-start(bf16[2,1792,128]{2,1,0:T(8,128)(2,1)} %get-tuple-element.35), channel_id=1, source_target_pairs={{0,2},{1,3},{2,0},{3,1},{4,6},{5,7},{6,4},{7,5},{8,10},{9,11},{10,... | collective-permute-start | bytes 2752520 | tf_op jit(solution)/shard_map/ppermute | solution.py:36
  34.5 25.6 %copy-start.8 = (s32[64]{0:T(128)}, s32[64]{0:T(128)S(1)}, u32[]{:S(2)}) copy-start(s32[64]{0:T(128)S(1)} %get-tuple-element.52) | copy-start | bytes 772
  37.8 40.0 %collective-permute-start.3 = (bf16[2,128,1792]{2,1,0:T(8,128)(2,1)}, bf16[2,128,1792]{2,1,0:T(8,128)(2,1)}, u32[]{:S(2)}, u32[]{:S(2)}) collective-permute-start(bf16[2,128,1792]{2,1,0:T(8,128)(2,1)} %bitcast.33), channel_id=1, source_target_pairs={{0,2},{1,3},{2,0},{3,1},{4,6},{5,7},{6,4},{7,5},{8,10},{9,11},{10,... | collective-permute-start | bytes 2752520 | tf_op jit(solution)/shard_map/ppermute | solution.py:36
  62.8 16.4 %all-to-all-start.1 = ((bf16[4,64,1792]{2,1,0:T(8,128)(2,1)}), bf16[4,64,1792]{2,1,0:T(8,128)(2,1)S(1)}, u32[]{:S(2)}, u32[]{:S(2)}) async-start(bf16[4,64,1792]{2,1,0:T(8,128)(2,1)} %bitcast.31), calls=%async_computation.1 | async-start | bytes 1835008 | tf_op jit(solution)/shard_map/all_to_all | solution.py:29
  81.5 5.6 %collective-permute-start.4 = (f32[3,256,128]{1,2,0:T(8,128)S(1)}, f32[3,256,128]{1,2,0:T(8,128)S(1)}, u32[]{:S(2)}, u32[]{:S(2)}) collective-permute-start(f32[3,256,128]{1,2,0:T(8,128)S(1)} %pad_maximum_fusion.1), channel_id=1, source_target_pairs={{0,1},{1,0},{2,3},{3,2},{4,5},{5,4},{6,7},{7,6},{8,9},{9,8},{10,11... | collective-permute-start | bytes 1179656 | tf_op jit(solution)/shard_map/ppermute | solution.py:36
  88.7 9.4 %collective-permute-start.5 = (f32[2,256,128]{1,2,0:T(8,128)S(1)}, f32[2,256,128]{1,2,0:T(8,128)S(1)}, u32[]{:S(2)}, u32[]{:S(2)}) collective-permute-start(f32[2,256,128]{1,2,0:T(8,128)S(1)} %pad_maximum_fusion.3), channel_id=1, source_target_pairs={{0,2},{1,3},{2,0},{3,1},{4,6},{5,7},{6,4},{7,5},{8,10},{9,11},{10,... | collective-permute-start | bytes 786440 | tf_op jit(solution)/shard_map/ppermute | solution.py:36
  98.6 4.0 %collective-permute-start.6 = (bf16[256,128]{0,1:T(8,128)(2,1)S(1)}, bf16[256,128]{0,1:T(8,128)(2,1)S(1)}, u32[]{:S(2)}, u32[]{:S(2)}) collective-permute-start(bf16[256,128]{0,1:T(8,128)(2,1)S(1)} %multiply_convert_fusion.1), channel_id=1, source_target_pairs={{0,1},{1,0},{2,3},{3,2},{4,5},{5,4},{6,7},{7,6},{8,9},{9,8},{10,11... | collective-permute-start | bytes 196616 | tf_op jit(solution)/shard_map/ppermute | solution.py:36
  102.6 6.6 %collective-permute-start.7 = (bf16[2,256,128]{1,2,0:T(8,128)(2,1)S(1)}, bf16[2,256,128]{1,2,0:T(8,128)(2,1)S(1)}, u32[]{:S(2)}, u32[]{:S(2)}) collective-permute-start(bf16[2,256,128]{1,2,0:T(8,128)(2,1)S(1)} %pad_maximum_fusion.5), channel_id=1, source_target_pairs={{0,2},{1,3},{2,0},{3,1},{4,6},{5,7},{6,4},{7,5},{8,10},{9,11},{10,... | collective-permute-start | bytes 393224 | tf_op jit(solution)/shard_map/ppermute | solution.py:36
  110.8 16.0 %all-to-all-start.2 = ((bf16[4,64,1792]{2,1,0:T(8,128)(2,1)}), bf16[4,64,1792]{2,1,0:T(8,128)(2,1)S(1)}, u32[]{:S(2)}, u32[]{:S(2)}) async-start(bf16[4,64,1792]{2,1,0:T(8,128)(2,1)} %bitcast.255), calls=%async_computation.2 | async-start | bytes 1835008 | tf_op jit(solution)/shard_map/all_to_all | solution.py:29
  128.4 38.1 %all-to-all-start.3 = ((bf16[4,64,896]{2,1,0:T(8,128)(2,1)}), bf16[4,64,896]{2,1,0:T(8,128)(2,1)S(1)}, u32[]{:S(2)}, u32[]{:S(2)}) async-start(bf16[4,64,896]{2,1,0:T(8,128)(2,1)} %bitcast.55), calls=%async_computation.3 | async-start | bytes 917504 | tf_op jit(solution)/shard_map/all_to_all | solution.py:29
  140.6 60.6 %copy-start.6 = (pred[4,64,128]{2,1,0:T(32,128)(4,1)S(1)}, pred[4,64,128]{2,1,0:T(32,128)(4,1)}, u32[]{:S(2)}) copy-start(pred[4,64,128]{2,1,0:T(32,128)(4,1)} %get-tuple-element.45) | copy-start | bytes 98308
  166.7 9.5 %collective-permute-start.8 = (bf16[64,896]{1,0:T(8,128)(2,1)S(1)}, bf16[64,896]{1,0:T(8,128)(2,1)S(1)}, u32[]{:S(2)}, u32[]{:S(2)}) collective-permute-start(bf16[64,896]{1,0:T(8,128)(2,1)S(1)} %fusion.87), channel_id=1, source_target_pairs={{0,64},{1,65},{2,66},{3,67},{4,68},{5,69},{6,70},{7,71},{8,72},{9,... | collective-permute-start | bytes 344072 | tf_op jit(solution)/shard_map/ppermute | solution.py:46
  176.2 13.0 %collective-permute-start.9 = (bf16[64,896]{1,0:T(8,128)(2,1)S(1)}, bf16[64,896]{1,0:T(8,128)(2,1)S(1)}, u32[]{:S(2)}, u32[]{:S(2)}) collective-permute-start(bf16[64,896]{1,0:T(8,128)(2,1)S(1)} %collective-permute-done.8), channel_id=1, source_target_pairs={{0,8},{1,9},{2,10},{3,11},{4,12},{5,13},{6,14},{7,15},{8,0},{9,1},... | collective-permute-start | bytes 344072 | tf_op jit(solution)/shard_map/ppermute | solution.py:36
  189.2 11.4 %collective-permute-start.10 = (bf16[128,896]{1,0:T(8,128)(2,1)S(1)}, bf16[128,896]{1,0:T(8,128)(2,1)S(1)}, u32[]{:S(2)}, u32[]{:S(2)}) collective-permute-start(bf16[128,896]{1,0:T(8,128)(2,1)S(1)} %constant_dynamic-update-slice_fusion), channel_id=1, source_target_pairs={{0,4},{1,5},{2,6},{3,7},{4,0},{5,1},{6,2},{7,3},{8,12},{9,13},{10,... | collective-permute-start | bytes 688136 | tf_op jit(solution)/shard_map/ppermute | solution.py:36
  219.9 4.7 %collective-permute-start.11 = (f32[3,256,128]{1,2,0:T(8,128)S(1)}, f32[3,256,128]{1,2,0:T(8,128)S(1)}, u32[]{:S(2)}, u32[]{:S(2)}) collective-permute-start(f32[3,256,128]{1,2,0:T(8,128)S(1)} %pad_maximum_fusion.2), channel_id=1, source_target_pairs={{0,1},{1,0},{2,3},{3,2},{4,5},{5,4},{6,7},{7,6},{8,9},{9,8},{10,11... | collective-permute-start | bytes 1179656 | tf_op jit(solution)/shard_map/ppermute | solution.py:36
  226.2 9.4 %collective-permute-start.12 = (f32[2,256,128]{1,2,0:T(8,128)S(1)}, f32[2,256,128]{1,2,0:T(8,128)S(1)}, u32[]{:S(2)}, u32[]{:S(2)}) collective-permute-start(f32[2,256,128]{1,2,0:T(8,128)S(1)} %pad_maximum_fusion.4), channel_id=1, source_target_pairs={{0,2},{1,3},{2,0},{3,1},{4,6},{5,7},{6,4},{7,5},{8,10},{9,11},{10,... | collective-permute-start | bytes 786440 | tf_op jit(solution)/shard_map/ppermute | solution.py:36
  236.1 4.0 %collective-permute-start.13 = (bf16[256,128]{0,1:T(8,128)(2,1)S(1)}, bf16[256,128]{0,1:T(8,128)(2,1)S(1)}, u32[]{:S(2)}, u32[]{:S(2)}) collective-permute-start(bf16[256,128]{0,1:T(8,128)(2,1)S(1)} %multiply_convert_fusion), channel_id=1, source_target_pairs={{0,1},{1,0},{2,3},{3,2},{4,5},{5,4},{6,7},{7,6},{8,9},{9,8},{10,11... | collective-permute-start | bytes 196616 | tf_op jit(solution)/shard_map/ppermute | solution.py:36
  240.1 6.6 %collective-permute-start.14 = (bf16[2,256,128]{1,2,0:T(8,128)(2,1)S(1)}, bf16[2,256,128]{1,2,0:T(8,128)(2,1)S(1)}, u32[]{:S(2)}, u32[]{:S(2)}) collective-permute-start(bf16[2,256,128]{1,2,0:T(8,128)(2,1)S(1)} %pad_maximum_fusion.6), channel_id=1, source_target_pairs={{0,2},{1,3},{2,0},{3,1},{4,6},{5,7},{6,4},{7,5},{8,10},{9,11},{10,... | collective-permute-start | bytes 393224 | tf_op jit(solution)/shard_map/ppermute | solution.py:36
  248.4 16.1 %all-to-all-start.5 = ((bf16[4,64,1792]{2,1,0:T(8,128)(2,1)}), bf16[4,64,1792]{2,1,0:T(8,128)(2,1)S(1)}, u32[]{:S(2)}, u32[]{:S(2)}) async-start(bf16[4,64,1792]{2,1,0:T(8,128)(2,1)} %bitcast.73), calls=%async_computation.5 | async-start | bytes 1835008 | tf_op jit(solution)/shard_map/all_to_all | solution.py:29
  294.1 18.1 %collective-permute-start.15 = (bf16[8,7168]{1,0:T(8,128)(2,1)S(1)}, bf16[8,7168]{1,0:T(8,128)(2,1)S(1)}, u32[]{:S(2)}, u32[]{:S(2)}) collective-permute-start(bf16[8,7168]{1,0:T(8,128)(2,1)S(1)} %bitcast.277), channel_id=1, source_target_pairs={{0,64},{1,65},{2,66},{3,67},{4,68},{5,69},{6,70},{7,71},{8,72},{9,... | collective-permute-start | bytes 344072 | tf_op jit(solution)/shard_map/ppermute | solution.py:46
  (9 other events, 123.5 us)

commit v7 on v5

--- a/solution.py
+++ b/solution.py
@@ -78,8 +78,28 @@
     mine = (slot[:, None] // CAP == at[None, :] // rows_dev)[None]
     picked = mine & routed[:, None, :] & (rank[:, None, :] == (slot % CAP)[None, :, None])
     weigher = jnp.where(picked, weight[:, None, :], 0.0)
-    shape = (peers * slots, rows)
-    return picked.astype(jnp.bfloat16).reshape(shape), weigher.reshape(shape)
+    return picked.astype(jnp.bfloat16), weigher
+
+
+def pick(picker, rows):
+    return lax.dot_general(
+        picker, rows, (((2,), (0,)), ((), ())), preferred_element_type=jnp.float32
+    ).astype(jnp.bfloat16)
+
+
+def mix(weigher, outputs):
+    return jnp.dot(
+        weigher.reshape(-1, weigher.shape[-1]).T,
+        outputs.reshape(-1, outputs.shape[-1]).astype(jnp.float32),
+        precision=lax.Precision.HIGHEST,
+        preferred_element_type=jnp.float32,
+    )
+
+
+def whole_quarter(mine, other, pair):
+    pieces = jnp.stack([mine, other, mine], axis=1)
+    pieces = lax.dynamic_slice_in_dim(pieces, pair, 2, 1)
+    return pieces.reshape(mine.shape[0], -1)
 
 
 def body(hidden, norm_gain, w_up, w_down, expert_ids, route_gates):
@@ -111,20 +131,30 @@
     arrived, up, up_far, down = lax.optimization_barrier((arrived, up, up_far, down))
     arrived = arrived.reshape(HALVES, block, part + LANES)
     arrived = lax.dynamic_slice_in_dim(jnp.concatenate([arrived, arrived]), half, HALVES, 0)
-    arrived = arrived.reshape(HALVES * block, part + LANES)
-    rows = arrived[:, :part]
-    facts = arrived[:, part:].astype(jnp.float32)
-    routes = facts[:, : 4 * passes * top].reshape(HALVES * block, 4, passes, top)
+    own, other = arrived[0, :, :part], arrived[1, :, :part]
+    facts = arrived[:, :, part:].astype(jnp.float32)
+    routes = facts[:, :, : 4 * passes * top].reshape(HALVES, block, 4, passes, top)
 
     up = [up[0], up[1], up_far[0], up_far[1]]
     gain = lax.dynamic_slice_in_dim(norm_gain[0], place % PAIR * part, part, 0)
 
     for t in range(passes):
-        ids = routes[:, 0, t].astype(jnp.int32)
-        gates = jnp.sum(routes[:, 1:, t], axis=1)
-        picker, weigher = tables(ids, gates, half, peers, rows_dev)
-        slots = jnp.dot(picker, rows, preferred_element_type=jnp.float32).astype(jnp.bfloat16)
-        slots = exchange(slots, same_place)
+        ids = routes[:, :, 0, t].astype(jnp.int32)
+        gates = jnp.sum(routes[:, :, 1:, t], axis=2)
+        own_picker, own_weigher = tables(ids[0], gates[0], half, peers, rows_dev)
+        other_picker, other_weigher = tables(ids[1], gates[1], half, peers, rows_dev)
+        if t == 0:
+            slots = jnp.concatenate([pick(own_picker, own), pick(other_picker, other)], axis=1)
+            slots = exchange(slots, same_place)
+        else:
+            mine = next_section(mine)
+            theirs = swap(mine, 8)
+            own = whole_quarter(mine, swap(mine, 4), pair)
+            own_slots = exchange(pick(own_picker, own), same_place)
+            other = whole_quarter(theirs, swap(theirs, 4), pair)
+            other_slots = exchange(pick(other_picker, other), same_place)
+            slots = jnp.concatenate([own_slots, other_slots], axis=1)
+        slots = slots.reshape(-1, part)
         if t == 0:
             slots, down_far = lax.optimization_barrier((slots, down_far))
             down = jnp.concatenate([down, down_far]).reshape(PAIR * HID_DEV, part)
@@ -146,30 +176,24 @@
         active = jnp.concatenate([active, swap(active, 2)])
         active = jnp.concatenate([active[k] for k in range(PAIR)], axis=1)
         outputs = jnp.dot(active, down, preferred_element_type=jnp.float32).astype(jnp.bfloat16)
-        outputs = exchange(outputs, same_place)
-        mixture = jnp.dot(
-            weigher.T,
-            outputs.astype(jnp.float32),
-            precision=lax.Precision.HIGHEST,
-            preferred_element_type=jnp.float32,
-        )
+        outputs = outputs.reshape(peers, HALVES, -1, part)
         if t + 1 < passes:
-            mixture = mixture.reshape(2 * block, 2, piece)
-            mine = take(mixture, pair, 1)
-            mine = mine + swap(take(mixture, 1 - pair, 1).astype(jnp.bfloat16), 4).astype(
-                jnp.float32
-            )
-            kept = take(rows[block:].reshape(block, 2, piece), pair, 1).astype(jnp.float32)
-            other = swap(mine[:block].astype(jnp.bfloat16), 8).astype(jnp.float32)
-            own = next_section((kept + mine[block:] + other).astype(jnp.bfloat16))
-            rows = jnp.concatenate([own, swap(own, 8)])
-            pieces = jnp.stack([rows, swap(rows, 4), rows], axis=1)
-            rows = lax.dynamic_slice_in_dim(pieces, pair, 2, 1).reshape(2 * block, part)
+            own_mix = mix(own_weigher, exchange(outputs[:, 0], same_place))
+            crossed = swap(own_mix.astype(jnp.bfloat16), 8).astype(jnp.float32)
+            other_mix = mix(other_weigher, exchange(outputs[:, 1], same_place)) + crossed
+            other_mix = other_mix.reshape(block, 2, piece)
+            given = swap(take(other_mix, 1 - pair, 1).astype(jnp.bfloat16), 4)
+            kept = take(other.reshape(block, 2, piece), pair, 1).astype(jnp.float32)
+            mine = kept + take(other_mix, pair, 1) + given.astype(jnp.float32)
+            mine = mine.astype(jnp.bfloat16)
         else:
-            own = mixture[:block].astype(jnp.bfloat16)
-            kept = jnp.where(pair == 0, rows[block:].astype(jnp.float32), 0.0)
-            other = (kept + mixture[block:]).astype(jnp.bfloat16)
-            both = lax.dynamic_slice_in_dim(jnp.stack([other, own, other]), half, HALVES, 0)
+            outputs = exchange(outputs.reshape(peers, -1, part), same_place)
+            outputs = outputs.reshape(peers, HALVES, -1, part)
+            own_mix = mix(own_weigher, outputs[:, 0]).astype(jnp.bfloat16)
+            kept = jnp.where(pair == 0, other.astype(jnp.float32), 0.0)
+            other_mix = (kept + mix(other_weigher, outputs[:, 1])).astype(jnp.bfloat16)
+            both = jnp.stack([other_mix, own_mix, other_mix])
+            both = lax.dynamic_slice_in_dim(both, half, HALVES, 0)
             both = exchange(both.reshape(HALVES * GROUP, rows_dev, part), same_row)
             both = both.reshape(2 * HALVES, PAIR, rows_dev, part).astype(jnp.float32)
             done = jnp.sum(both, axis=0).astype(jnp.bfloat16)

time: 328 us -> 362 us (1.10)
  starting transfers between devices: 81.7 us -> 100 us
  waiting for transfers between devices: 152 us -> 165 us
  blocking collectives: 47.9 us -> 41.3 us
  local copies, waits for them, and re-layouts: 13.7 us -> 18.2 us
    ppermute x16 -> x17, waiting for transfers between devices: 99.1 us -> 114 us  [swap(): return lax.ppermute(value, 'expert', [(i, i ^ bit) for i in range(count)])]
    ppermute x2, starting transfers between devices: 5.57 us -> 13.5 us  [next_section(): return lax.ppermute(value, ('section', 'expert'), route)]
    all_to_all x4 -> x6, starting transfers between devices: 24 us -> 31.6 us  [exchange(): lax.all_to_all(value, 'expert', split_axis=0, concat_axis=0, axis_index_g...]
    all_to_all x2, blocking collectives: 47.9 us -> 41.3 us  [exchange(): lax.all_to_all(value, 'expert', split_axis=0, concat_axis=0, axis_index_g...]
    all_to_all x4 -> x6, waiting for transfers between devices: 24.3 us -> 20.2 us  [exchange(): lax.all_to_all(value, 'expert', split_axis=0, concat_axis=0, axis_index_g...]
    ppermute x16 -> x17, starting transfers between devices: 52.1 us -> 55.2 us  [swap(): return lax.ppermute(value, 'expert', [(i, i ^ bit) for i in range(count)])]
    dot_general x4 -> x8, matrix products: 4.69 us -> 7.27 us  [the longest x4 5.17 us: mix(): jnp.dot(weigher.reshape(-1, weigher.shape[-1]).T, outputs.reshape(-1, out...]
  transfers between devices with their start and end apart: 22 -> 25, of which waited for: 19 -> 21; matrix products, arithmetic and copies ran while one was open for 5% -> 6% of each run, Pallas kernels for 0% -> 0%
where the time goes in v7:
time: 362 us; the launch traced here: 359 us
  waiting for transfers between devices  165 us (46%)
  starting transfers between devices  100 us (28%)
  blocking collectives  41.3 us (11%)
  matrix products  19.1 us (5%)
  local copies, waits for them, and re-layouts  18.2 us (5%)
  other arithmetic  14.8 us (4%)
    ppermute x17, waiting for transfers between devices, swap(): return lax.ppermute(value, 'expert', [(i, i ^ bit) for i in range(count)])  114 us
    ppermute x17, starting transfers between devices, swap(): return lax.ppermute(value, 'expert', [(i, i ^ bit) for i in range(count)])  55.2 us
    all_to_all x2, blocking collectives, exchange(): lax.all_to_all(value, 'expert', split_axis=0, concat_axis=0, axis_index_g...  41.3 us
    all_to_all x6, starting transfers between devices, exchange(): lax.all_to_all(value, 'expert', split_axis=0, concat_axis=0, axis_index_g...  31.6 us
    ppermute x2, waiting for transfers between devices, next_section(): return lax.ppermute(value, ('section', 'expert'), route)  31.2 us
    all_to_all x6, waiting for transfers between devices, exchange(): lax.all_to_all(value, 'expert', split_axis=0, concat_axis=0, axis_index_g...  20.2 us
    ppermute x2, starting transfers between devices, next_section(): return lax.ppermute(value, ('section', 'expert'), route)  13.5 us
    dot_general x8, matrix products, body(): jnp.dot(scaled, up[k], preferred_element_type=jnp.float32)  8.84 us
  transfers between devices with their start and end apart: 25, of which 21 were waited for; matrix products, arithmetic and copies ran while one was open for 6% of the time, Pallas kernels for 0%

profile of v7, /device:TPU:7, one launch (start us, length us, event | category | flops | bytes accessed | tf_op | source)
XLA Modules:
  0.0 359.3 jit_solution(1523247876940999253)
XLA Ops:
  9.0 12.7 %all-to-all-start = ((bf16[16,8,1920]{2,1,0:T(8,128)(2,1)}), bf16[16,8,1920]{2,1,0:T(8,128)(2,1)S(1)}, u32[]{:S(2)}, u32[]{:S(2)}) async-start(bf16[16,8,1920]{2,1,0:T(8,128)(2,1)} %maximum_maximum_fusion), calls=%async_computation | async-start | bytes 983040 | tf_op jit(solution)/shard_map/all_to_all | solution.py:23
  41.4 16.8 %collective-permute-done.1 = bf16[2,1792,128]{2,1,0:T(8,128)(2,1)} collective-permute-done((bf16[2,1792,128]{2,1,0:T(8,128)(2,1)}, bf16[2,1792,128]{2,1,0:T(8,128)(2,1)}, u32[]{:S(2)}, u32[]{:S(2)}) %collective-permute-start.1) | collective-permute-done | bytes 917536 | tf_op jit(solution)/shard_map/ppermute | solution.py:30
  61.4 4.3 %all-to-all-start.1 = ((bf16[4,64,1792]{2,1,0:T(8,128)(2,1)}), bf16[4,64,1792]{2,1,0:T(8,128)(2,1)S(1)}, u32[]{:S(2)}, u32[]{:S(2)}) async-start(bf16[4,64,1792]{2,1,0:T(8,128)(2,1)} %pad_maximum_fusion.1), calls=%async_computation.1 | async-start | bytes 1835008 | tf_op jit(solution)/shard_map/all_to_all | solution.py:23
  65.7 12.1 %collective-permute-done.3 = bf16[2,128,1792]{2,1,0:T(8,128)(2,1)} collective-permute-done((bf16[2,128,1792]{2,1,0:T(8,128)(2,1)}, bf16[2,128,1792]{2,1,0:T(8,128)(2,1)}, u32[]{:S(2)}, u32[]{:S(2)}) %collective-permute-start.3) | collective-permute-done | bytes 917536 | tf_op jit(solution)/shard_map/ppermute | solution.py:30
  80.2 4.3 %collective-permute-start.4 = (f32[3,256,128]{1,2,0:T(8,128)S(1)}, f32[3,256,128]{1,2,0:T(8,128)S(1)}, u32[]{:S(2)}, u32[]{:S(2)}) collective-permute-start(f32[3,256,128]{1,2,0:T(8,128)S(1)} %pad_maximum_fusion.3), channel_id=1, source_target_pairs={{0,1},{1,0},{2,3},{3,2},{4,5},{5,4},{6,7},{7,6},{8,9},{9,8},{10,11... | collective-permute-start | bytes 1179656 | tf_op jit(solution)/shard_map/ppermute | solution.py:30
  89.4 7.5 %collective-permute-done.5 = f32[2,256,128]{1,2,0:T(8,128)S(1)} collective-permute-done((f32[2,256,128]{1,2,0:T(8,128)S(1)}, f32[2,256,128]{1,2,0:T(8,128)S(1)}, u32[]{:S(2)}, u32[]{:S(2)}) %collective-permute-start.5) | collective-permute-done | bytes 262176 | tf_op jit(solution)/shard_map/ppermute | solution.py:30
  113.3 7.2 %all-to-all-done.3 = bf16[4,32,1792]{2,1,0:T(8,128)(2,1)S(1)} async-done(((bf16[4,32,1792]{2,1,0:T(8,128)(2,1)}), bf16[4,32,1792]{2,1,0:T(8,128)(2,1)S(1)}, u32[]{:S(2)}, u32[]{:S(2)}) %all-to-all-start.3) | async-done | bytes 458784 | tf_op jit(solution)/shard_map/all_to_all | solution.py:23
  126.9 12.4 %collective-permute-start.8 = (bf16[64,1792]{1,0:T(8,128)(2,1)}, bf16[64,1792]{1,0:T(8,128)(2,1)}, u32[]{:S(2)}, u32[]{:S(2)}) collective-permute-start(bf16[64,1792]{1,0:T(8,128)(2,1)} %fusion), channel_id=1, source_target_pairs={{0,8},{1,9},{2,10},{3,11},{4,12},{5,13},{6,14},{7,15},{8,0},{9,1},... | collective-permute-start | bytes 688136 | tf_op jit(solution)/shard_map/ppermute | solution.py:30
  139.3 21.0 %collective-permute-done.8 = bf16[64,1792]{1,0:T(8,128)(2,1)} collective-permute-done((bf16[64,1792]{1,0:T(8,128)(2,1)}, bf16[64,1792]{1,0:T(8,128)(2,1)}, u32[]{:S(2)}, u32[]{:S(2)}) %collective-permute-start.8) | collective-permute-done | bytes 229408 | tf_op jit(solution)/shard_map/ppermute | solution.py:30
  167.8 7.4 %collective-permute-done.9 = bf16[64,896]{0,1:T(8,128)(2,1)S(1)} collective-permute-done((bf16[64,896]{0,1:T(8,128)(2,1)S(1)}, bf16[64,896]{0,1:T(8,128)(2,1)S(1)}, u32[]{:S(2)}, u32[]{:S(2)}) %collective-permute-start.9) | collective-permute-done | bytes 114720 | tf_op jit(solution)/shard_map/ppermute | solution.py:30
  176.3 7.2 %collective-permute-start.10 = (bf16[64,896]{0,1:T(8,128)(2,1)S(1)}, bf16[64,896]{0,1:T(8,128)(2,1)S(1)}, u32[]{:S(2)}, u32[]{:S(2)}) collective-permute-start(bf16[64,896]{0,1:T(8,128)(2,1)S(1)} %fusion.43), channel_id=1, source_target_pairs={{0,72},{1,73},{2,74},{3,75},{4,76},{5,77},{6,78},{7,79},{8,64},{9,... | collective-permute-start | bytes 344072 | tf_op jit(solution)/shard_map/ppermute | solution.py:40
  183.7 18.5 %collective-permute-done.10 = bf16[64,896]{0,1:T(8,128)(2,1)S(1)} collective-permute-done((bf16[64,896]{0,1:T(8,128)(2,1)S(1)}, bf16[64,896]{0,1:T(8,128)(2,1)S(1)}, u32[]{:S(2)}, u32[]{:S(2)}) %collective-permute-start.10) | collective-permute-done | bytes 114720 | tf_op jit(solution)/shard_map/ppermute | solution.py:40
  207.7 4.0 %collective-permute-done.13 = bf16[64,896]{0,1:T(8,128)(2,1)S(1)} collective-permute-done((bf16[64,896]{0,1:T(8,128)(2,1)S(1)}, bf16[64,896]{0,1:T(8,128)(2,1)S(1)}, u32[]{:S(2)}, u32[]{:S(2)}) %collective-permute-start.13) | collective-permute-done | bytes 114720 | tf_op jit(solution)/shard_map/ppermute | solution.py:30
  212.1 19.5 %collective-permute-done.11 = bf16[64,896]{0,1:T(8,128)(2,1)S(1)} collective-permute-done((bf16[64,896]{0,1:T(8,128)(2,1)S(1)}, bf16[64,896]{0,1:T(8,128)(2,1)S(1)}, u32[]{:S(2)}, u32[]{:S(2)}) %collective-permute-start.11) | collective-permute-done | bytes 114720 | tf_op jit(solution)/shard_map/ppermute | solution.py:30
  234.6 4.2 %all-to-all-start.4 = ((bf16[4,32,1792]{2,1,0:T(8,128)(2,1)}), bf16[4,32,1792]{2,1,0:T(8,128)(2,1)S(1)}, u32[]{:S(2)}, u32[]{:S(2)}) async-start(bf16[4,32,1792]{2,1,0:T(8,128)(2,1)} %convolution_convert_fusion.3), calls=%async_computation.4 | async-start | bytes 917504 | tf_op jit(solution)/shard_map/all_to_all | solution.py:23
  238.8 5.5 %collective-permute-done.12 = bf16[64,896]{0,1:T(8,128)(2,1)S(1)} collective-permute-done((bf16[64,896]{0,1:T(8,128)(2,1)S(1)}, bf16[64,896]{0,1:T(8,128)(2,1)S(1)}, u32[]{:S(2)}, u32[]{:S(2)}) %collective-permute-start.12) | collective-permute-done | bytes 114720 | tf_op jit(solution)/shard_map/ppermute | solution.py:30
  246.5 9.9 %all_to_all.40 = bf16[4,32,1792]{2,1,0:T(8,128)(2,1)S(1)} all-to-all(bf16[4,32,1792]{2,1,0:T(8,128)(2,1)S(1)} %convolution_convert_fusion.2), channel_id=1, replica_groups={{0,16,32,48},{1,17,33,49},{2,18,34,50},{3,19,35,51},{4,20,36,52},{5,21,..., dimensions={0} | all-to-all | bytes 917504 | tf_op jit(solution)/shard_map/all_to_all | solution.py:23
  260.9 5.1 %collective-permute-start.14 = (f32[3,256,128]{1,2,0:T(8,128)S(1)}, f32[3,256,128]{1,2,0:T(8,128)S(1)}, u32[]{:S(2)}, u32[]{:S(2)}) collective-permute-start(f32[3,256,128]{1,2,0:T(8,128)S(1)} %pad_maximum_fusion.4), channel_id=1, source_target_pairs={{0,1},{1,0},{2,3},{3,2},{4,5},{5,4},{6,7},{7,6},{8,9},{9,8},{10,11... | collective-permute-start | bytes 1179656 | tf_op jit(solution)/shard_map/ppermute | solution.py:30
  271.0 7.3 %collective-permute-done.15 = f32[2,256,128]{1,2,0:T(8,128)S(1)} collective-permute-done((f32[2,256,128]{1,2,0:T(8,128)S(1)}, f32[2,256,128]{1,2,0:T(8,128)S(1)}, u32[]{:S(2)}, u32[]{:S(2)}) %collective-permute-start.15) | collective-permute-done | bytes 262176 | tf_op jit(solution)/shard_map/ppermute | solution.py:30
  284.8 4.7 %collective-permute-done.17 = bf16[2,256,128]{1,2,0:T(8,128)(2,1)S(1)} collective-permute-done((bf16[2,256,128]{1,2,0:T(8,128)(2,1)S(1)}, bf16[2,256,128]{1,2,0:T(8,128)(2,1)S(1)}, u32[]{:S(2)}, u32[]{:S(2)}) %collective-permute-start.17) | collective-permute-done | bytes 131104 | tf_op jit(solution)/shard_map/ppermute | solution.py:30
  294.9 12.2 %all-to-all-done.6 = bf16[4,64,1792]{2,1,0:T(8,128)(2,1)S(1)} async-done(((bf16[4,64,1792]{2,1,0:T(8,128)(2,1)}), bf16[4,64,1792]{2,1,0:T(8,128)(2,1)S(1)}, u32[]{:S(2)}, u32[]{:S(2)}) %all-to-all-start.6) | async-done | bytes 917536 | tf_op jit(solution)/shard_map/all_to_all | solution.py:23
  308.2 31.3 %all_to_all.41 = bf16[16,8,1792]{2,1,0:T(8,128)(2,1)S(1)} all-to-all(bf16[16,8,1792]{2,1,0:T(8,128)(2,1)S(1)} %bitcast.295), channel_id=1, replica_groups={{0,1,2,3,4,5,6,7,8,9,10,11,12,13,14,15},{16,17,18,19,20,21,22,23,24,25,..., dimensions={0} | all-to-all | bytes 917504 | tf_op jit(solution)/shard_map/all_to_all | solution.py:23
  339.7 6.3 %collective-permute-start.18 = (bf16[8,7168]{1,0:T(8,128)(2,1)S(1)}, bf16[8,7168]{1,0:T(8,128)(2,1)S(1)}, u32[]{:S(2)}, u32[]{:S(2)}) collective-permute-start(bf16[8,7168]{1,0:T(8,128)(2,1)S(1)} %bitcast.313), channel_id=1, source_target_pairs={{0,72},{1,73},{2,74},{3,75},{4,76},{5,77},{6,78},{7,79},{8,64},{9,... | collective-permute-start | bytes 344072 | tf_op jit(solution)/shard_map/ppermute | solution.py:40
  346.0 12.7 %collective-permute-done.18 = bf16[8,7168]{1,0:T(8,128)(2,1)S(1)} collective-permute-done((bf16[8,7168]{1,0:T(8,128)(2,1)S(1)}, bf16[8,7168]{1,0:T(8,128)(2,1)S(1)}, u32[]{:S(2)}, u32[]{:S(2)}) %collective-permute-start.18) | collective-permute-done | bytes 114720 | tf_op jit(solution)/shard_map/ppermute | solution.py:40
  (123 shorter events, 104.4 us)
Async XLA Ops:
  6.4 21.7 %collective-permute-start = (bf16[2,1792,128]{2,1,0:T(8,128)(2,1)}, bf16[2,1792,128]{2,1,0:T(8,128)(2,1)}, u32[]{:S(2)}, u32[]{:S(2)}) collective-permute-start(bf16[2,1792,128]{2,1,0:T(8,128)(2,1)} %get-tuple-element.39), channel_id=1, source_target_pairs={{0,1},{1,0},{2,3},{3,2},{4,5},{5,4},{6,7},{7,6},{8,9},{9,8},{10,11... | collective-permute-start | bytes 2752520 | tf_op jit(solution)/shard_map/ppermute | solution.py:30
  9.0 49.2 %all-to-all-start = ((bf16[16,8,1920]{2,1,0:T(8,128)(2,1)}), bf16[16,8,1920]{2,1,0:T(8,128)(2,1)S(1)}, u32[]{:S(2)}, u32[]{:S(2)}) async-start(bf16[16,8,1920]{2,1,0:T(8,128)(2,1)} %maximum_maximum_fusion), calls=%async_computation | async-start | bytes 983040 | tf_op jit(solution)/shard_map/all_to_all | solution.py:23
  26.0 8.6 %collective-permute-start.2 = (bf16[2,128,1792]{1,2,0:T(8,128)(2,1)}, bf16[2,128,1792]{1,2,0:T(8,128)(2,1)S(1)}, u32[]{:S(2)}, u32[]{:S(2)}) collective-permute-start(bf16[2,128,1792]{1,2,0:T(8,128)(2,1)} %get-tuple-element.35), channel_id=1, source_target_pairs={{0,1},{1,0},{2,3},{3,2},{4,5},{5,4},{6,7},{7,6},{8,9},{9,8},{10,11... | collective-permute-start | bytes 2752520 | tf_op jit(solution)/shard_map/ppermute | solution.py:30
  30.9 27.3 %collective-permute-start.1 = (bf16[2,1792,128]{2,1,0:T(8,128)(2,1)}, bf16[2,1792,128]{2,1,0:T(8,128)(2,1)}, u32[]{:S(2)}, u32[]{:S(2)}) collective-permute-start(bf16[2,1792,128]{2,1,0:T(8,128)(2,1)} %get-tuple-element.37), channel_id=1, source_target_pairs={{0,2},{1,3},{2,0},{3,1},{4,6},{5,7},{6,4},{7,5},{8,10},{9,11},{10,... | collective-permute-start | bytes 2752520 | tf_op jit(solution)/shard_map/ppermute | solution.py:30
  39.5 38.4 %collective-permute-start.3 = (bf16[2,128,1792]{2,1,0:T(8,128)(2,1)}, bf16[2,128,1792]{2,1,0:T(8,128)(2,1)}, u32[]{:S(2)}, u32[]{:S(2)}) collective-permute-start(bf16[2,128,1792]{2,1,0:T(8,128)(2,1)} %bitcast.30), channel_id=1, source_target_pairs={{0,2},{1,3},{2,0},{3,1},{4,6},{5,7},{6,4},{7,5},{8,10},{9,11},{10,... | collective-permute-start | bytes 2752520 | tf_op jit(solution)/shard_map/ppermute | solution.py:30
  61.4 16.6 %all-to-all-start.1 = ((bf16[4,64,1792]{2,1,0:T(8,128)(2,1)}), bf16[4,64,1792]{2,1,0:T(8,128)(2,1)S(1)}, u32[]{:S(2)}, u32[]{:S(2)}) async-start(bf16[4,64,1792]{2,1,0:T(8,128)(2,1)} %pad_maximum_fusion.1), calls=%async_computation.1 | async-start | bytes 1835008 | tf_op jit(solution)/shard_map/all_to_all | solution.py:23
  80.2 5.7 %collective-permute-start.4 = (f32[3,256,128]{1,2,0:T(8,128)S(1)}, f32[3,256,128]{1,2,0:T(8,128)S(1)}, u32[]{:S(2)}, u32[]{:S(2)}) collective-permute-start(f32[3,256,128]{1,2,0:T(8,128)S(1)} %pad_maximum_fusion.3), channel_id=1, source_target_pairs={{0,1},{1,0},{2,3},{3,2},{4,5},{5,4},{6,7},{7,6},{8,9},{9,8},{10,11... | collective-permute-start | bytes 1179656 | tf_op jit(solution)/shard_map/ppermute | solution.py:30
  87.3 9.5 %collective-permute-start.5 = (f32[2,256,128]{1,2,0:T(8,128)S(1)}, f32[2,256,128]{1,2,0:T(8,128)S(1)}, u32[]{:S(2)}, u32[]{:S(2)}) collective-permute-start(f32[2,256,128]{1,2,0:T(8,128)S(1)} %pad_maximum_fusion.5), channel_id=1, source_target_pairs={{0,2},{1,3},{2,0},{3,1},{4,6},{5,7},{6,4},{7,5},{8,10},{9,11},{10,... | collective-permute-start | bytes 786440 | tf_op jit(solution)/shard_map/ppermute | solution.py:30
  101.4 6.6 %collective-permute-start.7 = (bf16[2,256,128]{1,2,0:T(8,128)(2,1)S(1)}, bf16[2,256,128]{1,2,0:T(8,128)(2,1)S(1)}, u32[]{:S(2)}, u32[]{:S(2)}) collective-permute-start(bf16[2,256,128]{1,2,0:T(8,128)(2,1)S(1)} %pad_maximum_fusion.7), channel_id=1, source_target_pairs={{0,2},{1,3},{2,0},{3,1},{4,6},{5,7},{6,4},{7,5},{8,10},{9,11},{10,... | collective-permute-start | bytes 393224 | tf_op jit(solution)/shard_map/ppermute | solution.py:30
  109.7 10.8 %all-to-all-start.3 = ((bf16[4,32,1792]{2,1,0:T(8,128)(2,1)}), bf16[4,32,1792]{2,1,0:T(8,128)(2,1)S(1)}, u32[]{:S(2)}, u32[]{:S(2)}) async-start(bf16[4,32,1792]{2,1,0:T(8,128)(2,1)} %get-tuple-element.46), calls=%async_computation.3 | async-start | bytes 917504 | tf_op jit(solution)/shard_map/all_to_all | solution.py:23
  121.2 18.1 %all-to-all-start.2 = ((bf16[4,32,1792]{2,1,0:T(8,128)(2,1)}), bf16[4,32,1792]{2,1,0:T(8,128)(2,1)S(1)}, u32[]{:S(2)}, u32[]{:S(2)}) async-start(bf16[4,32,1792]{2,1,0:T(8,128)(2,1)} %get-tuple-element.45), calls=%async_computation.2 | async-start | bytes 917504 | tf_op jit(solution)/shard_map/all_to_all | solution.py:23
  126.9 33.4 %collective-permute-start.8 = (bf16[64,1792]{1,0:T(8,128)(2,1)}, bf16[64,1792]{1,0:T(8,128)(2,1)}, u32[]{:S(2)}, u32[]{:S(2)}) collective-permute-start(bf16[64,1792]{1,0:T(8,128)(2,1)} %fusion), channel_id=1, source_target_pairs={{0,8},{1,9},{2,10},{3,11},{4,12},{5,13},{6,14},{7,15},{8,0},{9,1},... | collective-permute-start | bytes 688136 | tf_op jit(solution)/shard_map/ppermute | solution.py:30
  165.8 9.4 %collective-permute-start.9 = (bf16[64,896]{0,1:T(8,128)(2,1)S(1)}, bf16[64,896]{0,1:T(8,128)(2,1)S(1)}, u32[]{:S(2)}, u32[]{:S(2)}) collective-permute-start(bf16[64,896]{0,1:T(8,128)(2,1)S(1)} %fusion.91), channel_id=1, source_target_pairs={{0,4},{1,5},{2,6},{3,7},{4,0},{5,1},{6,2},{7,3},{8,12},{9,13},{10,... | collective-permute-start | bytes 344072 | tf_op jit(solution)/shard_map/ppermute | solution.py:30
  176.3 25.9 %collective-permute-start.10 = (bf16[64,896]{0,1:T(8,128)(2,1)S(1)}, bf16[64,896]{0,1:T(8,128)(2,1)S(1)}, u32[]{:S(2)}, u32[]{:S(2)}) collective-permute-start(bf16[64,896]{0,1:T(8,128)(2,1)S(1)} %fusion.43), channel_id=1, source_target_pairs={{0,72},{1,73},{2,74},{3,75},{4,76},{5,77},{6,78},{7,79},{8,64},{9,... | collective-permute-start | bytes 344072 | tf_op jit(solution)/shard_map/ppermute | solution.py:40
  202.2 9.5 %collective-permute-start.13 = (bf16[64,896]{0,1:T(8,128)(2,1)S(1)}, bf16[64,896]{0,1:T(8,128)(2,1)S(1)}, u32[]{:S(2)}, u32[]{:S(2)}) collective-permute-start(bf16[64,896]{0,1:T(8,128)(2,1)S(1)} %collective-permute-done.10), channel_id=1, source_target_pairs={{0,4},{1,5},{2,6},{3,7},{4,0},{5,1},{6,2},{7,3},{8,12},{9,13},{10,... | collective-permute-start | bytes 344072 | tf_op jit(solution)/shard_map/ppermute | solution.py:30
  204.3 27.2 %collective-permute-start.11 = (bf16[64,896]{0,1:T(8,128)(2,1)S(1)}, bf16[64,896]{0,1:T(8,128)(2,1)S(1)}, u32[]{:S(2)}, u32[]{:S(2)}) collective-permute-start(bf16[64,896]{0,1:T(8,128)(2,1)S(1)} %collective-permute-done.10), channel_id=1, source_target_pairs={{0,8},{1,9},{2,10},{3,11},{4,12},{5,13},{6,14},{7,15},{8,0},{9,1},... | collective-permute-start | bytes 344072 | tf_op jit(solution)/shard_map/ppermute | solution.py:30
  231.6 12.7 %collective-permute-start.12 = (bf16[64,896]{0,1:T(8,128)(2,1)S(1)}, bf16[64,896]{0,1:T(8,128)(2,1)S(1)}, u32[]{:S(2)}, u32[]{:S(2)}) collective-permute-start(bf16[64,896]{0,1:T(8,128)(2,1)S(1)} %collective-permute-done.11), channel_id=1, source_target_pairs={{0,4},{1,5},{2,6},{3,7},{4,0},{5,1},{6,2},{7,3},{8,12},{9,13},{10,... | collective-permute-start | bytes 344072 | tf_op jit(solution)/shard_map/ppermute | solution.py:30
  234.6 11.1 %all-to-all-start.4 = ((bf16[4,32,1792]{2,1,0:T(8,128)(2,1)}), bf16[4,32,1792]{2,1,0:T(8,128)(2,1)S(1)}, u32[]{:S(2)}, u32[]{:S(2)}) async-start(bf16[4,32,1792]{2,1,0:T(8,128)(2,1)} %convolution_convert_fusion.3), calls=%async_computation.4 | async-start | bytes 917504 | tf_op jit(solution)/shard_map/all_to_all | solution.py:23
  260.9 6.5 %collective-permute-start.14 = (f32[3,256,128]{1,2,0:T(8,128)S(1)}, f32[3,256,128]{1,2,0:T(8,128)S(1)}, u32[]{:S(2)}, u32[]{:S(2)}) collective-permute-start(f32[3,256,128]{1,2,0:T(8,128)S(1)} %pad_maximum_fusion.4), channel_id=1, source_target_pairs={{0,1},{1,0},{2,3},{3,2},{4,5},{5,4},{6,7},{7,6},{8,9},{9,8},{10,11... | collective-permute-start | bytes 1179656 | tf_op jit(solution)/shard_map/ppermute | solution.py:30
  268.9 9.4 %collective-permute-start.15 = (f32[2,256,128]{1,2,0:T(8,128)S(1)}, f32[2,256,128]{1,2,0:T(8,128)S(1)}, u32[]{:S(2)}, u32[]{:S(2)}) collective-permute-start(f32[2,256,128]{1,2,0:T(8,128)S(1)} %pad_maximum_fusion.6), channel_id=1, source_target_pairs={{0,2},{1,3},{2,0},{3,1},{4,6},{5,7},{6,4},{7,5},{8,10},{9,11},{10,... | collective-permute-start | bytes 786440 | tf_op jit(solution)/shard_map/ppermute | solution.py:30
  278.8 4.0 %collective-permute-start.16 = (bf16[256,128]{0,1:T(8,128)(2,1)S(1)}, bf16[256,128]{0,1:T(8,128)(2,1)S(1)}, u32[]{:S(2)}, u32[]{:S(2)}) collective-permute-start(bf16[256,128]{0,1:T(8,128)(2,1)S(1)} %multiply_convert_fusion), channel_id=1, source_target_pairs={{0,1},{1,0},{2,3},{3,2},{4,5},{5,4},{6,7},{7,6},{8,9},{9,8},{10,11... | collective-permute-start | bytes 196616 | tf_op jit(solution)/shard_map/ppermute | solution.py:30
  282.9 6.6 %collective-permute-start.17 = (bf16[2,256,128]{1,2,0:T(8,128)(2,1)S(1)}, bf16[2,256,128]{1,2,0:T(8,128)(2,1)S(1)}, u32[]{:S(2)}, u32[]{:S(2)}) collective-permute-start(bf16[2,256,128]{1,2,0:T(8,128)(2,1)S(1)} %pad_maximum_fusion.8), channel_id=1, source_target_pairs={{0,2},{1,3},{2,0},{3,1},{4,6},{5,7},{6,4},{7,5},{8,10},{9,11},{10,... | collective-permute-start | bytes 393224 | tf_op jit(solution)/shard_map/ppermute | solution.py:30
  291.1 16.0 %all-to-all-start.6 = ((bf16[4,64,1792]{2,1,0:T(8,128)(2,1)}), bf16[4,64,1792]{2,1,0:T(8,128)(2,1)S(1)}, u32[]{:S(2)}, u32[]{:S(2)}) async-start(bf16[4,64,1792]{2,1,0:T(8,128)(2,1)} %bitcast.85), calls=%async_computation.6 | async-start | bytes 1835008 | tf_op jit(solution)/shard_map/all_to_all | solution.py:23
  339.7 19.0 %collective-permute-start.18 = (bf16[8,7168]{1,0:T(8,128)(2,1)S(1)}, bf16[8,7168]{1,0:T(8,128)(2,1)S(1)}, u32[]{:S(2)}, u32[]{:S(2)}) collective-permute-start(bf16[8,7168]{1,0:T(8,128)(2,1)S(1)} %bitcast.313), channel_id=1, source_target_pairs={{0,72},{1,73},{2,74},{3,75},{4,76},{5,77},{6,78},{7,79},{8,64},{9,... | collective-permute-start | bytes 344072 | tf_op jit(solution)/shard_map/ppermute | solution.py:40
  (8 other events, 122.5 us)

commit v8 on v5

v8 whole, which is shorter than its diff:
```python
import jax
import jax.numpy as jnp
from jax import lax
from jax.sharding import PartitionSpec as P

HID = 1024
HID_DEV = 128
GROUP = HID // HID_DEV
PAIR = 4
CAP = 4
HALVES = 2
LANES = 128


def groups(count):
    span = GROUP * HALVES
    same_row = [[first + k for k in range(span)] for first in range(0, count, span)]
    same_place = [[first + k for first in range(0, count, span)] for k in range(span)]
    return same_row, same_place


def exchange(value, within):
    return lax.all_to_all(
        value, "expert", split_axis=0, concat_axis=0, axis_index_groups=within, tiled=True
    )


def swap(value, bit):
    count = lax.axis_size("expert")
    return lax.ppermute(value, "expert", [(i, i ^ bit) for i in range(count)])


def next_section(value):
    sections, count = lax.axis_size("section"), lax.axis_size("expert")
    route = [
        (s * count + i, (s + 1) % sections * count + (i ^ GROUP))
        for s in range(sections)
        for i in range(count)
    ]
    return lax.ppermute(value, ("section", "expert"), route)


def head(value):
    return lax.reduce_precision(value, exponent_bits=8, mantissa_bits=7)


def in_three(value):
    first = head(value)
    second = head(value - first)
    third = head(value - first - second)
    return [part.astype(jnp.bfloat16) for part in (first, second, third)]


def take(value, index, axis):
    return lax.dynamic_index_in_dim(value, index, axis, keepdims=False)


def recut(quarters, chip, core):
    near = swap(take(quarters, 1 - core, 1), 1)
    both = jnp.stack([take(quarters, core, 1), near], axis=1)
    far = swap(take(both, 1 - chip, 0), 2)
    return take(both, chip, 0), far


def tables(ids, gates, half, peers, rows_dev):
    rows = ids.shape[0]
    wanted = 2 * jnp.arange(peers, dtype=jnp.int32) + half
    hit = ids.T[None, :, :] == wanted[:, None, None]
    routed = jnp.any(hit, axis=1)
    weight = jnp.sum(jnp.where(hit, gates.T[None, :, :], 0.0), axis=1)
    at = jnp.arange(rows, dtype=jnp.int32)
    before = (at[:, None] < at[None, :]) & (at[:, None] // rows_dev == at[None, :] // rows_dev)
    rank = jnp.dot(
        routed.astype(jnp.bfloat16), before.astype(jnp.bfloat16), preferred_element_type=jnp.float32
    ).astype(jnp.int32)
    slots = rows // rows_dev * CAP
    slot = jnp.arange(slots, dtype=jnp.int32)
    mine = (slot[:, None] // CAP == at[None, :] // rows_dev)[None]
    picked = mine & routed[:, None, :] & (rank[:, None, :] == (slot % CAP)[None, :, None])
    weigher = jnp.where(picked, weight[:, None, :], 0.0)
    shape = (peers * slots, rows)
    return picked.astype(jnp.bfloat16).reshape(shape), weigher.reshape(shape)


def normed_quarters(current, gain):
    values = current.astype(jnp.float32)
    inverse_rms = lax.rsqrt(jnp.mean(values * values, axis=-1, keepdims=True) + 1e-06)
    normed = (values * inverse_rms * gain).astype(jnp.bfloat16)
    return normed.reshape(current.shape[0], PAIR, -1).transpose(1, 0, 2)


def body(hidden, norm_gain, w_up, w_down, expert_ids, route_gates):
    width = hidden.shape[-1]
    rows_dev = hidden.shape[1]
    passes, top = expert_ids.shape[1], expert_ids.shape[-1]
    count = lax.axis_size("expert")
    peers = count // (GROUP * HALVES)
    part = width // PAIR
    block = GROUP * rows_dev
    total = HALVES * block
    same_row, same_place = groups(count)
    place = lax.axis_index("expert")
    core, chip, half = place % 2, place // 2 % 2, place // GROUP % HALVES
    gain = norm_gain[0]
    current = hidden[0]

    facts = [expert_ids[0].astype(jnp.bfloat16)] + in_three(route_gates[0])
    facts = jnp.stack(facts).transpose(2, 0, 1, 3).reshape(rows_dev, -1)
    facts = jnp.pad(facts, ((0, 0), (0, LANES - facts.shape[1])))

    for t in range(passes):
        sent = normed_quarters(current, gain)
        if t == 0:
            facts = jnp.broadcast_to(facts[None], (PAIR, rows_dev, LANES))
            sent = jnp.concatenate([sent, facts], axis=2)
        sent = jnp.concatenate([sent] * (2 * HALVES))
        if t == 0:
            sent, w_up, w_down = lax.optimization_barrier((sent, w_up, w_down))
        arrived = exchange(sent, same_row)
        if t == 0:
            up, up_far = recut(w_up[0].reshape(2, 2, part, HID_DEV), chip, core)
            down = w_down[0].reshape(HID_DEV, 2, 2, part).transpose(1, 2, 0, 3)
            down, down_far = recut(down, chip, core)
            arrived, up, up_far, down = lax.optimization_barrier((arrived, up, up_far, down))
            up = [up[0], up[1], up_far[0], up_far[1]]
            facts = arrived[:, :, part:].astype(jnp.float32).reshape(total, LANES)
            routes = facts[:, : 4 * passes * top].reshape(total, 4, passes, top)
            arrived = arrived[:, :, :part]
        rows = arrived.reshape(total, part)

        ids = routes[:, 0, t].astype(jnp.int32)
        gates = jnp.sum(routes[:, 1:, t], axis=1)
        picker, weigher = tables(ids, gates, half, peers, rows_dev)
        slots = jnp.dot(picker, rows, preferred_element_type=jnp.float32).astype(jnp.bfloat16)
        slots = exchange(slots, same_place)
        if t == 0:
            slots, down_far = lax.optimization_barrier((slots, down_far))
            down = jnp.concatenate([down, down_far]).reshape(PAIR * HID_DEV, part)
        sums = [jnp.dot(slots, up[k], preferred_element_type=jnp.float32) for k in range(PAIR)]
        came = swap(jnp.stack([sums[1], sums[3]]), 1)
        came_far = swap(sums[2] + came[1], 2)
        active = jax.nn.silu(sums[0] + came[0] + came_far).astype(jnp.bfloat16)
        active = jnp.stack([active, swap(active, 1)])
        active = jnp.concatenate([active, swap(active, 2)])
        active = jnp.concatenate([active[k] for k in range(PAIR)], axis=1)
        outputs = jnp.dot(active, down, preferred_element_type=jnp.float32).astype(jnp.bfloat16)
        outputs, current = lax.optimization_barrier((outputs, current))
        residual = swap(current, GROUP)
        outputs, residual = lax.optimization_barrier((exchange(outputs, same_place), residual))
        mixture = jnp.dot(
            weigher.T,
            outputs.astype(jnp.float32),
            precision=lax.Precision.HIGHEST,
            preferred_element_type=jnp.float32,
        )
        mixture = mixture.astype(jnp.bfloat16).reshape(HALVES, GROUP, rows_dev, part)
        mixture = jnp.concatenate([mixture[1], mixture[0]])
        came = exchange(mixture, same_row).reshape(2 * HALVES, PAIR, rows_dev, part)
        came = jnp.sum(came.astype(jnp.float32), axis=0).transpose(1, 0, 2)
        updated = residual.astype(jnp.float32) + came.reshape(rows_dev, width)
        current = next_section(updated.astype(jnp.bfloat16))
    return current[None]


def solution(mesh):
    placed = (
        P("section", "expert", None),
        P("section", None),
        P("section", None, "expert"),
        P("section", "expert", None),
        P("section", None, "expert", None),
        P("section", None, "expert", None),
    )
    return jax.shard_map(
        body, mesh=mesh, in_specs=placed, out_specs=P("section", "expert", None), check_vma=False
    )
```

time: 328 us -> 329 us (level)
  blocking collectives: 47.9 us -> 107 us
  waiting for transfers between devices: 152 us -> 97.9 us
  matrix products: 16.1 us -> 11.2 us
    all_to_all x2 -> x4, blocking collectives: 47.9 us -> 107 us  [exchange(): lax.all_to_all(value, 'expert', split_axis=0, concat_axis=0, axis_index_g...]
    ppermute x16 -> x14, waiting for transfers between devices: 99.1 us -> 70.9 us  [swap(): return lax.ppermute(value, 'expert', [(i, i ^ bit) for i in range(count)])]
    all_to_all x4, waiting for transfers between devices: 24.3 us -> 0.01 us  [exchange(): lax.all_to_all(value, 'expert', split_axis=0, concat_axis=0, axis_index_g...]
    ppermute x2, starting transfers between devices: 5.57 us -> 11.1 us  [next_section(): return lax.ppermute(value, ('section', 'expert'), route)]
    ppermute x16 -> x14, starting transfers between devices: 52.1 us -> 49.5 us  [swap(): return lax.ppermute(value, 'expert', [(i, i ^ bit) for i in range(count)])]
  transfers between devices with their start and end apart: 22 -> 20, of which waited for: 19 -> 14; matrix products, arithmetic and copies ran while one was open for 5% -> 5% of each run, Pallas kernels for 0% -> 0%
where the time goes in v8:
time: 329 us; the launch traced here: 327 us
  blocking collectives  107 us (33%)
  waiting for transfers between devices  97.9 us (30%)
  starting transfers between devices  84.8 us (26%)
  other arithmetic  13.4 us (4%)
  local copies, waits for them, and re-layouts  12.4 us (4%)
  matrix products  11.2 us (3%)
    all_to_all x4, blocking collectives, exchange(): lax.all_to_all(value, 'expert', split_axis=0, concat_axis=0, axis_index_g...  107 us
    ppermute x14, waiting for transfers between devices, swap(): return lax.ppermute(value, 'expert', [(i, i ^ bit) for i in range(count)])  70.9 us
    ppermute x14, starting transfers between devices, swap(): return lax.ppermute(value, 'expert', [(i, i ^ bit) for i in range(count)])  49.5 us
    ppermute x2, waiting for transfers between devices, next_section(): return lax.ppermute(value, ('section', 'expert'), route)  27 us
    all_to_all x4, starting transfers between devices, exchange(): lax.all_to_all(value, 'expert', split_axis=0, concat_axis=0, axis_index_g...  24.2 us
    ppermute x2, starting transfers between devices, next_section(): return lax.ppermute(value, ('section', 'expert'), route)  11.1 us
  transfers between devices with their start and end apart: 20, of which 14 were waited for; matrix products, arithmetic and copies ran while one was open for 5% of the time, Pallas kernels for 0%

profile of v8, /device:TPU:7, one launch (start us, length us, event | category | flops | bytes accessed | tf_op | source)
XLA Modules:
  0.0 327.0 jit_solution(15420205137109339820)
XLA Ops:
  11.8 12.7 %all-to-all-start = ((bf16[16,8,1920]{2,1,0:T(8,128)(2,1)}), bf16[16,8,1920]{2,1,0:T(8,128)(2,1)S(1)}, u32[]{:S(2)}, u32[]{:S(2)}) async-start(bf16[16,8,1920]{2,1,0:T(8,128)(2,1)} %maximum_maximum_fusion), calls=%async_computation | async-start | bytes 983040 | tf_op jit(solution)/shard_map/all_to_all | solution.py:23
  24.5 3.3 %copy.52 = bf16[1,128,7168]{1,2,0:T(8,128)(2,1)S(1)} copy(bf16[1,128,7168]{2,1,0:T(8,128)(2,1)} %param.9) | data formatting | bytes 3670016 | tf_op jit(solution)/shard_map/optimization_barrier | solution.py:118
  33.7 3.5 %collective-permute-start.1 = (bf16[2,1792,128]{2,1,0:T(8,128)(2,1)}, bf16[2,1792,128]{2,1,0:T(8,128)(2,1)S(1)}, u32[]{:S(2)}, u32[]{:S(2)}) collective-permute-start(bf16[2,1792,128]{2,1,0:T(8,128)(2,1)} %get-tuple-element.49), channel_id=1, source_target_pairs={{0,2},{1,3},{2,0},{3,1},{4,6},{5,7},{6,4},{7,5},{8,10},{9,11},{10,... | collective-permute-start | bytes 2752520 | tf_op jit(solution)/shard_map/ppermute | solution.py:30
  45.3 15.6 %collective-permute-done.1 = bf16[2,1792,128]{2,1,0:T(8,128)(2,1)S(1)} collective-permute-done((bf16[2,1792,128]{2,1,0:T(8,128)(2,1)}, bf16[2,1792,128]{2,1,0:T(8,128)(2,1)S(1)}, u32[]{:S(2)}, u32[]{:S(2)}) %collective-permute-start.1) | collective-permute-done | bytes 917536 | tf_op jit(solution)/shard_map/ppermute | solution.py:30
  63.0 4.2 %all-to-all-start.1 = ((bf16[4,64,1792]{2,1,0:T(8,128)(2,1)}), bf16[4,64,1792]{2,1,0:T(8,128)(2,1)S(1)}, u32[]{:S(2)}, u32[]{:S(2)}) async-start(bf16[4,64,1792]{2,1,0:T(8,128)(2,1)} %bitcast.26), calls=%async_computation.1 | async-start | bytes 1835008 | tf_op jit(solution)/shard_map/all_to_all | solution.py:23
  67.2 13.5 %collective-permute-done.3 = bf16[2,128,1792]{2,1,0:T(8,128)(2,1)} collective-permute-done((bf16[2,128,1792]{2,1,0:T(8,128)(2,1)}, bf16[2,128,1792]{2,1,0:T(8,128)(2,1)}, u32[]{:S(2)}, u32[]{:S(2)}) %collective-permute-start.3) | collective-permute-done | bytes 917536 | tf_op jit(solution)/shard_map/ppermute | solution.py:30
  89.2 4.7 %collective-permute-done.5 = f32[256,128]{0,1:T(8,128)S(1)} collective-permute-done((f32[256,128]{0,1:T(8,128)S(1)}, f32[256,128]{0,1:T(8,128)S(1)}, u32[]{:S(2)}, u32[]{:S(2)}) %collective-permute-start.5) | collective-permute-done | bytes 131104 | tf_op jit(solution)/shard_map/ppermute | solution.py:30
  101.7 3.3 %collective-permute-done.7 = bf16[2,256,128]{1,2,0:T(8,128)(2,1)S(1)} collective-permute-done((bf16[2,256,128]{1,2,0:T(8,128)(2,1)S(1)}, bf16[2,256,128]{1,2,0:T(8,128)(2,1)S(1)}, u32[]{:S(2)}, u32[]{:S(2)}) %collective-permute-start.7) | collective-permute-done | bytes 131104 | tf_op jit(solution)/shard_map/ppermute | solution.py:30
  106.7 3.9 %all-to-all-start.2 = ((bf16[4,64,1792]{2,1,0:T(8,128)(2,1)}), bf16[4,64,1792]{2,1,0:T(8,128)(2,1)S(1)}, u32[]{:S(2)}, u32[]{:S(2)}) async-start(bf16[4,64,1792]{2,1,0:T(8,128)(2,1)} %bitcast.203), calls=%async_computation.2 | async-start | bytes 1835008 | tf_op jit(solution)/shard_map/all_to_all | solution.py:23
  110.6 12.5 %collective-permute-start.8 = (bf16[8,7168]{1,0:T(8,128)(2,1)S(1)}, bf16[8,7168]{1,0:T(8,128)(2,1)S(1)}, u32[]{:S(2)}, u32[]{:S(2)}) collective-permute-start(bf16[8,7168]{1,0:T(8,128)(2,1)S(1)} %bitcast.214), channel_id=1, source_target_pairs={{0,8},{1,9},{2,10},{3,11},{4,12},{5,13},{6,14},{7,15},{8,0},{9,1},... | collective-permute-start | bytes 344072 | tf_op jit(solution)/shard_map/ppermute | solution.py:30
  123.3 10.3 %collective-permute-done.8 = bf16[8,7168]{1,0:T(8,128)(2,1)S(1)} collective-permute-done((bf16[8,7168]{1,0:T(8,128)(2,1)S(1)}, bf16[8,7168]{1,0:T(8,128)(2,1)S(1)}, u32[]{:S(2)}, u32[]{:S(2)}) %collective-permute-start.8) | collective-permute-done | bytes 114720 | tf_op jit(solution)/shard_map/ppermute | solution.py:30
  134.3 28.7 %all_to_all.68 = bf16[16,8,1792]{2,1,0:T(8,128)(2,1)S(1)} all-to-all(bf16[16,8,1792]{2,1,0:T(8,128)(2,1)S(1)} %pad_maximum_fusion.1), channel_id=1, replica_groups={{0,1,2,3,4,5,6,7,8,9,10,11,12,13,14,15},{16,17,18,19,20,21,22,23,24,25,..., dimensions={0} | all-to-all | bytes 917504 | tf_op jit(solution)/shard_map/all_to_all | solution.py:23
  163.2 5.4 %collective-permute-start.9 = (bf16[8,7168]{1,0:T(8,128)(2,1)S(1)}, bf16[8,7168]{1,0:T(8,128)(2,1)S(1)}, u32[]{:S(2)}, u32[]{:S(2)}) collective-permute-start(bf16[8,7168]{1,0:T(8,128)(2,1)S(1)} %add_convert_fusion.1), channel_id=1, source_target_pairs={{0,72},{1,73},{2,74},{3,75},{4,76},{5,77},{6,78},{7,79},{8,64},{9,... | collective-permute-start | bytes 344072 | tf_op jit(solution)/shard_map/ppermute | solution.py:40
  168.6 13.6 %collective-permute-done.9 = bf16[8,7168]{1,0:T(8,128)(2,1)S(1)} collective-permute-done((bf16[8,7168]{1,0:T(8,128)(2,1)S(1)}, bf16[8,7168]{1,0:T(8,128)(2,1)S(1)}, u32[]{:S(2)}, u32[]{:S(2)}) %collective-permute-start.9) | collective-permute-done | bytes 114720 | tf_op jit(solution)/shard_map/ppermute | solution.py:40
  182.5 29.3 %all_to_all.69 = bf16[16,8,1792]{2,1,0:T(8,128)(2,1)S(1)} all-to-all(bf16[16,8,1792]{2,1,0:T(8,128)(2,1)S(1)} %pad_maximum_fusion.2), channel_id=1, replica_groups={{0,1,2,3,4,5,6,7,8,9,10,11,12,13,14,15},{16,17,18,19,20,21,22,23,24,25,..., dimensions={0} | all-to-all | bytes 917504 | tf_op jit(solution)/shard_map/all_to_all | solution.py:23
  212.3 17.7 %all_to_all.70 = bf16[4,64,1792]{2,1,0:T(8,128)(2,1)S(1)} all-to-all(bf16[4,64,1792]{2,1,0:T(8,128)(2,1)S(1)} %bitcast.205), channel_id=1, replica_groups={{0,16,32,48},{1,17,33,49},{2,18,34,50},{3,19,35,51},{4,20,36,52},{5,21,..., dimensions={0} | all-to-all | bytes 1835008 | tf_op jit(solution)/shard_map/all_to_all | solution.py:23
  238.8 3.4 %collective-permute-done.11 = f32[256,128]{0,1:T(8,128)S(1)} collective-permute-done((f32[256,128]{0,1:T(8,128)S(1)}, f32[256,128]{0,1:T(8,128)S(1)}, u32[]{:S(2)}, u32[]{:S(2)}) %collective-permute-start.11) | collective-permute-done | bytes 131104 | tf_op jit(solution)/shard_map/ppermute | solution.py:30
  249.9 3.4 %collective-permute-done.13 = bf16[2,256,128]{1,2,0:T(8,128)(2,1)S(1)} collective-permute-done((bf16[2,256,128]{1,2,0:T(8,128)(2,1)S(1)}, bf16[2,256,128]{1,2,0:T(8,128)(2,1)S(1)}, u32[]{:S(2)}, u32[]{:S(2)}) %collective-permute-start.13) | collective-permute-done | bytes 131104 | tf_op jit(solution)/shard_map/ppermute | solution.py:30
  254.9 3.5 %all-to-all-start.6 = ((bf16[4,64,1792]{2,1,0:T(8,128)(2,1)}), bf16[4,64,1792]{2,1,0:T(8,128)(2,1)S(1)}, u32[]{:S(2)}, u32[]{:S(2)}) async-start(bf16[4,64,1792]{2,1,0:T(8,128)(2,1)} %bitcast.67), calls=%async_computation.6 | async-start | bytes 1835008 | tf_op jit(solution)/shard_map/all_to_all | solution.py:23
  258.4 4.6 %collective-permute-start.14 = (bf16[8,7168]{1,0:T(8,128)(2,1)S(1)}, bf16[8,7168]{1,0:T(8,128)(2,1)S(1)}, u32[]{:S(2)}, u32[]{:S(2)}) collective-permute-start(bf16[8,7168]{1,0:T(8,128)(2,1)S(1)} %collective-permute-done.9), channel_id=1, source_target_pairs={{0,8},{1,9},{2,10},{3,11},{4,12},{5,13},{6,14},{7,15},{8,0},{9,1},... | collective-permute-start | bytes 344072 | tf_op jit(solution)/shard_map/ppermute | solution.py:30
  263.0 12.6 %collective-permute-done.14 = bf16[8,7168]{1,0:T(8,128)(2,1)S(1)} collective-permute-done((bf16[8,7168]{1,0:T(8,128)(2,1)S(1)}, bf16[8,7168]{1,0:T(8,128)(2,1)S(1)}, u32[]{:S(2)}, u32[]{:S(2)}) %collective-permute-start.14) | collective-permute-done | bytes 114720 | tf_op jit(solution)/shard_map/ppermute | solution.py:30
  276.3 31.0 %all_to_all.71 = bf16[16,8,1792]{2,1,0:T(8,128)(2,1)S(1)} all-to-all(bf16[16,8,1792]{2,1,0:T(8,128)(2,1)S(1)} %pad_maximum_fusion.3), channel_id=1, replica_groups={{0,1,2,3,4,5,6,7,8,9,10,11,12,13,14,15},{16,17,18,19,20,21,22,23,24,25,..., dimensions={0} | all-to-all | bytes 917504 | tf_op jit(solution)/shard_map/all_to_all | solution.py:23
  307.4 5.7 %collective-permute-start.15 = (bf16[8,7168]{1,0:T(8,128)(2,1)S(1)}, bf16[8,7168]{1,0:T(8,128)(2,1)S(1)}, u32[]{:S(2)}, u32[]{:S(2)}) collective-permute-start(bf16[8,7168]{1,0:T(8,128)(2,1)S(1)} %add_convert_fusion), channel_id=1, source_target_pairs={{0,72},{1,73},{2,74},{3,75},{4,76},{5,77},{6,78},{7,79},{8,64},{9,... | collective-permute-start | bytes 344072 | tf_op jit(solution)/shard_map/ppermute | solution.py:40
  313.0 13.4 %collective-permute-done.15 = bf16[8,7168]{1,0:T(8,128)(2,1)S(1)} collective-permute-done((bf16[8,7168]{1,0:T(8,128)(2,1)S(1)}, bf16[8,7168]{1,0:T(8,128)(2,1)S(1)}, u32[]{:S(2)}, u32[]{:S(2)}) %collective-permute-start.15) | collective-permute-done | bytes 114720 | tf_op jit(solution)/shard_map/ppermute | solution.py:40
  (105 shorter events, 66.7 us)
Async XLA Ops:
  9.2 21.7 %collective-permute-start = (bf16[2,1792,128]{2,1,0:T(8,128)(2,1)}, bf16[2,1792,128]{2,1,0:T(8,128)(2,1)}, u32[]{:S(2)}, u32[]{:S(2)}) collective-permute-start(bf16[2,1792,128]{2,1,0:T(8,128)(2,1)} %get-tuple-element.51), channel_id=1, source_target_pairs={{0,1},{1,0},{2,3},{3,2},{4,5},{5,4},{6,7},{7,6},{8,9},{9,8},{10,11... | collective-permute-start | bytes 2752520 | tf_op jit(solution)/shard_map/ppermute | solution.py:30
  11.8 49.1 %all-to-all-start = ((bf16[16,8,1920]{2,1,0:T(8,128)(2,1)}), bf16[16,8,1920]{2,1,0:T(8,128)(2,1)S(1)}, u32[]{:S(2)}, u32[]{:S(2)}) async-start(bf16[16,8,1920]{2,1,0:T(8,128)(2,1)} %maximum_maximum_fusion), calls=%async_computation | async-start | bytes 983040 | tf_op jit(solution)/shard_map/all_to_all | solution.py:23
  28.8 8.6 %collective-permute-start.2 = (bf16[2,128,1792]{1,2,0:T(8,128)(2,1)}, bf16[2,128,1792]{1,2,0:T(8,128)(2,1)S(1)}, u32[]{:S(2)}, u32[]{:S(2)}) collective-permute-start(bf16[2,128,1792]{1,2,0:T(8,128)(2,1)} %get-tuple-element.47), channel_id=1, source_target_pairs={{0,1},{1,0},{2,3},{3,2},{4,5},{5,4},{6,7},{7,6},{8,9},{9,8},{10,11... | collective-permute-start | bytes 2752520 | tf_op jit(solution)/shard_map/ppermute | solution.py:30
  33.7 27.2 %collective-permute-start.1 = (bf16[2,1792,128]{2,1,0:T(8,128)(2,1)}, bf16[2,1792,128]{2,1,0:T(8,128)(2,1)S(1)}, u32[]{:S(2)}, u32[]{:S(2)}) collective-permute-start(bf16[2,1792,128]{2,1,0:T(8,128)(2,1)} %get-tuple-element.49), channel_id=1, source_target_pairs={{0,2},{1,3},{2,0},{3,1},{4,6},{5,7},{6,4},{7,5},{8,10},{9,11},{10,... | collective-permute-start | bytes 2752520 | tf_op jit(solution)/shard_map/ppermute | solution.py:30
  43.4 37.3 %collective-permute-start.3 = (bf16[2,128,1792]{2,1,0:T(8,128)(2,1)}, bf16[2,128,1792]{2,1,0:T(8,128)(2,1)}, u32[]{:S(2)}, u32[]{:S(2)}) collective-permute-start(bf16[2,128,1792]{2,1,0:T(8,128)(2,1)} %bitcast.209), channel_id=1, source_target_pairs={{0,2},{1,3},{2,0},{3,1},{4,6},{5,7},{6,4},{7,5},{8,10},{9,11},{10,... | collective-permute-start | bytes 2752520 | tf_op jit(solution)/shard_map/ppermute | solution.py:30
  60.9 25.9 %copy-start = (bf16[2,1792,128]{2,1,0:T(8,128)(2,1)}, bf16[2,1792,128]{2,1,0:T(8,128)(2,1)S(1)}, u32[]{:S(2)}) copy-start(bf16[2,1792,128]{2,1,0:T(8,128)(2,1)S(1)} %collective-permute-done.1) | copy-start | bytes 2752516
  63.0 17.7 %all-to-all-start.1 = ((bf16[4,64,1792]{2,1,0:T(8,128)(2,1)}), bf16[4,64,1792]{2,1,0:T(8,128)(2,1)S(1)}, u32[]{:S(2)}, u32[]{:S(2)}) async-start(bf16[4,64,1792]{2,1,0:T(8,128)(2,1)} %bitcast.26), calls=%async_computation.1 | async-start | bytes 1835008 | tf_op jit(solution)/shard_map/all_to_all | solution.py:23
  82.7 4.2 %collective-permute-start.4 = (f32[2,256,128]{1,2,0:T(8,128)S(1)}, f32[2,256,128]{1,2,0:T(8,128)S(1)}, u32[]{:S(2)}, u32[]{:S(2)}) collective-permute-start(f32[2,256,128]{1,2,0:T(8,128)S(1)} %pad_maximum_fusion.4), channel_id=1, source_target_pairs={{0,1},{1,0},{2,3},{3,2},{4,5},{5,4},{6,7},{7,6},{8,9},{9,8},{10,11... | collective-permute-start | bytes 786440 | tf_op jit(solution)/shard_map/ppermute | solution.py:30
  87.3 6.6 %collective-permute-start.5 = (f32[256,128]{0,1:T(8,128)S(1)}, f32[256,128]{0,1:T(8,128)S(1)}, u32[]{:S(2)}, u32[]{:S(2)}) collective-permute-start(f32[256,128]{0,1:T(8,128)S(1)} %convolution_add_fusion), channel_id=1, source_target_pairs={{0,2},{1,3},{2,0},{3,1},{4,6},{5,7},{6,4},{7,5},{8,10},{9,11},{10,... | collective-permute-start | bytes 393224 | tf_op jit(solution)/shard_map/ppermute | solution.py:30
  94.4 4.0 %collective-permute-start.6 = (bf16[256,128]{0,1:T(8,128)(2,1)S(1)}, bf16[256,128]{0,1:T(8,128)(2,1)S(1)}, u32[]{:S(2)}, u32[]{:S(2)}) collective-permute-start(bf16[256,128]{0,1:T(8,128)(2,1)S(1)} %multiply_convert_fusion.1), channel_id=1, source_target_pairs={{0,1},{1,0},{2,3},{3,2},{4,5},{5,4},{6,7},{7,6},{8,9},{9,8},{10,11... | collective-permute-start | bytes 196616 | tf_op jit(solution)/shard_map/ppermute | solution.py:30
  98.4 6.6 %collective-permute-start.7 = (bf16[2,256,128]{1,2,0:T(8,128)(2,1)S(1)}, bf16[2,256,128]{1,2,0:T(8,128)(2,1)S(1)}, u32[]{:S(2)}, u32[]{:S(2)}) collective-permute-start(bf16[2,256,128]{1,2,0:T(8,128)(2,1)S(1)} %pad_maximum_fusion.6), channel_id=1, source_target_pairs={{0,2},{1,3},{2,0},{3,1},{4,6},{5,7},{6,4},{7,5},{8,10},{9,11},{10,... | collective-permute-start | bytes 393224 | tf_op jit(solution)/shard_map/ppermute | solution.py:30
  106.7 26.9 %all-to-all-start.2 = ((bf16[4,64,1792]{2,1,0:T(8,128)(2,1)}), bf16[4,64,1792]{2,1,0:T(8,128)(2,1)S(1)}, u32[]{:S(2)}, u32[]{:S(2)}) async-start(bf16[4,64,1792]{2,1,0:T(8,128)(2,1)} %bitcast.203), calls=%async_computation.2 | async-start | bytes 1835008 | tf_op jit(solution)/shard_map/all_to_all | solution.py:23
  110.6 23.0 %collective-permute-start.8 = (bf16[8,7168]{1,0:T(8,128)(2,1)S(1)}, bf16[8,7168]{1,0:T(8,128)(2,1)S(1)}, u32[]{:S(2)}, u32[]{:S(2)}) collective-permute-start(bf16[8,7168]{1,0:T(8,128)(2,1)S(1)} %bitcast.214), channel_id=1, source_target_pairs={{0,8},{1,9},{2,10},{3,11},{4,12},{5,13},{6,14},{7,15},{8,0},{9,1},... | collective-permute-start | bytes 344072 | tf_op jit(solution)/shard_map/ppermute | solution.py:30
  134.2 48.2 %copy-start.6 = (f32[1,7168]{1,0:T(1,128)S(1)}, f32[1,7168]{1,0:T(1,128)}, u32[]{:S(2)}) copy-start(f32[1,7168]{1,0:T(1,128)} %param.7) | copy-start | bytes 86020
  163.2 19.0 %collective-permute-start.9 = (bf16[8,7168]{1,0:T(8,128)(2,1)S(1)}, bf16[8,7168]{1,0:T(8,128)(2,1)S(1)}, u32[]{:S(2)}, u32[]{:S(2)}) collective-permute-start(bf16[8,7168]{1,0:T(8,128)(2,1)S(1)} %add_convert_fusion.1), channel_id=1, source_target_pairs={{0,72},{1,73},{2,74},{3,75},{4,76},{5,77},{6,78},{7,79},{8,64},{9,... | collective-permute-start | bytes 344072 | tf_op jit(solution)/shard_map/ppermute | solution.py:40
  211.9 18.1 %copy-start.3 = (bf16[2,1792,128]{2,1,0:T(8,128)(2,1)S(1)}, bf16[2,1792,128]{2,1,0:T(8,128)(2,1)}, u32[]{:S(2)}) copy-start(bf16[2,1792,128]{2,1,0:T(8,128)(2,1)} %get-tuple-element.27) | copy-start | bytes 2752516
  212.3 18.2 %copy-start.1 = (bf16[2,1792,128]{2,1,0:T(8,128)(2,1)S(1)}, bf16[2,1792,128]{2,1,0:T(8,128)(2,1)}, u32[]{:S(2)}) copy-start(bf16[2,1792,128]{2,1,0:T(8,128)(2,1)} %copy-done) | copy-start | bytes 2752516
  230.9 4.2 %collective-permute-start.10 = (f32[2,256,128]{1,2,0:T(8,128)S(1)}, f32[2,256,128]{1,2,0:T(8,128)S(1)}, u32[]{:S(2)}, u32[]{:S(2)}) collective-permute-start(f32[2,256,128]{1,2,0:T(8,128)S(1)} %pad_maximum_fusion.5), channel_id=1, source_target_pairs={{0,1},{1,0},{2,3},{3,2},{4,5},{5,4},{6,7},{7,6},{8,9},{9,8},{10,11... | collective-permute-start | bytes 786440 | tf_op jit(solution)/shard_map/ppermute | solution.py:30
  235.6 6.6 %collective-permute-start.11 = (f32[256,128]{0,1:T(8,128)S(1)}, f32[256,128]{0,1:T(8,128)S(1)}, u32[]{:S(2)}, u32[]{:S(2)}) collective-permute-start(f32[256,128]{0,1:T(8,128)S(1)} %fusion.11), channel_id=1, source_target_pairs={{0,2},{1,3},{2,0},{3,1},{4,6},{5,7},{6,4},{7,5},{8,10},{9,11},{10,... | collective-permute-start | bytes 393224 | tf_op jit(solution)/shard_map/ppermute | solution.py:30
  242.7 4.0 %collective-permute-start.12 = (bf16[256,128]{0,1:T(8,128)(2,1)S(1)}, bf16[256,128]{0,1:T(8,128)(2,1)S(1)}, u32[]{:S(2)}, u32[]{:S(2)}) collective-permute-start(bf16[256,128]{0,1:T(8,128)(2,1)S(1)} %multiply_convert_fusion), channel_id=1, source_target_pairs={{0,1},{1,0},{2,3},{3,2},{4,5},{5,4},{6,7},{7,6},{8,9},{9,8},{10,11... | collective-permute-start | bytes 196616 | tf_op jit(solution)/shard_map/ppermute | solution.py:30
  246.7 6.6 %collective-permute-start.13 = (bf16[2,256,128]{1,2,0:T(8,128)(2,1)S(1)}, bf16[2,256,128]{1,2,0:T(8,128)(2,1)S(1)}, u32[]{:S(2)}, u32[]{:S(2)}) collective-permute-start(bf16[2,256,128]{1,2,0:T(8,128)(2,1)S(1)} %pad_maximum_fusion.7), channel_id=1, source_target_pairs={{0,2},{1,3},{2,0},{3,1},{4,6},{5,7},{6,4},{7,5},{8,10},{9,11},{10,... | collective-permute-start | bytes 393224 | tf_op jit(solution)/shard_map/ppermute | solution.py:30
  254.9 20.7 %all-to-all-start.6 = ((bf16[4,64,1792]{2,1,0:T(8,128)(2,1)}), bf16[4,64,1792]{2,1,0:T(8,128)(2,1)S(1)}, u32[]{:S(2)}, u32[]{:S(2)}) async-start(bf16[4,64,1792]{2,1,0:T(8,128)(2,1)} %bitcast.67), calls=%async_computation.6 | async-start | bytes 1835008 | tf_op jit(solution)/shard_map/all_to_all | solution.py:23
  258.4 17.2 %collective-permute-start.14 = (bf16[8,7168]{1,0:T(8,128)(2,1)S(1)}, bf16[8,7168]{1,0:T(8,128)(2,1)S(1)}, u32[]{:S(2)}, u32[]{:S(2)}) collective-permute-start(bf16[8,7168]{1,0:T(8,128)(2,1)S(1)} %collective-permute-done.9), channel_id=1, source_target_pairs={{0,8},{1,9},{2,10},{3,11},{4,12},{5,13},{6,14},{7,15},{8,0},{9,1},... | collective-permute-start | bytes 344072 | tf_op jit(solution)/shard_map/ppermute | solution.py:30
  307.4 19.0 %collective-permute-start.15 = (bf16[8,7168]{1,0:T(8,128)(2,1)S(1)}, bf16[8,7168]{1,0:T(8,128)(2,1)S(1)}, u32[]{:S(2)}, u32[]{:S(2)}) collective-permute-start(bf16[8,7168]{1,0:T(8,128)(2,1)S(1)} %add_convert_fusion), channel_id=1, source_target_pairs={{0,72},{1,73},{2,74},{3,75},{4,76},{5,77},{6,78},{7,79},{8,64},{9,... | collective-permute-start | bytes 344072 | tf_op jit(solution)/shard_map/ppermute | solution.py:40
  (3 other events, 18.2 us)

commit v9 on v8

--- a/solution.py
+++ b/solution.py
@@ -55,11 +55,13 @@
     return lax.dynamic_index_in_dim(value, index, axis, keepdims=False)
 
 
-def recut(quarters, chip, core):
+def from_sibling(quarters, core):
     near = swap(take(quarters, 1 - core, 1), 1)
-    both = jnp.stack([take(quarters, core, 1), near], axis=1)
-    far = swap(take(both, 1 - chip, 0), 2)
-    return take(both, chip, 0), far
+    return jnp.stack([take(quarters, core, 1), near], axis=1)
+
+
+def from_chip(both, chip):
+    return take(both, chip, 0), swap(take(both, 1 - chip, 0), 2)
 
 
 def tables(ids, gates, half, peers, rows_dev):
@@ -101,6 +103,8 @@
     same_row, same_place = groups(count)
     place = lax.axis_index("expert")
     core, chip, half = place % 2, place // 2 % 2, place // GROUP % HALVES
+    if passes % 2:
+        raise ValueError("odd passes")
     gain = norm_gain[0]
     current = hidden[0]
 
@@ -114,18 +118,21 @@
             facts = jnp.broadcast_to(facts[None], (PAIR, rows_dev, LANES))
             sent = jnp.concatenate([sent, facts], axis=2)
         sent = jnp.concatenate([sent] * (2 * HALVES))
-        if t == 0:
-            sent, w_up, w_down = lax.optimization_barrier((sent, w_up, w_down))
         arrived = exchange(sent, same_row)
         if t == 0:
-            up, up_far = recut(w_up[0].reshape(2, 2, part, HID_DEV), chip, core)
+            up_both = from_sibling(w_up[0].reshape(2, 2, part, HID_DEV), core)
+            w_down, up_both = lax.optimization_barrier((w_down, up_both))
+            up, up_far = from_chip(up_both, chip)
             down = w_down[0].reshape(HID_DEV, 2, 2, part).transpose(1, 2, 0, 3)
-            down, down_far = recut(down, chip, core)
+            down, down_far = from_chip(from_sibling(down, core), chip)
             arrived, up, up_far, down = lax.optimization_barrier((arrived, up, up_far, down))
             up = [up[0], up[1], up_far[0], up_far[1]]
             facts = arrived[:, :, part:].astype(jnp.float32).reshape(total, LANES)
             routes = facts[:, : 4 * passes * top].reshape(total, 4, passes, top)
             arrived = arrived[:, :, :part]
+        arrived = arrived.reshape(HALVES, block, part)
+        if t % 2 == 1:
+            arrived = jnp.concatenate([arrived[1:], arrived[:1]])
         rows = arrived.reshape(total, part)
 
         ids = routes[:, 0, t].astype(jnp.int32)
@@ -144,9 +151,7 @@
         active = jnp.concatenate([active, swap(active, 2)])
         active = jnp.concatenate([active[k] for k in range(PAIR)], axis=1)
         outputs = jnp.dot(active, down, preferred_element_type=jnp.float32).astype(jnp.bfloat16)
-        outputs, current = lax.optimization_barrier((outputs, current))
-        residual = swap(current, GROUP)
-        outputs, residual = lax.optimization_barrier((exchange(outputs, same_place), residual))
+        outputs = exchange(outputs, same_place)
         mixture = jnp.dot(
             weigher.T,
             outputs.astype(jnp.float32),
@@ -154,10 +159,12 @@
             preferred_element_type=jnp.float32,
         )
         mixture = mixture.astype(jnp.bfloat16).reshape(HALVES, GROUP, rows_dev, part)
-        mixture = jnp.concatenate([mixture[1], mixture[0]])
-        came = exchange(mixture, same_row).reshape(2 * HALVES, PAIR, rows_dev, part)
+        if t % 2 == 1:
+            mixture = jnp.concatenate([mixture[1:], mixture[:1]])
+        came = exchange(mixture.reshape(HALVES * GROUP, rows_dev, part), same_row)
+        came = came.reshape(2 * HALVES, PAIR, rows_dev, part)
         came = jnp.sum(came.astype(jnp.float32), axis=0).transpose(1, 0, 2)
-        updated = residual.astype(jnp.float32) + came.reshape(rows_dev, width)
+        updated = current.astype(jnp.float32) + came.reshape(rows_dev, width)
         current = next_section(updated.astype(jnp.bfloat16))
     return current[None]
 

time: 329 us -> 314 us (0.954)
  blocking collectives: 107 us -> 145 us
  starting transfers between devices: 84.8 us -> 58.8 us
  waiting for transfers between devices: 97.9 us -> 77.3 us
  other arithmetic: 13.4 us -> 8.17 us
    all_to_all x4 -> x6, blocking collectives: 107 us -> 145 us  [exchange(): lax.all_to_all(value, 'expert', split_axis=0, concat_axis=0, axis_index_g...]
    ppermute x14 -> x12, waiting for transfers between devices: 70.9 us -> 38.2 us  [swap(): return lax.ppermute(value, 'expert', [(i, i ^ bit) for i in range(count)])]
    ppermute x14 -> x12, starting transfers between devices: 49.5 us -> 30.8 us  [swap(): return lax.ppermute(value, 'expert', [(i, i ^ bit) for i in range(count)])]
    all_to_all x4 -> x2, waiting for transfers between devices: 0.01 us -> 12.2 us  [exchange(): lax.all_to_all(value, 'expert', split_axis=0, concat_axis=0, axis_index_g...]
    all_to_all x4 -> x2, starting transfers between devices: 24.2 us -> 16.8 us  [exchange(): lax.all_to_all(value, 'expert', split_axis=0, concat_axis=0, axis_index_g...]
  transfers between devices with their start and end apart: 20 -> 16, of which waited for: 14 -> 13; matrix products, arithmetic and copies ran while one was open for 5% -> 6% of each run, Pallas kernels for 0% -> 0%
where the time goes in v9:
time: 314 us; the launch traced here: 313 us
  blocking collectives  145 us (46%)
  waiting for transfers between devices  77.3 us (25%)
  starting transfers between devices  58.8 us (19%)
  local copies, waits for them, and re-layouts  14.8 us (5%)
  matrix products  8.52 us (3%)
  other arithmetic  8.17 us (3%)
    all_to_all x6, blocking collectives, exchange(): lax.all_to_all(value, 'expert', split_axis=0, concat_axis=0, axis_index_g...  145 us
    ppermute x12, waiting for transfers between devices, swap(): return lax.ppermute(value, 'expert', [(i, i ^ bit) for i in range(count)])  38.2 us
    ppermute x12, starting transfers between devices, swap(): return lax.ppermute(value, 'expert', [(i, i ^ bit) for i in range(count)])  30.8 us
    ppermute x2, waiting for transfers between devices, next_section(): return lax.ppermute(value, ('section', 'expert'), route)  26.9 us
    all_to_all x2, starting transfers between devices, exchange(): lax.all_to_all(value, 'expert', split_axis=0, concat_axis=0, axis_index_g...  16.8 us
    all_to_all x2, waiting for transfers between devices, exchange(): lax.all_to_all(value, 'expert', split_axis=0, concat_axis=0, axis_index_g...  12.2 us
    ppermute x2, starting transfers between devices, next_section(): return lax.ppermute(value, ('section', 'expert'), route)  11.1 us
  transfers between devices with their start and end apart: 16, of which 13 were waited for; matrix products, arithmetic and copies ran while one was open for 6% of the time, Pallas kernels for 0%

profile of v9, /device:TPU:7, one launch (start us, length us, event | category | flops | bytes accessed | tf_op | source)
XLA Modules:
  0.0 312.7 jit_solution(17350195724816847299)
XLA Ops:
  6.8 12.7 %all-to-all-start = ((bf16[16,8,1920]{2,1,0:T(8,128)(2,1)}), bf16[16,8,1920]{2,1,0:T(8,128)(2,1)S(1)}, u32[]{:S(2)}, u32[]{:S(2)}) async-start(bf16[16,8,1920]{2,1,0:T(8,128)(2,1)} %maximum_maximum_fusion), calls=%async_computation | async-start | bytes 983040 | tf_op jit(solution)/shard_map/all_to_all | solution.py:23
  21.8 3.9 %copy.52 = bf16[1,128,7168]{1,2,0:T(8,128)(2,1)} copy(bf16[1,128,7168]{2,1,0:T(8,128)(2,1)} %param.9) | data formatting | bytes 3670016 | tf_op jit(solution)/shard_map/optimization_barrier | solution.py:124
  25.7 2.8 dynamic-slice_bitcast_fusion
  31.9 3.5 %collective-permute-start.1 = (bf16[2,1792,128]{2,1,0:T(8,128)(2,1)}, bf16[2,1792,128]{2,1,0:T(8,128)(2,1)S(1)}, u32[]{:S(2)}, u32[]{:S(2)}) collective-permute-start(bf16[2,1792,128]{2,1,0:T(8,128)(2,1)} %get-tuple-element.31), channel_id=1, source_target_pairs={{0,2},{1,3},{2,0},{3,1},{4,6},{5,7},{6,4},{7,5},{8,10},{9,11},{10,... | collective-permute-start | bytes 2752520 | tf_op jit(solution)/shard_map/ppermute | solution.py:30
  42.8 15.9 %collective-permute-done.1 = bf16[2,1792,128]{2,1,0:T(8,128)(2,1)S(1)} collective-permute-done((bf16[2,1792,128]{2,1,0:T(8,128)(2,1)}, bf16[2,1792,128]{2,1,0:T(8,128)(2,1)S(1)}, u32[]{:S(2)}, u32[]{:S(2)}) %collective-permute-start.1) | collective-permute-done | bytes 917536 | tf_op jit(solution)/shard_map/ppermute | solution.py:30
  59.8 16.1 %all_to_all.62 = bf16[4,64,1792]{2,1,0:T(8,128)(2,1)S(1)} all-to-all(bf16[4,64,1792]{2,1,0:T(8,128)(2,1)S(1)} %bitcast.197), channel_id=1, replica_groups={{0,16,32,48},{1,17,33,49},{2,18,34,50},{3,19,35,51},{4,20,36,52},{5,21,..., dimensions={0} | all-to-all | bytes 1835008 | tf_op jit(solution)/shard_map/all_to_all | solution.py:23
  79.4 2.7 collective-permute-start.4
  85.7 4.7 %collective-permute-done.5 = f32[256,128]{0,1:T(8,128)S(1)} collective-permute-done((f32[256,128]{0,1:T(8,128)S(1)}, f32[256,128]{0,1:T(8,128)S(1)}, u32[]{:S(2)}, u32[]{:S(2)}) %collective-permute-start.5) | collective-permute-done | bytes 131104 | tf_op jit(solution)/shard_map/ppermute | solution.py:30
  90.9 3.1 collective-permute-start.6
  98.1 3.3 %collective-permute-done.7 = bf16[2,256,128]{1,2,0:T(8,128)(2,1)S(1)} collective-permute-done((bf16[2,256,128]{1,2,0:T(8,128)(2,1)S(1)}, bf16[2,256,128]{1,2,0:T(8,128)(2,1)S(1)}, u32[]{:S(2)}, u32[]{:S(2)}) %collective-permute-start.7) | collective-permute-done | bytes 131104 | tf_op jit(solution)/shard_map/ppermute | solution.py:30
  103.1 4.2 %all-to-all-start.2 = ((bf16[4,64,1792]{2,1,0:T(8,128)(2,1)}), bf16[4,64,1792]{2,1,0:T(8,128)(2,1)S(1)}, u32[]{:S(2)}, u32[]{:S(2)}) async-start(bf16[4,64,1792]{2,1,0:T(8,128)(2,1)} %bitcast.195), calls=%async_computation.2 | async-start | bytes 1835008 | tf_op jit(solution)/shard_map/all_to_all | solution.py:23
  107.4 12.2 %all-to-all-done.2 = bf16[4,64,1792]{2,1,0:T(8,128)(2,1)S(1)} async-done(((bf16[4,64,1792]{2,1,0:T(8,128)(2,1)}), bf16[4,64,1792]{2,1,0:T(8,128)(2,1)S(1)}, u32[]{:S(2)}, u32[]{:S(2)}) %all-to-all-start.2) | async-done | bytes 917536 | tf_op jit(solution)/shard_map/all_to_all | solution.py:23
  120.2 35.4 %all_to_all.63 = bf16[16,8,1792]{2,1,0:T(8,128)(2,1)S(1)} all-to-all(bf16[16,8,1792]{2,1,0:T(8,128)(2,1)S(1)} %fusion.2), channel_id=1, replica_groups={{0,1,2,3,4,5,6,7,8,9,10,11,12,13,14,15},{16,17,18,19,20,21,22,23,24,25,..., dimensions={0} | all-to-all | bytes 917504 | tf_op jit(solution)/shard_map/all_to_all | solution.py:23
  155.7 5.4 %collective-permute-start.8 = (bf16[8,7168]{1,0:T(8,128)(2,1)S(1)}, bf16[8,7168]{1,0:T(8,128)(2,1)S(1)}, u32[]{:S(2)}, u32[]{:S(2)}) collective-permute-start(bf16[8,7168]{1,0:T(8,128)(2,1)S(1)} %fusion.54), channel_id=1, source_target_pairs={{0,72},{1,73},{2,74},{3,75},{4,76},{5,77},{6,78},{7,79},{8,64},{9,... | collective-permute-start | bytes 344072 | tf_op jit(solution)/shard_map/ppermute | solution.py:40
  161.2 13.6 %collective-permute-done.8 = bf16[8,7168]{1,0:T(8,128)(2,1)S(1)} collective-permute-done((bf16[8,7168]{1,0:T(8,128)(2,1)S(1)}, bf16[8,7168]{1,0:T(8,128)(2,1)S(1)}, u32[]{:S(2)}, u32[]{:S(2)}) %collective-permute-start.8) | collective-permute-done | bytes 114720 | tf_op jit(solution)/shard_map/ppermute | solution.py:40
  175.1 29.3 %all_to_all.64 = bf16[16,8,1792]{2,1,0:T(8,128)(2,1)S(1)} all-to-all(bf16[16,8,1792]{2,1,0:T(8,128)(2,1)S(1)} %pad_maximum_fusion.2), channel_id=1, replica_groups={{0,1,2,3,4,5,6,7,8,9,10,11,12,13,14,15},{16,17,18,19,20,21,22,23,24,25,..., dimensions={0} | all-to-all | bytes 917504 | tf_op jit(solution)/shard_map/all_to_all | solution.py:23
  205.0 16.6 %all_to_all.65 = bf16[4,64,1792]{2,1,0:T(8,128)(2,1)S(1)} all-to-all(bf16[4,64,1792]{2,1,0:T(8,128)(2,1)S(1)} %bitcast.198), channel_id=1, replica_groups={{0,16,32,48},{1,17,33,49},{2,18,34,50},{3,19,35,51},{4,20,36,52},{5,21,..., dimensions={0} | all-to-all | bytes 1835008 | tf_op jit(solution)/shard_map/all_to_all | solution.py:23
  229.4 3.9 %collective-permute-done.10 = f32[256,128]{0,1:T(8,128)S(1)} collective-permute-done((f32[256,128]{0,1:T(8,128)S(1)}, f32[256,128]{0,1:T(8,128)S(1)}, u32[]{:S(2)}, u32[]{:S(2)}) %collective-permute-start.10) | collective-permute-done | bytes 131104 | tf_op jit(solution)/shard_map/ppermute | solution.py:30
  233.7 3.1 collective-permute-start.11
  240.5 3.9 %collective-permute-done.12 = bf16[2,256,128]{1,2,0:T(8,128)(2,1)S(1)} collective-permute-done((bf16[2,256,128]{1,2,0:T(8,128)(2,1)S(1)}, bf16[2,256,128]{1,2,0:T(8,128)(2,1)S(1)}, u32[]{:S(2)}, u32[]{:S(2)}) %collective-permute-start.12) | collective-permute-done | bytes 131104 | tf_op jit(solution)/shard_map/ppermute | solution.py:30
  245.1 15.0 %all_to_all.66 = bf16[4,64,1792]{2,1,0:T(8,128)(2,1)S(1)} all-to-all(bf16[4,64,1792]{2,1,0:T(8,128)(2,1)S(1)} %bitcast.196), channel_id=1, replica_groups={{0,16,32,48},{1,17,33,49},{2,18,34,50},{3,19,35,51},{4,20,36,52},{5,21,..., dimensions={0} | all-to-all | bytes 1835008 | tf_op jit(solution)/shard_map/all_to_all | solution.py:23
  260.7 32.2 %all_to_all.67 = bf16[16,8,1792]{2,1,0:T(8,128)(2,1)S(1)} all-to-all(bf16[16,8,1792]{2,1,0:T(8,128)(2,1)S(1)} %bitcast.199), channel_id=1, replica_groups={{0,1,2,3,4,5,6,7,8,9,10,11,12,13,14,15},{16,17,18,19,20,21,22,23,24,25,..., dimensions={0} | all-to-all | bytes 917504 | tf_op jit(solution)/shard_map/all_to_all | solution.py:23
  293.0 5.7 %collective-permute-start.13 = (bf16[8,7168]{1,0:T(8,128)(2,1)S(1)}, bf16[8,7168]{1,0:T(8,128)(2,1)S(1)}, u32[]{:S(2)}, u32[]{:S(2)}) collective-permute-start(bf16[8,7168]{1,0:T(8,128)(2,1)S(1)} %fusion.52), channel_id=1, source_target_pairs={{0,72},{1,73},{2,74},{3,75},{4,76},{5,77},{6,78},{7,79},{8,64},{9,... | collective-permute-start | bytes 344072 | tf_op jit(solution)/shard_map/ppermute | solution.py:40
  298.7 13.3 %collective-permute-done.13 = bf16[8,7168]{1,0:T(8,128)(2,1)S(1)} collective-permute-done((bf16[8,7168]{1,0:T(8,128)(2,1)S(1)}, bf16[8,7168]{1,0:T(8,128)(2,1)S(1)}, u32[]{:S(2)}, u32[]{:S(2)}) %collective-permute-start.13) | collective-permute-done | bytes 114720 | tf_op jit(solution)/shard_map/ppermute | solution.py:40
  (101 shorter events, 49.7 us)
Async XLA Ops:
  0.0 4.3 %copy-start.8 = (f32[1,2,8,2]{2,3,1,0:T(2,128)S(1)}, f32[1,2,8,2]{2,3,1,0:T(2,128)}, u32[]{:S(2)}) copy-start(f32[1,2,8,2]{2,3,1,0:T(2,128)} %param.11) | copy-start | bytes 388
  0.0 4.3 %copy-start.7 = (s32[1,2,8,2]{2,3,1,0:T(2,128)S(1)}, s32[1,2,8,2]{2,3,1,0:T(2,128)}, u32[]{:S(2)}) copy-start(s32[1,2,8,2]{2,3,1,0:T(2,128)} %param.10) | copy-start | bytes 388
  0.0 4.3 %copy-start.4 = (bf16[1,8,7168]{2,1,0:T(8,128)(2,1)S(1)}, bf16[1,8,7168]{2,1,0:T(8,128)(2,1)}, u32[]{:S(2)}) copy-start(bf16[1,8,7168]{2,1,0:T(8,128)(2,1)} %param.6) | copy-start | bytes 344068
  0.0 5.1 %copy-start.6 = (f32[1,7168]{1,0:T(1,128)S(1)}, f32[1,7168]{1,0:T(1,128)}, u32[]{:S(2)}) copy-start(f32[1,7168]{1,0:T(1,128)} %param.7) | copy-start | bytes 86020
  1.7 17.8 %collective-permute-start = (bf16[2,1792,128]{2,1,0:T(8,128)(2,1)S(1)}, bf16[2,1792,128]{2,1,0:T(8,128)(2,1)S(1)}, u32[]{:S(2)}, u32[]{:S(2)}) collective-permute-start(bf16[2,1792,128]{2,1,0:T(8,128)(2,1)S(1)} %get-tuple-element.34), channel_id=1, source_target_pairs={{0,1},{1,0},{2,3},{3,2},{4,5},{5,4},{6,7},{7,6},{8,9},{9,8},{10,11... | collective-permute-start | bytes 2752520 | tf_op jit(solution)/shard_map/ppermute | solution.py:30
  6.8 51.8 %all-to-all-start = ((bf16[16,8,1920]{2,1,0:T(8,128)(2,1)}), bf16[16,8,1920]{2,1,0:T(8,128)(2,1)S(1)}, u32[]{:S(2)}, u32[]{:S(2)}) async-start(bf16[16,8,1920]{2,1,0:T(8,128)(2,1)} %maximum_maximum_fusion), calls=%async_computation | async-start | bytes 983040 | tf_op jit(solution)/shard_map/all_to_all | solution.py:23
  28.5 7.1 %collective-permute-start.2 = (bf16[2,128,1792]{1,2,0:T(8,128)(2,1)}, bf16[2,128,1792]{1,2,0:T(8,128)(2,1)}, u32[]{:S(2)}, u32[]{:S(2)}) collective-permute-start(bf16[2,128,1792]{1,2,0:T(8,128)(2,1)} %get-tuple-element.29), channel_id=1, source_target_pairs={{0,1},{1,0},{2,3},{3,2},{4,5},{5,4},{6,7},{7,6},{8,9},{9,8},{10,11... | collective-permute-start | bytes 2752520 | tf_op jit(solution)/shard_map/ppermute | solution.py:30
  31.9 26.8 %collective-permute-start.1 = (bf16[2,1792,128]{2,1,0:T(8,128)(2,1)}, bf16[2,1792,128]{2,1,0:T(8,128)(2,1)S(1)}, u32[]{:S(2)}, u32[]{:S(2)}) collective-permute-start(bf16[2,1792,128]{2,1,0:T(8,128)(2,1)} %get-tuple-element.31), channel_id=1, source_target_pairs={{0,2},{1,3},{2,0},{3,1},{4,6},{5,7},{6,4},{7,5},{8,10},{9,11},{10,... | collective-permute-start | bytes 2752520 | tf_op jit(solution)/shard_map/ppermute | solution.py:30
  40.9 37.6 %collective-permute-start.3 = (bf16[2,128,1792]{2,1,0:T(8,128)(2,1)}, bf16[2,128,1792]{2,1,0:T(8,128)(2,1)}, u32[]{:S(2)}, u32[]{:S(2)}) collective-permute-start(bf16[2,128,1792]{2,1,0:T(8,128)(2,1)} %bitcast.206), channel_id=1, source_target_pairs={{0,2},{1,3},{2,0},{3,1},{4,6},{5,7},{6,4},{7,5},{8,10},{9,11},{10,... | collective-permute-start | bytes 2752520 | tf_op jit(solution)/shard_map/ppermute | solution.py:30
  58.7 24.6 %copy-start = (bf16[2,1792,128]{2,1,0:T(8,128)(2,1)}, bf16[2,1792,128]{2,1,0:T(8,128)(2,1)S(1)}, u32[]{:S(2)}) copy-start(bf16[2,1792,128]{2,1,0:T(8,128)(2,1)S(1)} %collective-permute-done.1) | copy-start | bytes 2752516
  58.7 19.7 %copy-start.2 = (bf16[2,1792,128]{2,1,0:T(8,128)(2,1)S(1)}, bf16[2,1792,128]{2,1,0:T(8,128)(2,1)}, u32[]{:S(2)}) copy-start(bf16[2,1792,128]{2,1,0:T(8,128)(2,1)} %get-tuple-element.17) | copy-start | bytes 2752516
  79.4 3.9 %collective-permute-start.4 = (f32[2,256,128]{1,2,0:T(8,128)S(1)}, f32[2,256,128]{1,2,0:T(8,128)S(1)}, u32[]{:S(2)}, u32[]{:S(2)}) collective-permute-start(f32[2,256,128]{1,2,0:T(8,128)S(1)} %pad_maximum_fusion.5), channel_id=1, source_target_pairs={{0,1},{1,0},{2,3},{3,2},{4,5},{5,4},{6,7},{7,6},{8,9},{9,8},{10,11... | collective-permute-start | bytes 786440 | tf_op jit(solution)/shard_map/ppermute | solution.py:30
  83.8 6.6 %collective-permute-start.5 = (f32[256,128]{0,1:T(8,128)S(1)}, f32[256,128]{0,1:T(8,128)S(1)}, u32[]{:S(2)}, u32[]{:S(2)}) collective-permute-start(f32[256,128]{0,1:T(8,128)S(1)} %convolution_add_fusion), channel_id=1, source_target_pairs={{0,2},{1,3},{2,0},{3,1},{4,6},{5,7},{6,4},{7,5},{8,10},{9,11},{10,... | collective-permute-start | bytes 393224 | tf_op jit(solution)/shard_map/ppermute | solution.py:30
  90.9 4.0 %collective-permute-start.6 = (bf16[256,128]{0,1:T(8,128)(2,1)S(1)}, bf16[256,128]{0,1:T(8,128)(2,1)S(1)}, u32[]{:S(2)}, u32[]{:S(2)}) collective-permute-start(bf16[256,128]{0,1:T(8,128)(2,1)S(1)} %multiply_convert_fusion.2), channel_id=1, source_target_pairs={{0,1},{1,0},{2,3},{3,2},{4,5},{5,4},{6,7},{7,6},{8,9},{9,8},{10,11... | collective-permute-start | bytes 196616 | tf_op jit(solution)/shard_map/ppermute | solution.py:30
  94.9 6.6 %collective-permute-start.7 = (bf16[2,256,128]{1,2,0:T(8,128)(2,1)S(1)}, bf16[2,256,128]{1,2,0:T(8,128)(2,1)S(1)}, u32[]{:S(2)}, u32[]{:S(2)}) collective-permute-start(bf16[2,256,128]{1,2,0:T(8,128)(2,1)S(1)} %pad_maximum_fusion.7), channel_id=1, source_target_pairs={{0,2},{1,3},{2,0},{3,1},{4,6},{5,7},{6,4},{7,5},{8,10},{9,11},{10,... | collective-permute-start | bytes 393224 | tf_op jit(solution)/shard_map/ppermute | solution.py:30
  103.1 16.5 %all-to-all-start.2 = ((bf16[4,64,1792]{2,1,0:T(8,128)(2,1)}), bf16[4,64,1792]{2,1,0:T(8,128)(2,1)S(1)}, u32[]{:S(2)}, u32[]{:S(2)}) async-start(bf16[4,64,1792]{2,1,0:T(8,128)(2,1)} %bitcast.195), calls=%async_computation.2 | async-start | bytes 1835008 | tf_op jit(solution)/shard_map/all_to_all | solution.py:23
  155.7 19.0 %collective-permute-start.8 = (bf16[8,7168]{1,0:T(8,128)(2,1)S(1)}, bf16[8,7168]{1,0:T(8,128)(2,1)S(1)}, u32[]{:S(2)}, u32[]{:S(2)}) collective-permute-start(bf16[8,7168]{1,0:T(8,128)(2,1)S(1)} %fusion.54), channel_id=1, source_target_pairs={{0,72},{1,73},{2,74},{3,75},{4,76},{5,77},{6,78},{7,79},{8,64},{9,... | collective-permute-start | bytes 344072 | tf_op jit(solution)/shard_map/ppermute | solution.py:40
  204.5 17.0 %copy-start.3 = (bf16[2,1792,128]{2,1,0:T(8,128)(2,1)S(1)}, bf16[2,1792,128]{2,1,0:T(8,128)(2,1)}, u32[]{:S(2)}) copy-start(bf16[2,1792,128]{2,1,0:T(8,128)(2,1)} %get-tuple-element.17) | copy-start | bytes 2752516
  205.0 17.1 %copy-start.1 = (bf16[2,1792,128]{2,1,0:T(8,128)(2,1)S(1)}, bf16[2,1792,128]{2,1,0:T(8,128)(2,1)}, u32[]{:S(2)}) copy-start(bf16[2,1792,128]{2,1,0:T(8,128)(2,1)} %copy-done) | copy-start | bytes 2752516
  222.5 3.6 %collective-permute-start.9 = (f32[2,256,128]{1,2,0:T(8,128)S(1)}, f32[2,256,128]{1,2,0:T(8,128)S(1)}, u32[]{:S(2)}, u32[]{:S(2)}) collective-permute-start(f32[2,256,128]{1,2,0:T(8,128)S(1)} %pad_maximum_fusion.6), channel_id=1, source_target_pairs={{0,1},{1,0},{2,3},{3,2},{4,5},{5,4},{6,7},{7,6},{8,9},{9,8},{10,11... | collective-permute-start | bytes 786440 | tf_op jit(solution)/shard_map/ppermute | solution.py:30
  226.6 6.6 %collective-permute-start.10 = (f32[256,128]{0,1:T(8,128)S(1)}, f32[256,128]{0,1:T(8,128)S(1)}, u32[]{:S(2)}, u32[]{:S(2)}) collective-permute-start(f32[256,128]{0,1:T(8,128)S(1)} %fusion.9), channel_id=1, source_target_pairs={{0,2},{1,3},{2,0},{3,1},{4,6},{5,7},{6,4},{7,5},{8,10},{9,11},{10,... | collective-permute-start | bytes 393224 | tf_op jit(solution)/shard_map/ppermute | solution.py:30
  233.7 4.0 %collective-permute-start.11 = (bf16[256,128]{0,1:T(8,128)(2,1)S(1)}, bf16[256,128]{0,1:T(8,128)(2,1)S(1)}, u32[]{:S(2)}, u32[]{:S(2)}) collective-permute-start(bf16[256,128]{0,1:T(8,128)(2,1)S(1)} %multiply_convert_fusion.1), channel_id=1, source_target_pairs={{0,1},{1,0},{2,3},{3,2},{4,5},{5,4},{6,7},{7,6},{8,9},{9,8},{10,11... | collective-permute-start | bytes 196616 | tf_op jit(solution)/shard_map/ppermute | solution.py:30
  237.7 6.6 %collective-permute-start.12 = (bf16[2,256,128]{1,2,0:T(8,128)(2,1)S(1)}, bf16[2,256,128]{1,2,0:T(8,128)(2,1)S(1)}, u32[]{:S(2)}, u32[]{:S(2)}) collective-permute-start(bf16[2,256,128]{1,2,0:T(8,128)(2,1)S(1)} %pad_maximum_fusion.8), channel_id=1, source_target_pairs={{0,2},{1,3},{2,0},{3,1},{4,6},{5,7},{6,4},{7,5},{8,10},{9,11},{10,... | collective-permute-start | bytes 393224 | tf_op jit(solution)/shard_map/ppermute | solution.py:30
  293.0 19.0 %collective-permute-start.13 = (bf16[8,7168]{1,0:T(8,128)(2,1)S(1)}, bf16[8,7168]{1,0:T(8,128)(2,1)S(1)}, u32[]{:S(2)}, u32[]{:S(2)}) collective-permute-start(bf16[8,7168]{1,0:T(8,128)(2,1)S(1)} %fusion.52), channel_id=1, source_target_pairs={{0,72},{1,73},{2,74},{3,75},{4,76},{5,77},{6,78},{7,79},{8,64},{9,... | collective-permute-start | bytes 344072 | tf_op jit(solution)/shard_map/ppermute | solution.py:40
  (1 other events, 0.9 us)

commit v10 on v9

--- a/solution.py
+++ b/solution.py
@@ -55,13 +55,12 @@
     return lax.dynamic_index_in_dim(value, index, axis, keepdims=False)
 
 
-def from_sibling(quarters, core):
-    near = swap(take(quarters, 1 - core, 1), 1)
-    return jnp.stack([take(quarters, core, 1), near], axis=1)
+def from_sibling(keep, give):
+    return jnp.stack([keep, swap(give, 1)], axis=1)
 
 
-def from_chip(both, chip):
-    return take(both, chip, 0), swap(take(both, 1 - chip, 0), 2)
+def for_chip(both, chip):
+    return take(both, chip, 0), take(both, 1 - chip, 0)
 
 
 def tables(ids, gates, half, peers, rows_dev):
@@ -120,11 +119,16 @@
         sent = jnp.concatenate([sent] * (2 * HALVES))
         arrived = exchange(sent, same_row)
         if t == 0:
-            up_both = from_sibling(w_up[0].reshape(2, 2, part, HID_DEV), core)
-            w_down, up_both = lax.optimization_barrier((w_down, up_both))
-            up, up_far = from_chip(up_both, chip)
-            down = w_down[0].reshape(HID_DEV, 2, 2, part).transpose(1, 2, 0, 3)
-            down, down_far = from_chip(from_sibling(down, core), chip)
+            quarters = w_up[0].reshape(2, 2, part, HID_DEV)
+            up_both = from_sibling(take(quarters, core, 1), take(quarters, 1 - core, 1))
+            up, give = for_chip(up_both, chip)
+            core, give = lax.optimization_barrier((core, give))
+            up_far = swap(give, 2)
+            quarters = [w_down[0, :, k * part : (k + 1) * part] for k in range(PAIR)]
+            even, odd = jnp.stack(quarters[0::2]), jnp.stack(quarters[1::2])
+            keep, give = jnp.where(core == 0, even, odd), jnp.where(core == 0, odd, even)
+            down, give = for_chip(from_sibling(keep, give), chip)
+            down_far = swap(give, 2)
             arrived, up, up_far, down = lax.optimization_barrier((arrived, up, up_far, down))
             up = [up[0], up[1], up_far[0], up_far[1]]
             facts = arrived[:, :, part:].astype(jnp.float32).reshape(total, LANES)

time: 314 us -> 315 us (level)
  local copies, waits for them, and re-layouts: 14.8 us -> 6.06 us
  other arithmetic: 8.17 us -> 13 us
    squeeze x0 -> x2, other arithmetic: none -> 4.57 us  [take(): return lax.dynamic_index_in_dim(value, index, axis, keepdims=False)]
    dynamic_slice x3 -> x0, local copies, waits for them, and re-layouts: 4.41 us -> none  [take(): return lax.dynamic_index_in_dim(value, index, axis, keepdims=False)]
    select_n x0 -> x2, other arithmetic: none -> 4.22 us  [the longest x1 2.9 us: body(): jnp.where(core == 0, odd, even)]
    optimization_barrier x1 -> x0, local copies, waits for them, and re-layouts: 3.9 us -> none  [body(): w_down, up_both = lax.optimization_barrier((w_down, up_both))]
    another operation x2 -> x0, other arithmetic: 3.89 us -> none  [from_sibling(): return jnp.stack([take(quarters, core, 1), near], axis=1)]
  transfers between devices with their start and end apart: 16 -> 16, of which waited for: 13 -> 13; matrix products, arithmetic and copies ran while one was open for 6% -> 5% of each run, Pallas kernels for 0% -> 0%
where the time goes in v10:
time: 315 us; the launch traced here: 314 us
  blocking collectives  147 us (47%)
  waiting for transfers between devices  79.6 us (25%)
  starting transfers between devices  58.8 us (19%)
  other arithmetic  13 us (4%)
  matrix products  8.49 us (3%)
  local copies, waits for them, and re-layouts  6.06 us (2%)
    all_to_all x6, blocking collectives, exchange(): lax.all_to_all(value, 'expert', split_axis=0, concat_axis=0, axis_index_g...  147 us
    ppermute x12, waiting for transfers between devices, swap(): return lax.ppermute(value, 'expert', [(i, i ^ bit) for i in range(count)])  40.5 us
    ppermute x12, starting transfers between devices, swap(): return lax.ppermute(value, 'expert', [(i, i ^ bit) for i in range(count)])  30.9 us
    ppermute x2, waiting for transfers between devices, next_section(): return lax.ppermute(value, ('section', 'expert'), route)  27 us
    all_to_all x2, starting transfers between devices, exchange(): lax.all_to_all(value, 'expert', split_axis=0, concat_axis=0, axis_index_g...  16.8 us
    all_to_all x2, waiting for transfers between devices, exchange(): lax.all_to_all(value, 'expert', split_axis=0, concat_axis=0, axis_index_g...  12.2 us
    ppermute x2, starting transfers between devices, next_section(): return lax.ppermute(value, ('section', 'expert'), route)  11.1 us
  transfers between devices with their start and end apart: 16, of which 13 were waited for; matrix products, arithmetic and copies ran while one was open for 5% of the time, Pallas kernels for 0%

profile of v10, /device:TPU:7, one launch (start us, length us, event | category | flops | bytes accessed | tf_op | source)
XLA Modules:
  0.0 313.7 jit_solution(1874874002056174588)
XLA Ops:
  7.9 12.7 %all-to-all-start = ((bf16[16,8,1920]{2,1,0:T(8,128)(2,1)}), bf16[16,8,1920]{2,1,0:T(8,128)(2,1)S(1)}, u32[]{:S(2)}, u32[]{:S(2)}) async-start(bf16[16,8,1920]{2,1,0:T(8,128)(2,1)} %maximum_maximum_fusion), calls=%async_computation | async-start | bytes 983040 | tf_op jit(solution)/shard_map/all_to_all | solution.py:23
  24.8 2.9 maximum_select_fusion.1
  29.8 3.5 %collective-permute-start.1 = (bf16[2,1792,128]{2,1,0:T(8,128)(2,1)}, bf16[2,1792,128]{2,1,0:T(8,128)(2,1)S(1)}, u32[]{:S(2)}, u32[]{:S(2)}) collective-permute-start(bf16[2,1792,128]{2,1,0:T(8,128)(2,1)} %get-tuple-element.13), channel_id=1, source_target_pairs={{0,2},{1,3},{2,0},{3,1},{4,6},{5,7},{6,4},{7,5},{8,10},{9,11},{10,... | collective-permute-start | bytes 2752520 | tf_op jit(solution)/shard_map/ppermute | solution.py:30
  39.0 18.0 %collective-permute-done.1 = bf16[2,1792,128]{2,1,0:T(8,128)(2,1)S(1)} collective-permute-done((bf16[2,1792,128]{2,1,0:T(8,128)(2,1)}, bf16[2,1792,128]{2,1,0:T(8,128)(2,1)S(1)}, u32[]{:S(2)}, u32[]{:S(2)}) %collective-permute-start.1) | collective-permute-done | bytes 917536 | tf_op jit(solution)/shard_map/ppermute | solution.py:30
  58.1 16.0 %all_to_all.62 = bf16[4,64,1792]{2,1,0:T(8,128)(2,1)S(1)} all-to-all(bf16[4,64,1792]{2,1,0:T(8,128)(2,1)S(1)} %bitcast.200), channel_id=1, replica_groups={{0,16,32,48},{1,17,33,49},{2,18,34,50},{3,19,35,51},{4,20,36,52},{5,21,..., dimensions={0} | all-to-all | bytes 1835008 | tf_op jit(solution)/shard_map/all_to_all | solution.py:23
  84.0 4.7 %collective-permute-done.5 = f32[256,128]{0,1:T(8,128)S(1)} collective-permute-done((f32[256,128]{0,1:T(8,128)S(1)}, f32[256,128]{0,1:T(8,128)S(1)}, u32[]{:S(2)}, u32[]{:S(2)}) %collective-permute-start.5) | collective-permute-done | bytes 131104 | tf_op jit(solution)/shard_map/ppermute | solution.py:30
  89.1 3.1 collective-permute-start.6
  96.4 3.3 %collective-permute-done.7 = bf16[2,256,128]{1,2,0:T(8,128)(2,1)S(1)} collective-permute-done((bf16[2,256,128]{1,2,0:T(8,128)(2,1)S(1)}, bf16[2,256,128]{1,2,0:T(8,128)(2,1)S(1)}, u32[]{:S(2)}, u32[]{:S(2)}) %collective-permute-start.7) | collective-permute-done | bytes 131104 | tf_op jit(solution)/shard_map/ppermute | solution.py:30
  101.4 4.2 %all-to-all-start.2 = ((bf16[4,64,1792]{2,1,0:T(8,128)(2,1)}), bf16[4,64,1792]{2,1,0:T(8,128)(2,1)S(1)}, u32[]{:S(2)}, u32[]{:S(2)}) async-start(bf16[4,64,1792]{2,1,0:T(8,128)(2,1)} %bitcast.198), calls=%async_computation.2 | async-start | bytes 1835008 | tf_op jit(solution)/shard_map/all_to_all | solution.py:23
  105.7 12.2 %all-to-all-done.2 = bf16[4,64,1792]{2,1,0:T(8,128)(2,1)S(1)} async-done(((bf16[4,64,1792]{2,1,0:T(8,128)(2,1)}), bf16[4,64,1792]{2,1,0:T(8,128)(2,1)S(1)}, u32[]{:S(2)}, u32[]{:S(2)}) %all-to-all-start.2) | async-done | bytes 917536 | tf_op jit(solution)/shard_map/all_to_all | solution.py:23
  118.5 38.2 %all_to_all.63 = bf16[16,8,1792]{2,1,0:T(8,128)(2,1)S(1)} all-to-all(bf16[16,8,1792]{2,1,0:T(8,128)(2,1)S(1)} %fusion.2), channel_id=1, replica_groups={{0,1,2,3,4,5,6,7,8,9,10,11,12,13,14,15},{16,17,18,19,20,21,22,23,24,25,..., dimensions={0} | all-to-all | bytes 917504 | tf_op jit(solution)/shard_map/all_to_all | solution.py:23
  156.8 5.4 %collective-permute-start.8 = (bf16[8,7168]{1,0:T(8,128)(2,1)S(1)}, bf16[8,7168]{1,0:T(8,128)(2,1)S(1)}, u32[]{:S(2)}, u32[]{:S(2)}) collective-permute-start(bf16[8,7168]{1,0:T(8,128)(2,1)S(1)} %fusion.60), channel_id=1, source_target_pairs={{0,72},{1,73},{2,74},{3,75},{4,76},{5,77},{6,78},{7,79},{8,64},{9,... | collective-permute-start | bytes 344072 | tf_op jit(solution)/shard_map/ppermute | solution.py:40
  162.2 13.6 %collective-permute-done.8 = bf16[8,7168]{1,0:T(8,128)(2,1)S(1)} collective-permute-done((bf16[8,7168]{1,0:T(8,128)(2,1)S(1)}, bf16[8,7168]{1,0:T(8,128)(2,1)S(1)}, u32[]{:S(2)}, u32[]{:S(2)}) %collective-permute-start.8) | collective-permute-done | bytes 114720 | tf_op jit(solution)/shard_map/ppermute | solution.py:40
  176.2 29.3 %all_to_all.64 = bf16[16,8,1792]{2,1,0:T(8,128)(2,1)S(1)} all-to-all(bf16[16,8,1792]{2,1,0:T(8,128)(2,1)S(1)} %pad_maximum_fusion.1), channel_id=1, replica_groups={{0,1,2,3,4,5,6,7,8,9,10,11,12,13,14,15},{16,17,18,19,20,21,22,23,24,25,..., dimensions={0} | all-to-all | bytes 917504 | tf_op jit(solution)/shard_map/all_to_all | solution.py:23
  206.0 16.6 %all_to_all.65 = bf16[4,64,1792]{2,1,0:T(8,128)(2,1)S(1)} all-to-all(bf16[4,64,1792]{2,1,0:T(8,128)(2,1)S(1)} %bitcast.201), channel_id=1, replica_groups={{0,16,32,48},{1,17,33,49},{2,18,34,50},{3,19,35,51},{4,20,36,52},{5,21,..., dimensions={0} | all-to-all | bytes 1835008 | tf_op jit(solution)/shard_map/all_to_all | solution.py:23
  227.7 2.7 collective-permute-start.10
  230.4 3.9 %collective-permute-done.10 = f32[256,128]{0,1:T(8,128)S(1)} collective-permute-done((f32[256,128]{0,1:T(8,128)S(1)}, f32[256,128]{0,1:T(8,128)S(1)}, u32[]{:S(2)}, u32[]{:S(2)}) %collective-permute-start.10) | collective-permute-done | bytes 131104 | tf_op jit(solution)/shard_map/ppermute | solution.py:30
  234.8 3.1 collective-permute-start.11
  238.8 2.7 collective-permute-start.12
  241.5 3.9 %collective-permute-done.12 = bf16[2,256,128]{1,2,0:T(8,128)(2,1)S(1)} collective-permute-done((bf16[2,256,128]{1,2,0:T(8,128)(2,1)S(1)}, bf16[2,256,128]{1,2,0:T(8,128)(2,1)S(1)}, u32[]{:S(2)}, u32[]{:S(2)}) %collective-permute-start.12) | collective-permute-done | bytes 131104 | tf_op jit(solution)/shard_map/ppermute | solution.py:30
  246.1 15.0 %all_to_all.66 = bf16[4,64,1792]{2,1,0:T(8,128)(2,1)S(1)} all-to-all(bf16[4,64,1792]{2,1,0:T(8,128)(2,1)S(1)} %bitcast.199), channel_id=1, replica_groups={{0,16,32,48},{1,17,33,49},{2,18,34,50},{3,19,35,51},{4,20,36,52},{5,21,..., dimensions={0} | all-to-all | bytes 1835008 | tf_op jit(solution)/shard_map/all_to_all | solution.py:23
  261.8 32.2 %all_to_all.67 = bf16[16,8,1792]{2,1,0:T(8,128)(2,1)S(1)} all-to-all(bf16[16,8,1792]{2,1,0:T(8,128)(2,1)S(1)} %bitcast.202), channel_id=1, replica_groups={{0,1,2,3,4,5,6,7,8,9,10,11,12,13,14,15},{16,17,18,19,20,21,22,23,24,25,..., dimensions={0} | all-to-all | bytes 917504 | tf_op jit(solution)/shard_map/all_to_all | solution.py:23
  294.1 5.7 %collective-permute-start.13 = (bf16[8,7168]{1,0:T(8,128)(2,1)S(1)}, bf16[8,7168]{1,0:T(8,128)(2,1)S(1)}, u32[]{:S(2)}, u32[]{:S(2)}) collective-permute-start(bf16[8,7168]{1,0:T(8,128)(2,1)S(1)} %fusion.58), channel_id=1, source_target_pairs={{0,72},{1,73},{2,74},{3,75},{4,76},{5,77},{6,78},{7,79},{8,64},{9,... | collective-permute-start | bytes 344072 | tf_op jit(solution)/shard_map/ppermute | solution.py:40
  299.7 13.3 %collective-permute-done.13 = bf16[8,7168]{1,0:T(8,128)(2,1)S(1)} collective-permute-done((bf16[8,7168]{1,0:T(8,128)(2,1)S(1)}, bf16[8,7168]{1,0:T(8,128)(2,1)S(1)}, u32[]{:S(2)}, u32[]{:S(2)}) %collective-permute-start.13) | collective-permute-done | bytes 114720 | tf_op jit(solution)/shard_map/ppermute | solution.py:40
  (103 shorter events, 47.0 us)
Async XLA Ops:
  0.0 6.9 %copy-start.9 = (s32[1,2,8,2]{2,3,1,0:T(2,128)S(1)}, s32[1,2,8,2]{2,3,1,0:T(2,128)}, u32[]{:S(2)}) copy-start(s32[1,2,8,2]{2,3,1,0:T(2,128)} %param.10) | copy-start | bytes 388
  2.7 17.9 %copy-start.4 = (bf16[1,128,7168]{2,1,0:T(8,128)(2,1)S(1)}, bf16[1,128,7168]{2,1,0:T(8,128)(2,1)}, u32[]{:S(2)}) copy-start(bf16[1,128,7168]{2,1,0:T(8,128)(2,1)} %param.9) | copy-start | bytes 5505028
  2.7 19.9 %collective-permute-start = (bf16[2,1792,128]{2,1,0:T(8,128)(2,1)}, bf16[2,1792,128]{2,1,0:T(8,128)(2,1)}, u32[]{:S(2)}, u32[]{:S(2)}) collective-permute-start(bf16[2,1792,128]{2,1,0:T(8,128)(2,1)} %get-tuple-element.39), channel_id=1, source_target_pairs={{0,1},{1,0},{2,3},{3,2},{4,5},{5,4},{6,7},{7,6},{8,9},{9,8},{10,11... | collective-permute-start | bytes 2752520 | tf_op jit(solution)/shard_map/ppermute | solution.py:30
  7.9 49.1 %all-to-all-start = ((bf16[16,8,1920]{2,1,0:T(8,128)(2,1)}), bf16[16,8,1920]{2,1,0:T(8,128)(2,1)S(1)}, u32[]{:S(2)}, u32[]{:S(2)}) async-start(bf16[16,8,1920]{2,1,0:T(8,128)(2,1)} %maximum_maximum_fusion), calls=%async_computation | async-start | bytes 983040 | tf_op jit(solution)/shard_map/all_to_all | solution.py:23
  24.8 63.8 %copy-start.2 = (bf16[2,1792,128]{2,1,0:T(8,128)(2,1)}, bf16[2,1792,128]{2,1,0:T(8,128)(2,1)S(1)}, u32[]{:S(2)}) copy-start(bf16[2,1792,128]{2,1,0:T(8,128)(2,1)S(1)} %get-tuple-element.17) | copy-start | bytes 2752516
  24.8 8.6 %copy-start.5 = (bf16[1,1,128,1792]{3,2,0,1:T(8,128)(2,1)S(1)}, bf16[1,1,128,1792]{3,2,0,1:T(8,128)(2,1)}, u32[]{:S(2)}) copy-start(bf16[1,1,128,1792]{3,2,0,1:T(8,128)(2,1)} %get-tuple-element.30) | copy-start | bytes 1376260
  24.8 8.6 %copy-start.6 = (bf16[1,1,128,1792]{3,2,0,1:T(8,128)(2,1)S(1)}, bf16[1,1,128,1792]{3,2,0,1:T(8,128)(2,1)}, u32[]{:S(2)}) copy-start(bf16[1,1,128,1792]{3,2,0,1:T(8,128)(2,1)} %get-tuple-element.31) | copy-start | bytes 1376260
  27.7 7.0 %collective-permute-start.2 = (bf16[2,128,1792]{2,1,0:T(8,128)(2,1)}, bf16[2,128,1792]{2,1,0:T(8,128)(2,1)}, u32[]{:S(2)}, u32[]{:S(2)}) collective-permute-start(bf16[2,128,1792]{2,1,0:T(8,128)(2,1)} %maximum_select_fusion.1), channel_id=1, source_target_pairs={{0,1},{1,0},{2,3},{3,2},{4,5},{5,4},{6,7},{7,6},{8,9},{9,8},{10,11... | collective-permute-start | bytes 2752520 | tf_op jit(solution)/shard_map/ppermute | solution.py:30
  29.8 27.2 %collective-permute-start.1 = (bf16[2,1792,128]{2,1,0:T(8,128)(2,1)}, bf16[2,1792,128]{2,1,0:T(8,128)(2,1)S(1)}, u32[]{:S(2)}, u32[]{:S(2)}) collective-permute-start(bf16[2,1792,128]{2,1,0:T(8,128)(2,1)} %get-tuple-element.13), channel_id=1, source_target_pairs={{0,2},{1,3},{2,0},{3,1},{4,6},{5,7},{6,4},{7,5},{8,10},{9,11},{10,... | collective-permute-start | bytes 2752520 | tf_op jit(solution)/shard_map/ppermute | solution.py:30
  37.1 39.7 %collective-permute-start.3 = (bf16[2,128,1792]{2,1,0:T(8,128)(2,1)}, bf16[2,128,1792]{2,1,0:T(8,128)(2,1)}, u32[]{:S(2)}, u32[]{:S(2)}) collective-permute-start(bf16[2,128,1792]{2,1,0:T(8,128)(2,1)} %get-tuple-element.27), channel_id=1, source_target_pairs={{0,2},{1,3},{2,0},{3,1},{4,6},{5,7},{6,4},{7,5},{8,10},{9,11},{10,... | collective-permute-start | bytes 2752520 | tf_op jit(solution)/shard_map/ppermute | solution.py:30
  57.0 24.6 %copy-start = (bf16[2,1792,128]{2,1,0:T(8,128)(2,1)}, bf16[2,1792,128]{2,1,0:T(8,128)(2,1)S(1)}, u32[]{:S(2)}) copy-start(bf16[2,1792,128]{2,1,0:T(8,128)(2,1)S(1)} %collective-permute-done.1) | copy-start | bytes 2752516
  77.7 3.8 %collective-permute-start.4 = (f32[2,256,128]{1,2,0:T(8,128)S(1)}, f32[2,256,128]{1,2,0:T(8,128)S(1)}, u32[]{:S(2)}, u32[]{:S(2)}) collective-permute-start(f32[2,256,128]{1,2,0:T(8,128)S(1)} %pad_maximum_fusion.4), channel_id=1, source_target_pairs={{0,1},{1,0},{2,3},{3,2},{4,5},{5,4},{6,7},{7,6},{8,9},{9,8},{10,11... | collective-permute-start | bytes 786440 | tf_op jit(solution)/shard_map/ppermute | solution.py:30
  82.0 6.6 %collective-permute-start.5 = (f32[256,128]{0,1:T(8,128)S(1)}, f32[256,128]{0,1:T(8,128)S(1)}, u32[]{:S(2)}, u32[]{:S(2)}) collective-permute-start(f32[256,128]{0,1:T(8,128)S(1)} %convolution_add_fusion), channel_id=1, source_target_pairs={{0,2},{1,3},{2,0},{3,1},{4,6},{5,7},{6,4},{7,5},{8,10},{9,11},{10,... | collective-permute-start | bytes 393224 | tf_op jit(solution)/shard_map/ppermute | solution.py:30
  89.1 4.0 %collective-permute-start.6 = (bf16[256,128]{0,1:T(8,128)(2,1)S(1)}, bf16[256,128]{0,1:T(8,128)(2,1)S(1)}, u32[]{:S(2)}, u32[]{:S(2)}) collective-permute-start(bf16[256,128]{0,1:T(8,128)(2,1)S(1)} %multiply_convert_fusion.2), channel_id=1, source_target_pairs={{0,1},{1,0},{2,3},{3,2},{4,5},{5,4},{6,7},{7,6},{8,9},{9,8},{10,11... | collective-permute-start | bytes 196616 | tf_op jit(solution)/shard_map/ppermute | solution.py:30
  93.2 6.6 %collective-permute-start.7 = (bf16[2,256,128]{1,2,0:T(8,128)(2,1)S(1)}, bf16[2,256,128]{1,2,0:T(8,128)(2,1)S(1)}, u32[]{:S(2)}, u32[]{:S(2)}) collective-permute-start(bf16[2,256,128]{1,2,0:T(8,128)(2,1)S(1)} %pad_maximum_fusion.6), channel_id=1, source_target_pairs={{0,2},{1,3},{2,0},{3,1},{4,6},{5,7},{6,4},{7,5},{8,10},{9,11},{10,... | collective-permute-start | bytes 393224 | tf_op jit(solution)/shard_map/ppermute | solution.py:30
  101.4 16.4 %all-to-all-start.2 = ((bf16[4,64,1792]{2,1,0:T(8,128)(2,1)}), bf16[4,64,1792]{2,1,0:T(8,128)(2,1)S(1)}, u32[]{:S(2)}, u32[]{:S(2)}) async-start(bf16[4,64,1792]{2,1,0:T(8,128)(2,1)} %bitcast.198), calls=%async_computation.2 | async-start | bytes 1835008 | tf_op jit(solution)/shard_map/all_to_all | solution.py:23
  156.8 19.0 %collective-permute-start.8 = (bf16[8,7168]{1,0:T(8,128)(2,1)S(1)}, bf16[8,7168]{1,0:T(8,128)(2,1)S(1)}, u32[]{:S(2)}, u32[]{:S(2)}) collective-permute-start(bf16[8,7168]{1,0:T(8,128)(2,1)S(1)} %fusion.60), channel_id=1, source_target_pairs={{0,72},{1,73},{2,74},{3,75},{4,76},{5,77},{6,78},{7,79},{8,64},{9,... | collective-permute-start | bytes 344072 | tf_op jit(solution)/shard_map/ppermute | solution.py:40
  205.6 17.0 %copy-start.3 = (bf16[2,1792,128]{2,1,0:T(8,128)(2,1)S(1)}, bf16[2,1792,128]{2,1,0:T(8,128)(2,1)}, u32[]{:S(2)}) copy-start(bf16[2,1792,128]{2,1,0:T(8,128)(2,1)} %copy-done.2) | copy-start | bytes 2752516
  206.0 17.1 %copy-start.1 = (bf16[2,1792,128]{2,1,0:T(8,128)(2,1)S(1)}, bf16[2,1792,128]{2,1,0:T(8,128)(2,1)}, u32[]{:S(2)}) copy-start(bf16[2,1792,128]{2,1,0:T(8,128)(2,1)} %copy-done) | copy-start | bytes 2752516
  223.6 3.7 %collective-permute-start.9 = (f32[2,256,128]{1,2,0:T(8,128)S(1)}, f32[2,256,128]{1,2,0:T(8,128)S(1)}, u32[]{:S(2)}, u32[]{:S(2)}) collective-permute-start(f32[2,256,128]{1,2,0:T(8,128)S(1)} %pad_maximum_fusion.5), channel_id=1, source_target_pairs={{0,1},{1,0},{2,3},{3,2},{4,5},{5,4},{6,7},{7,6},{8,9},{9,8},{10,11... | collective-permute-start | bytes 786440 | tf_op jit(solution)/shard_map/ppermute | solution.py:30
  227.7 6.6 %collective-permute-start.10 = (f32[256,128]{0,1:T(8,128)S(1)}, f32[256,128]{0,1:T(8,128)S(1)}, u32[]{:S(2)}, u32[]{:S(2)}) collective-permute-start(f32[256,128]{0,1:T(8,128)S(1)} %fusion.15), channel_id=1, source_target_pairs={{0,2},{1,3},{2,0},{3,1},{4,6},{5,7},{6,4},{7,5},{8,10},{9,11},{10,... | collective-permute-start | bytes 393224 | tf_op jit(solution)/shard_map/ppermute | solution.py:30
  234.8 4.0 %collective-permute-start.11 = (bf16[256,128]{0,1:T(8,128)(2,1)S(1)}, bf16[256,128]{0,1:T(8,128)(2,1)S(1)}, u32[]{:S(2)}, u32[]{:S(2)}) collective-permute-start(bf16[256,128]{0,1:T(8,128)(2,1)S(1)} %multiply_convert_fusion.1), channel_id=1, source_target_pairs={{0,1},{1,0},{2,3},{3,2},{4,5},{5,4},{6,7},{7,6},{8,9},{9,8},{10,11... | collective-permute-start | bytes 196616 | tf_op jit(solution)/shard_map/ppermute | solution.py:30
  238.8 6.6 %collective-permute-start.12 = (bf16[2,256,128]{1,2,0:T(8,128)(2,1)S(1)}, bf16[2,256,128]{1,2,0:T(8,128)(2,1)S(1)}, u32[]{:S(2)}, u32[]{:S(2)}) collective-permute-start(bf16[2,256,128]{1,2,0:T(8,128)(2,1)S(1)} %pad_maximum_fusion.7), channel_id=1, source_target_pairs={{0,2},{1,3},{2,0},{3,1},{4,6},{5,7},{6,4},{7,5},{8,10},{9,11},{10,... | collective-permute-start | bytes 393224 | tf_op jit(solution)/shard_map/ppermute | solution.py:30
  294.1 19.0 %collective-permute-start.13 = (bf16[8,7168]{1,0:T(8,128)(2,1)S(1)}, bf16[8,7168]{1,0:T(8,128)(2,1)S(1)}, u32[]{:S(2)}, u32[]{:S(2)}) collective-permute-start(bf16[8,7168]{1,0:T(8,128)(2,1)S(1)} %fusion.58), channel_id=1, source_target_pairs={{0,72},{1,73},{2,74},{3,75},{4,76},{5,77},{6,78},{7,79},{8,64},{9,... | collective-permute-start | bytes 344072 | tf_op jit(solution)/shard_map/ppermute | solution.py:40
  (3 other events, 19.4 us)

commit v11 on v10

--- a/solution.py
+++ b/solution.py
@@ -128,8 +128,8 @@
             even, odd = jnp.stack(quarters[0::2]), jnp.stack(quarters[1::2])
             keep, give = jnp.where(core == 0, even, odd), jnp.where(core == 0, odd, even)
             down, give = for_chip(from_sibling(keep, give), chip)
+            arrived, up, up_far, give = lax.optimization_barrier((arrived, up, up_far, give))
             down_far = swap(give, 2)
-            arrived, up, up_far, down = lax.optimization_barrier((arrived, up, up_far, down))
             up = [up[0], up[1], up_far[0], up_far[1]]
             facts = arrived[:, :, part:].astype(jnp.float32).reshape(total, LANES)
             routes = facts[:, : 4 * passes * top].reshape(total, 4, passes, top)
@@ -144,11 +144,11 @@
         picker, weigher = tables(ids, gates, half, peers, rows_dev)
         slots = jnp.dot(picker, rows, preferred_element_type=jnp.float32).astype(jnp.bfloat16)
         slots = exchange(slots, same_place)
-        if t == 0:
-            slots, down_far = lax.optimization_barrier((slots, down_far))
-            down = jnp.concatenate([down, down_far]).reshape(PAIR * HID_DEV, part)
         sums = [jnp.dot(slots, up[k], preferred_element_type=jnp.float32) for k in range(PAIR)]
         came = swap(jnp.stack([sums[1], sums[3]]), 1)
+        if t == 0:
+            came, down_far = lax.optimization_barrier((came, down_far))
+            down = jnp.concatenate([down, down_far]).reshape(PAIR * HID_DEV, part)
         came_far = swap(sums[2] + came[1], 2)
         active = jax.nn.silu(sums[0] + came[0] + came_far).astype(jnp.bfloat16)
         active = jnp.stack([active, swap(active, 1)])

time: 315 us -> 321 us (1.019)
  blocking collectives: 147 us -> 131 us
  waiting for transfers between devices: 79.6 us -> 92.1 us
  starting transfers between devices: 58.8 us -> 66.3 us
    all_to_all x6 -> x5, blocking collectives: 147 us -> 131 us  [exchange(): lax.all_to_all(value, 'expert', split_axis=0, concat_axis=0, axis_index_g...]
    all_to_all x2 -> x3, waiting for transfers between devices: 12.2 us -> 23 us  [exchange(): lax.all_to_all(value, 'expert', split_axis=0, concat_axis=0, axis_index_g...]
    all_to_all x2 -> x3, starting transfers between devices: 16.8 us -> 21.1 us  [exchange(): lax.all_to_all(value, 'expert', split_axis=0, concat_axis=0, axis_index_g...]
    ppermute x12, starting transfers between devices: 30.9 us -> 34.2 us  [swap(): return lax.ppermute(value, 'expert', [(i, i ^ bit) for i in range(count)])]
  transfers between devices with their start and end apart: 16 -> 17, of which waited for: 13 -> 13; matrix products, arithmetic and copies ran while one was open for 5% -> 5% of each run, Pallas kernels for 0% -> 0%
where the time goes in v11:
time: 321 us; the launch traced here: 319 us
  blocking collectives  131 us (41%)
  waiting for transfers between devices  92.1 us (29%)
  starting transfers between devices  66.3 us (21%)
  other arithmetic  12.8 us (4%)
  matrix products  10.4 us (3%)
  local copies, waits for them, and re-layouts  6.01 us (2%)
    all_to_all x5, blocking collectives, exchange(): lax.all_to_all(value, 'expert', split_axis=0, concat_axis=0, axis_index_g...  131 us
    ppermute x12, waiting for transfers between devices, swap(): return lax.ppermute(value, 'expert', [(i, i ^ bit) for i in range(count)])  42.1 us
    ppermute x12, starting transfers between devices, swap(): return lax.ppermute(value, 'expert', [(i, i ^ bit) for i in range(count)])  34.2 us
    ppermute x2, waiting for transfers between devices, next_section(): return lax.ppermute(value, ('section', 'expert'), route)  27 us
    all_to_all x3, waiting for transfers between devices, exchange(): lax.all_to_all(value, 'expert', split_axis=0, concat_axis=0, axis_index_g...  23 us
    all_to_all x3, starting transfers between devices, exchange(): lax.all_to_all(value, 'expert', split_axis=0, concat_axis=0, axis_index_g...  21.1 us
    ppermute x2, starting transfers between devices, next_section(): return lax.ppermute(value, ('section', 'expert'), route)  11.1 us
  transfers between devices with their start and end apart: 17, of which 13 were waited for; matrix products, arithmetic and copies ran while one was open for 5% of the time, Pallas kernels for 0%

profile of v11, /device:TPU:7, one launch (start us, length us, event | category | flops | bytes accessed | tf_op | source)
XLA Modules:
  0.0 319.4 jit_solution(14964709618297047325)
XLA Ops:
  7.9 12.7 %all-to-all-start = ((bf16[16,8,1920]{2,1,0:T(8,128)(2,1)}), bf16[16,8,1920]{2,1,0:T(8,128)(2,1)S(1)}, u32[]{:S(2)}, u32[]{:S(2)}) async-start(bf16[16,8,1920]{2,1,0:T(8,128)(2,1)} %maximum_maximum_fusion), calls=%async_computation | async-start | bytes 983040 | tf_op jit(solution)/shard_map/all_to_all | solution.py:23
  29.5 3.5 %collective-permute-start.1 = (bf16[2,1792,128]{2,1,0:T(8,128)(2,1)}, bf16[2,1792,128]{2,1,0:T(8,128)(2,1)S(1)}, u32[]{:S(2)}, u32[]{:S(2)}) collective-permute-start(bf16[2,1792,128]{2,1,0:T(8,128)(2,1)} %get-tuple-element.13), channel_id=1, source_target_pairs={{0,2},{1,3},{2,0},{3,1},{4,6},{5,7},{6,4},{7,5},{8,10},{9,11},{10,... | collective-permute-start | bytes 2752520 | tf_op jit(solution)/shard_map/ppermute | solution.py:30
  36.8 20.1 %collective-permute-done.1 = bf16[2,1792,128]{2,1,0:T(8,128)(2,1)S(1)} collective-permute-done((bf16[2,1792,128]{2,1,0:T(8,128)(2,1)}, bf16[2,1792,128]{2,1,0:T(8,128)(2,1)S(1)}, u32[]{:S(2)}, u32[]{:S(2)}) %collective-permute-start.1) | collective-permute-done | bytes 917536 | tf_op jit(solution)/shard_map/ppermute | solution.py:30
  59.0 4.2 %all-to-all-start.1 = ((bf16[4,64,1792]{2,1,0:T(8,128)(2,1)}), bf16[4,64,1792]{2,1,0:T(8,128)(2,1)S(1)}, u32[]{:S(2)}, u32[]{:S(2)}) async-start(bf16[4,64,1792]{2,1,0:T(8,128)(2,1)} %bitcast.25), calls=%async_computation.1 | async-start | bytes 1835008 | tf_op jit(solution)/shard_map/all_to_all | solution.py:23
  65.1 10.8 %all-to-all-done.1 = bf16[4,64,1792]{2,1,0:T(8,128)(2,1)S(1)} async-done(((bf16[4,64,1792]{2,1,0:T(8,128)(2,1)}), bf16[4,64,1792]{2,1,0:T(8,128)(2,1)S(1)}, u32[]{:S(2)}, u32[]{:S(2)}) %all-to-all-start.1) | async-done | bytes 917536 | tf_op jit(solution)/shard_map/all_to_all | solution.py:23
  77.9 3.8 %collective-permute-start.3 = (f32[2,256,128]{1,2,0:T(8,128)S(1)}, f32[2,256,128]{1,2,0:T(8,128)S(1)}, u32[]{:S(2)}, u32[]{:S(2)}) collective-permute-start(f32[2,256,128]{1,2,0:T(8,128)S(1)} %pad_maximum_fusion.4), channel_id=1, source_target_pairs={{0,1},{1,0},{2,3},{3,2},{4,5},{5,4},{6,7},{7,6},{8,9},{9,8},{10,11... | collective-permute-start | bytes 786440 | tf_op jit(solution)/shard_map/ppermute | solution.py:30
  81.7 4.5 %collective-permute-done.4 = bf16[2,128,1792]{2,1,0:T(8,128)(2,1)} collective-permute-done((bf16[2,128,1792]{2,1,0:T(8,128)(2,1)}, bf16[2,128,1792]{2,1,0:T(8,128)(2,1)}, u32[]{:S(2)}, u32[]{:S(2)}) %collective-permute-start.4) | collective-permute-done | bytes 917536 | tf_op jit(solution)/shard_map/ppermute | solution.py:30
  89.0 3.5 %collective-permute-done.5 = f32[256,128]{0,1:T(8,128)S(1)} collective-permute-done((f32[256,128]{0,1:T(8,128)S(1)}, f32[256,128]{0,1:T(8,128)S(1)}, u32[]{:S(2)}, u32[]{:S(2)}) %collective-permute-start.5) | collective-permute-done | bytes 131104 | tf_op jit(solution)/shard_map/ppermute | solution.py:30
  92.9 5.0 %collective-permute-start.6 = (bf16[256,128]{0,1:T(8,128)(2,1)S(1)}, bf16[256,128]{0,1:T(8,128)(2,1)S(1)}, u32[]{:S(2)}, u32[]{:S(2)}) collective-permute-start(bf16[256,128]{0,1:T(8,128)(2,1)S(1)} %multiply_convert_fusion.2), channel_id=1, source_target_pairs={{0,1},{1,0},{2,3},{3,2},{4,5},{5,4},{6,7},{7,6},{8,9},{9,8},{10,11... | collective-permute-start | bytes 196616 | tf_op jit(solution)/shard_map/ppermute | solution.py:30
  102.1 3.3 %collective-permute-done.7 = bf16[2,256,128]{1,2,0:T(8,128)(2,1)S(1)} collective-permute-done((bf16[2,256,128]{1,2,0:T(8,128)(2,1)S(1)}, bf16[2,256,128]{1,2,0:T(8,128)(2,1)S(1)}, u32[]{:S(2)}, u32[]{:S(2)}) %collective-permute-start.7) | collective-permute-done | bytes 131104 | tf_op jit(solution)/shard_map/ppermute | solution.py:30
  107.0 4.2 %all-to-all-start.2 = ((bf16[4,64,1792]{2,1,0:T(8,128)(2,1)}), bf16[4,64,1792]{2,1,0:T(8,128)(2,1)S(1)}, u32[]{:S(2)}, u32[]{:S(2)}) async-start(bf16[4,64,1792]{2,1,0:T(8,128)(2,1)} %bitcast.200), calls=%async_computation.2 | async-start | bytes 1835008 | tf_op jit(solution)/shard_map/all_to_all | solution.py:23
  111.3 12.2 %all-to-all-done.2 = bf16[4,64,1792]{2,1,0:T(8,128)(2,1)S(1)} async-done(((bf16[4,64,1792]{2,1,0:T(8,128)(2,1)}), bf16[4,64,1792]{2,1,0:T(8,128)(2,1)S(1)}, u32[]{:S(2)}, u32[]{:S(2)}) %all-to-all-start.2) | async-done | bytes 917536 | tf_op jit(solution)/shard_map/all_to_all | solution.py:23
  124.1 38.2 %all_to_all.62 = bf16[16,8,1792]{2,1,0:T(8,128)(2,1)S(1)} all-to-all(bf16[16,8,1792]{2,1,0:T(8,128)(2,1)S(1)} %fusion.2), channel_id=1, replica_groups={{0,1,2,3,4,5,6,7,8,9,10,11,12,13,14,15},{16,17,18,19,20,21,22,23,24,25,..., dimensions={0} | all-to-all | bytes 917504 | tf_op jit(solution)/shard_map/all_to_all | solution.py:23
  162.5 5.4 %collective-permute-start.8 = (bf16[8,7168]{1,0:T(8,128)(2,1)S(1)}, bf16[8,7168]{1,0:T(8,128)(2,1)S(1)}, u32[]{:S(2)}, u32[]{:S(2)}) collective-permute-start(bf16[8,7168]{1,0:T(8,128)(2,1)S(1)} %fusion.70), channel_id=1, source_target_pairs={{0,72},{1,73},{2,74},{3,75},{4,76},{5,77},{6,78},{7,79},{8,64},{9,... | collective-permute-start | bytes 344072 | tf_op jit(solution)/shard_map/ppermute | solution.py:40
  167.9 13.6 %collective-permute-done.8 = bf16[8,7168]{1,0:T(8,128)(2,1)S(1)} collective-permute-done((bf16[8,7168]{1,0:T(8,128)(2,1)S(1)}, bf16[8,7168]{1,0:T(8,128)(2,1)S(1)}, u32[]{:S(2)}, u32[]{:S(2)}) %collective-permute-start.8) | collective-permute-done | bytes 114720 | tf_op jit(solution)/shard_map/ppermute | solution.py:40
  181.9 29.3 %all_to_all.63 = bf16[16,8,1792]{2,1,0:T(8,128)(2,1)S(1)} all-to-all(bf16[16,8,1792]{2,1,0:T(8,128)(2,1)S(1)} %pad_maximum_fusion.1), channel_id=1, replica_groups={{0,1,2,3,4,5,6,7,8,9,10,11,12,13,14,15},{16,17,18,19,20,21,22,23,24,25,..., dimensions={0} | all-to-all | bytes 917504 | tf_op jit(solution)/shard_map/all_to_all | solution.py:23
  211.7 16.6 %all_to_all.64 = bf16[4,64,1792]{2,1,0:T(8,128)(2,1)S(1)} all-to-all(bf16[4,64,1792]{2,1,0:T(8,128)(2,1)S(1)} %bitcast.202), channel_id=1, replica_groups={{0,16,32,48},{1,17,33,49},{2,18,34,50},{3,19,35,51},{4,20,36,52},{5,21,..., dimensions={0} | all-to-all | bytes 1835008 | tf_op jit(solution)/shard_map/all_to_all | solution.py:23
  236.1 3.9 %collective-permute-done.10 = f32[256,128]{0,1:T(8,128)S(1)} collective-permute-done((f32[256,128]{0,1:T(8,128)S(1)}, f32[256,128]{0,1:T(8,128)S(1)}, u32[]{:S(2)}, u32[]{:S(2)}) %collective-permute-start.10) | collective-permute-done | bytes 131104 | tf_op jit(solution)/shard_map/ppermute | solution.py:30
  240.5 3.1 collective-permute-start.11
  247.2 3.9 %collective-permute-done.12 = bf16[2,256,128]{1,2,0:T(8,128)(2,1)S(1)} collective-permute-done((bf16[2,256,128]{1,2,0:T(8,128)(2,1)S(1)}, bf16[2,256,128]{1,2,0:T(8,128)(2,1)S(1)}, u32[]{:S(2)}, u32[]{:S(2)}) %collective-permute-start.12) | collective-permute-done | bytes 131104 | tf_op jit(solution)/shard_map/ppermute | solution.py:30
  251.8 15.0 %all_to_all.65 = bf16[4,64,1792]{2,1,0:T(8,128)(2,1)S(1)} all-to-all(bf16[4,64,1792]{2,1,0:T(8,128)(2,1)S(1)} %bitcast.201), channel_id=1, replica_groups={{0,16,32,48},{1,17,33,49},{2,18,34,50},{3,19,35,51},{4,20,36,52},{5,21,..., dimensions={0} | all-to-all | bytes 1835008 | tf_op jit(solution)/shard_map/all_to_all | solution.py:23
  267.5 32.2 %all_to_all.66 = bf16[16,8,1792]{2,1,0:T(8,128)(2,1)S(1)} all-to-all(bf16[16,8,1792]{2,1,0:T(8,128)(2,1)S(1)} %bitcast.203), channel_id=1, replica_groups={{0,1,2,3,4,5,6,7,8,9,10,11,12,13,14,15},{16,17,18,19,20,21,22,23,24,25,..., dimensions={0} | all-to-all | bytes 917504 | tf_op jit(solution)/shard_map/all_to_all | solution.py:23
  299.8 5.7 %collective-permute-start.13 = (bf16[8,7168]{1,0:T(8,128)(2,1)S(1)}, bf16[8,7168]{1,0:T(8,128)(2,1)S(1)}, u32[]{:S(2)}, u32[]{:S(2)}) collective-permute-start(bf16[8,7168]{1,0:T(8,128)(2,1)S(1)} %fusion.68), channel_id=1, source_target_pairs={{0,72},{1,73},{2,74},{3,75},{4,76},{5,77},{6,78},{7,79},{8,64},{9,... | collective-permute-start | bytes 344072 | tf_op jit(solution)/shard_map/ppermute | solution.py:40
  305.4 13.3 %collective-permute-done.13 = bf16[8,7168]{1,0:T(8,128)(2,1)S(1)} collective-permute-done((bf16[8,7168]{1,0:T(8,128)(2,1)S(1)}, bf16[8,7168]{1,0:T(8,128)(2,1)S(1)}, u32[]{:S(2)}, u32[]{:S(2)}) %collective-permute-start.13) | collective-permute-done | bytes 114720 | tf_op jit(solution)/shard_map/ppermute | solution.py:40
  (108 shorter events, 50.9 us)
Async XLA Ops:
  2.6 17.9 %copy-start.4 = (bf16[1,128,7168]{2,1,0:T(8,128)(2,1)S(1)}, bf16[1,128,7168]{2,1,0:T(8,128)(2,1)}, u32[]{:S(2)}) copy-start(bf16[1,128,7168]{2,1,0:T(8,128)(2,1)} %param.9) | copy-start | bytes 5505028
  2.6 19.9 %collective-permute-start = (bf16[2,1792,128]{2,1,0:T(8,128)(2,1)}, bf16[2,1792,128]{2,1,0:T(8,128)(2,1)}, u32[]{:S(2)}, u32[]{:S(2)}) collective-permute-start(bf16[2,1792,128]{2,1,0:T(8,128)(2,1)} %get-tuple-element.39), channel_id=1, source_target_pairs={{0,1},{1,0},{2,3},{3,2},{4,5},{5,4},{6,7},{7,6},{8,9},{9,8},{10,11... | collective-permute-start | bytes 2752520 | tf_op jit(solution)/shard_map/ppermute | solution.py:30
  7.9 49.1 %all-to-all-start = ((bf16[16,8,1920]{2,1,0:T(8,128)(2,1)}), bf16[16,8,1920]{2,1,0:T(8,128)(2,1)S(1)}, u32[]{:S(2)}, u32[]{:S(2)}) async-start(bf16[16,8,1920]{2,1,0:T(8,128)(2,1)} %maximum_maximum_fusion), calls=%async_computation | async-start | bytes 983040 | tf_op jit(solution)/shard_map/all_to_all | solution.py:23
  25.1 8.1 %copy-start.5 = (bf16[1,1,128,1792]{3,2,0,1:T(8,128)(2,1)S(1)}, bf16[1,1,128,1792]{3,2,0,1:T(8,128)(2,1)}, u32[]{:S(2)}) copy-start(bf16[1,1,128,1792]{3,2,0,1:T(8,128)(2,1)} %get-tuple-element.30) | copy-start | bytes 1376260
  25.1 8.1 %copy-start.6 = (bf16[1,1,128,1792]{3,2,0,1:T(8,128)(2,1)S(1)}, bf16[1,1,128,1792]{3,2,0,1:T(8,128)(2,1)}, u32[]{:S(2)}) copy-start(bf16[1,1,128,1792]{3,2,0,1:T(8,128)(2,1)} %get-tuple-element.31) | copy-start | bytes 1376260
  27.5 7.0 %collective-permute-start.2 = (bf16[2,128,1792]{2,1,0:T(8,128)(2,1)}, bf16[2,128,1792]{2,1,0:T(8,128)(2,1)}, u32[]{:S(2)}, u32[]{:S(2)}) collective-permute-start(bf16[2,128,1792]{2,1,0:T(8,128)(2,1)} %maximum_select_fusion.1), channel_id=1, source_target_pairs={{0,1},{1,0},{2,3},{3,2},{4,5},{5,4},{6,7},{7,6},{8,9},{9,8},{10,11... | collective-permute-start | bytes 2752520 | tf_op jit(solution)/shard_map/ppermute | solution.py:30
  29.5 27.4 %collective-permute-start.1 = (bf16[2,1792,128]{2,1,0:T(8,128)(2,1)}, bf16[2,1792,128]{2,1,0:T(8,128)(2,1)S(1)}, u32[]{:S(2)}, u32[]{:S(2)}) collective-permute-start(bf16[2,1792,128]{2,1,0:T(8,128)(2,1)} %get-tuple-element.13), channel_id=1, source_target_pairs={{0,2},{1,3},{2,0},{3,1},{4,6},{5,7},{6,4},{7,5},{8,10},{9,11},{10,... | collective-permute-start | bytes 2752520 | tf_op jit(solution)/shard_map/ppermute | solution.py:30
  56.9 29.3 %copy-start = (bf16[2,1792,128]{2,1,0:T(8,128)(2,1)}, bf16[2,1792,128]{2,1,0:T(8,128)(2,1)S(1)}, u32[]{:S(2)}) copy-start(bf16[2,1792,128]{2,1,0:T(8,128)(2,1)S(1)} %collective-permute-done.1) | copy-start | bytes 2752516
  59.0 16.9 %all-to-all-start.1 = ((bf16[4,64,1792]{2,1,0:T(8,128)(2,1)}), bf16[4,64,1792]{2,1,0:T(8,128)(2,1)S(1)}, u32[]{:S(2)}, u32[]{:S(2)}) async-start(bf16[4,64,1792]{2,1,0:T(8,128)(2,1)} %bitcast.25), calls=%async_computation.1 | async-start | bytes 1835008 | tf_op jit(solution)/shard_map/all_to_all | solution.py:23
  63.2 23.1 %collective-permute-start.4 = (bf16[2,128,1792]{2,1,0:T(8,128)(2,1)}, bf16[2,128,1792]{2,1,0:T(8,128)(2,1)}, u32[]{:S(2)}, u32[]{:S(2)}) collective-permute-start(bf16[2,128,1792]{2,1,0:T(8,128)(2,1)} %get-tuple-element.18), channel_id=1, source_target_pairs={{0,2},{1,3},{2,0},{3,1},{4,6},{5,7},{6,4},{7,5},{8,10},{9,11},{10,... | collective-permute-start | bytes 2752520 | tf_op jit(solution)/shard_map/ppermute | solution.py:30
  77.4 15.0 %copy-start.2 = (bf16[2,1792,128]{2,1,0:T(8,128)(2,1)S(1)}, bf16[2,1792,128]{2,1,0:T(8,128)(2,1)}, u32[]{:S(2)}) copy-start(bf16[2,1792,128]{2,1,0:T(8,128)(2,1)} %get-tuple-element.16) | copy-start | bytes 2752516
  77.9 8.3 %collective-permute-start.3 = (f32[2,256,128]{1,2,0:T(8,128)S(1)}, f32[2,256,128]{1,2,0:T(8,128)S(1)}, u32[]{:S(2)}, u32[]{:S(2)}) collective-permute-start(f32[2,256,128]{1,2,0:T(8,128)S(1)} %pad_maximum_fusion.4), channel_id=1, source_target_pairs={{0,1},{1,0},{2,3},{3,2},{4,5},{5,4},{6,7},{7,6},{8,9},{9,8},{10,11... | collective-permute-start | bytes 786440 | tf_op jit(solution)/shard_map/ppermute | solution.py:30
  86.7 5.7 %collective-permute-start.5 = (f32[256,128]{0,1:T(8,128)S(1)}, f32[256,128]{0,1:T(8,128)S(1)}, u32[]{:S(2)}, u32[]{:S(2)}) collective-permute-start(f32[256,128]{0,1:T(8,128)S(1)} %fusion.15), channel_id=1, source_target_pairs={{0,2},{1,3},{2,0},{3,1},{4,6},{5,7},{6,4},{7,5},{8,10},{9,11},{10,... | collective-permute-start | bytes 393224 | tf_op jit(solution)/shard_map/ppermute | solution.py:30
  92.9 5.8 %collective-permute-start.6 = (bf16[256,128]{0,1:T(8,128)(2,1)S(1)}, bf16[256,128]{0,1:T(8,128)(2,1)S(1)}, u32[]{:S(2)}, u32[]{:S(2)}) collective-permute-start(bf16[256,128]{0,1:T(8,128)(2,1)S(1)} %multiply_convert_fusion.2), channel_id=1, source_target_pairs={{0,1},{1,0},{2,3},{3,2},{4,5},{5,4},{6,7},{7,6},{8,9},{9,8},{10,11... | collective-permute-start | bytes 196616 | tf_op jit(solution)/shard_map/ppermute | solution.py:30
  98.8 6.6 %collective-permute-start.7 = (bf16[2,256,128]{1,2,0:T(8,128)(2,1)S(1)}, bf16[2,256,128]{1,2,0:T(8,128)(2,1)S(1)}, u32[]{:S(2)}, u32[]{:S(2)}) collective-permute-start(bf16[2,256,128]{1,2,0:T(8,128)(2,1)S(1)} %pad_maximum_fusion.6), channel_id=1, source_target_pairs={{0,2},{1,3},{2,0},{3,1},{4,6},{5,7},{6,4},{7,5},{8,10},{9,11},{10,... | collective-permute-start | bytes 393224 | tf_op jit(solution)/shard_map/ppermute | solution.py:30
  107.0 16.5 %all-to-all-start.2 = ((bf16[4,64,1792]{2,1,0:T(8,128)(2,1)}), bf16[4,64,1792]{2,1,0:T(8,128)(2,1)S(1)}, u32[]{:S(2)}, u32[]{:S(2)}) async-start(bf16[4,64,1792]{2,1,0:T(8,128)(2,1)} %bitcast.200), calls=%async_computation.2 | async-start | bytes 1835008 | tf_op jit(solution)/shard_map/all_to_all | solution.py:23
  162.5 19.0 %collective-permute-start.8 = (bf16[8,7168]{1,0:T(8,128)(2,1)S(1)}, bf16[8,7168]{1,0:T(8,128)(2,1)S(1)}, u32[]{:S(2)}, u32[]{:S(2)}) collective-permute-start(bf16[8,7168]{1,0:T(8,128)(2,1)S(1)} %fusion.70), channel_id=1, source_target_pairs={{0,72},{1,73},{2,74},{3,75},{4,76},{5,77},{6,78},{7,79},{8,64},{9,... | collective-permute-start | bytes 344072 | tf_op jit(solution)/shard_map/ppermute | solution.py:40
  211.3 17.0 %copy-start.3 = (bf16[2,1792,128]{2,1,0:T(8,128)(2,1)S(1)}, bf16[2,1792,128]{2,1,0:T(8,128)(2,1)}, u32[]{:S(2)}) copy-start(bf16[2,1792,128]{2,1,0:T(8,128)(2,1)} %get-tuple-element.16) | copy-start | bytes 2752516
  211.7 17.1 %copy-start.1 = (bf16[2,1792,128]{2,1,0:T(8,128)(2,1)S(1)}, bf16[2,1792,128]{2,1,0:T(8,128)(2,1)}, u32[]{:S(2)}) copy-start(bf16[2,1792,128]{2,1,0:T(8,128)(2,1)} %copy-done) | copy-start | bytes 2752516
  229.2 3.7 %collective-permute-start.9 = (f32[2,256,128]{1,2,0:T(8,128)S(1)}, f32[2,256,128]{1,2,0:T(8,128)S(1)}, u32[]{:S(2)}, u32[]{:S(2)}) collective-permute-start(f32[2,256,128]{1,2,0:T(8,128)S(1)} %pad_maximum_fusion.5), channel_id=1, source_target_pairs={{0,1},{1,0},{2,3},{3,2},{4,5},{5,4},{6,7},{7,6},{8,9},{9,8},{10,11... | collective-permute-start | bytes 786440 | tf_op jit(solution)/shard_map/ppermute | solution.py:30
  233.4 6.6 %collective-permute-start.10 = (f32[256,128]{0,1:T(8,128)S(1)}, f32[256,128]{0,1:T(8,128)S(1)}, u32[]{:S(2)}, u32[]{:S(2)}) collective-permute-start(f32[256,128]{0,1:T(8,128)S(1)} %fusion.18), channel_id=1, source_target_pairs={{0,2},{1,3},{2,0},{3,1},{4,6},{5,7},{6,4},{7,5},{8,10},{9,11},{10,... | collective-permute-start | bytes 393224 | tf_op jit(solution)/shard_map/ppermute | solution.py:30
  240.5 4.0 %collective-permute-start.11 = (bf16[256,128]{0,1:T(8,128)(2,1)S(1)}, bf16[256,128]{0,1:T(8,128)(2,1)S(1)}, u32[]{:S(2)}, u32[]{:S(2)}) collective-permute-start(bf16[256,128]{0,1:T(8,128)(2,1)S(1)} %multiply_convert_fusion.1), channel_id=1, source_target_pairs={{0,1},{1,0},{2,3},{3,2},{4,5},{5,4},{6,7},{7,6},{8,9},{9,8},{10,11... | collective-permute-start | bytes 196616 | tf_op jit(solution)/shard_map/ppermute | solution.py:30
  244.5 6.6 %collective-permute-start.12 = (bf16[2,256,128]{1,2,0:T(8,128)(2,1)S(1)}, bf16[2,256,128]{1,2,0:T(8,128)(2,1)S(1)}, u32[]{:S(2)}, u32[]{:S(2)}) collective-permute-start(bf16[2,256,128]{1,2,0:T(8,128)(2,1)S(1)} %pad_maximum_fusion.7), channel_id=1, source_target_pairs={{0,2},{1,3},{2,0},{3,1},{4,6},{5,7},{6,4},{7,5},{8,10},{9,11},{10,... | collective-permute-start | bytes 393224 | tf_op jit(solution)/shard_map/ppermute | solution.py:30
  299.8 19.0 %collective-permute-start.13 = (bf16[8,7168]{1,0:T(8,128)(2,1)S(1)}, bf16[8,7168]{1,0:T(8,128)(2,1)S(1)}, u32[]{:S(2)}, u32[]{:S(2)}) collective-permute-start(bf16[8,7168]{1,0:T(8,128)(2,1)S(1)} %fusion.68), channel_id=1, source_target_pairs={{0,72},{1,73},{2,74},{3,75},{4,76},{5,77},{6,78},{7,79},{8,64},{9,... | collective-permute-start | bytes 344072 | tf_op jit(solution)/shard_map/ppermute | solution.py:40
  (6 other events, 31.5 us)

commit v12 on v10

--- a/solution.py
+++ b/solution.py
@@ -129,8 +129,7 @@
             keep, give = jnp.where(core == 0, even, odd), jnp.where(core == 0, odd, even)
             down, give = for_chip(from_sibling(keep, give), chip)
             down_far = swap(give, 2)
-            arrived, up, up_far, down = lax.optimization_barrier((arrived, up, up_far, down))
-            up = [up[0], up[1], up_far[0], up_far[1]]
+            arrived, up, down = lax.optimization_barrier((arrived, up, down))
             facts = arrived[:, :, part:].astype(jnp.float32).reshape(total, LANES)
             routes = facts[:, : 4 * passes * top].reshape(total, 4, passes, top)
             arrived = arrived[:, :, :part]
@@ -145,7 +144,8 @@
         slots = jnp.dot(picker, rows, preferred_element_type=jnp.float32).astype(jnp.bfloat16)
         slots = exchange(slots, same_place)
         if t == 0:
-            slots, down_far = lax.optimization_barrier((slots, down_far))
+            slots, up_far, down_far = lax.optimization_barrier((slots, up_far, down_far))
+            up = [up[0], up[1], up_far[0], up_far[1]]
             down = jnp.concatenate([down, down_far]).reshape(PAIR * HID_DEV, part)
         sums = [jnp.dot(slots, up[k], preferred_element_type=jnp.float32) for k in range(PAIR)]
         came = swap(jnp.stack([sums[1], sums[3]]), 1)

time: 315 us -> 316 us (level)
  blocking collectives: 147 us -> 130 us
  waiting for transfers between devices: 79.6 us -> 89.3 us
  starting transfers between devices: 58.8 us -> 63.3 us
    all_to_all x6 -> x5, blocking collectives: 147 us -> 130 us  [exchange(): lax.all_to_all(value, 'expert', split_axis=0, concat_axis=0, axis_index_g...]
    all_to_all x2 -> x3, waiting for transfers between devices: 12.2 us -> 24.4 us  [exchange(): lax.all_to_all(value, 'expert', split_axis=0, concat_axis=0, axis_index_g...]
    all_to_all x2 -> x3, starting transfers between devices: 16.8 us -> 21.1 us  [exchange(): lax.all_to_all(value, 'expert', split_axis=0, concat_axis=0, axis_index_g...]
  transfers between devices with their start and end apart: 16 -> 17, of which waited for: 13 -> 15; matrix products, arithmetic and copies ran while one was open for 5% -> 6% of each run, Pallas kernels for 0% -> 0%
where the time goes in v12:
time: 316 us; the launch traced here: 315 us
  blocking collectives  130 us (41%)
  waiting for transfers between devices  89.3 us (28%)
  starting transfers between devices  63.3 us (20%)
  other arithmetic  13 us (4%)
  matrix products  10.6 us (3%)
  local copies, waits for them, and re-layouts  8.05 us (3%)
    all_to_all x5, blocking collectives, exchange(): lax.all_to_all(value, 'expert', split_axis=0, concat_axis=0, axis_index_g...  130 us
    ppermute x12, waiting for transfers between devices, swap(): return lax.ppermute(value, 'expert', [(i, i ^ bit) for i in range(count)])  37.9 us
    ppermute x12, starting transfers between devices, swap(): return lax.ppermute(value, 'expert', [(i, i ^ bit) for i in range(count)])  31.1 us
    ppermute x2, waiting for transfers between devices, next_section(): return lax.ppermute(value, ('section', 'expert'), route)  27 us
    all_to_all x3, waiting for transfers between devices, exchange(): lax.all_to_all(value, 'expert', split_axis=0, concat_axis=0, axis_index_g...  24.4 us
    all_to_all x3, starting transfers between devices, exchange(): lax.all_to_all(value, 'expert', split_axis=0, concat_axis=0, axis_index_g...  21.1 us
    ppermute x2, starting transfers between devices, next_section(): return lax.ppermute(value, ('section', 'expert'), route)  11.1 us
  transfers between devices with their start and end apart: 17, of which 15 were waited for; matrix products, arithmetic and copies ran while one was open for 6% of the time, Pallas kernels for 0%

profile of v12, /device:TPU:7, one launch (start us, length us, event | category | flops | bytes accessed | tf_op | source)
XLA Modules:
  0.0 314.5 jit_solution(13733357102730480748)
XLA Ops:
  7.7 12.7 %all-to-all-start = ((bf16[16,8,1920]{2,1,0:T(8,128)(2,1)}), bf16[16,8,1920]{2,1,0:T(8,128)(2,1)S(1)}, u32[]{:S(2)}, u32[]{:S(2)}) async-start(bf16[16,8,1920]{2,1,0:T(8,128)(2,1)} %maximum_maximum_fusion), calls=%async_computation | async-start | bytes 983040 | tf_op jit(solution)/shard_map/all_to_all | solution.py:23
  31.4 3.5 %collective-permute-start.2 = (bf16[2,1792,128]{2,1,0:T(8,128)(2,1)}, bf16[2,1792,128]{2,1,0:T(8,128)(2,1)S(1)}, u32[]{:S(2)}, u32[]{:S(2)}) collective-permute-start(bf16[2,1792,128]{2,1,0:T(8,128)(2,1)} %get-tuple-element.15), channel_id=1, source_target_pairs={{0,2},{1,3},{2,0},{3,1},{4,6},{5,7},{6,4},{7,5},{8,10},{9,11},{10,... | collective-permute-start | bytes 2752520 | tf_op jit(solution)/shard_map/ppermute | solution.py:30
  40.8 4.7 %all-to-all-done = bf16[16,8,1920]{2,1,0:T(8,128)(2,1)S(1)} async-done(((bf16[16,8,1920]{2,1,0:T(8,128)(2,1)}), bf16[16,8,1920]{2,1,0:T(8,128)(2,1)S(1)}, u32[]{:S(2)}, u32[]{:S(2)}) %all-to-all-start) | async-done | bytes 491552 | tf_op jit(solution)/shard_map/all_to_all | solution.py:23
  47.5 4.2 %all-to-all-start.1 = ((bf16[4,64,1792]{2,1,0:T(8,128)(2,1)}), bf16[4,64,1792]{2,1,0:T(8,128)(2,1)S(1)}, u32[]{:S(2)}, u32[]{:S(2)}) async-start(bf16[4,64,1792]{2,1,0:T(8,128)(2,1)} %bitcast.25), calls=%async_computation.1 | async-start | bytes 1835008 | tf_op jit(solution)/shard_map/all_to_all | solution.py:23
  51.7 6.3 %collective-permute-done.2 = bf16[2,1792,128]{2,1,0:T(8,128)(2,1)S(1)} collective-permute-done((bf16[2,1792,128]{2,1,0:T(8,128)(2,1)}, bf16[2,1792,128]{2,1,0:T(8,128)(2,1)S(1)}, u32[]{:S(2)}, u32[]{:S(2)}) %collective-permute-start.2) | collective-permute-done | bytes 917536 | tf_op jit(solution)/shard_map/ppermute | solution.py:30
  58.0 7.5 %all-to-all-done.1 = bf16[4,64,1792]{2,1,0:T(8,128)(2,1)S(1)} async-done(((bf16[4,64,1792]{2,1,0:T(8,128)(2,1)}), bf16[4,64,1792]{2,1,0:T(8,128)(2,1)S(1)}, u32[]{:S(2)}, u32[]{:S(2)}) %all-to-all-start.1) | async-done | bytes 917536 | tf_op jit(solution)/shard_map/all_to_all | solution.py:23
  65.6 12.2 %collective-permute-done.3 = bf16[2,128,1792]{2,1,0:T(8,128)(2,1)} collective-permute-done((bf16[2,128,1792]{2,1,0:T(8,128)(2,1)}, bf16[2,128,1792]{2,1,0:T(8,128)(2,1)}, u32[]{:S(2)}, u32[]{:S(2)}) %collective-permute-start.3) | collective-permute-done | bytes 917536 | tf_op jit(solution)/shard_map/ppermute | solution.py:30
  85.4 4.7 %collective-permute-done.5 = f32[256,128]{0,1:T(8,128)S(1)} collective-permute-done((f32[256,128]{0,1:T(8,128)S(1)}, f32[256,128]{0,1:T(8,128)S(1)}, u32[]{:S(2)}, u32[]{:S(2)}) %collective-permute-start.5) | collective-permute-done | bytes 131104 | tf_op jit(solution)/shard_map/ppermute | solution.py:30
  90.6 3.1 collective-permute-start.6
  97.9 3.3 %collective-permute-done.7 = bf16[2,256,128]{1,2,0:T(8,128)(2,1)S(1)} collective-permute-done((bf16[2,256,128]{1,2,0:T(8,128)(2,1)S(1)}, bf16[2,256,128]{1,2,0:T(8,128)(2,1)S(1)}, u32[]{:S(2)}, u32[]{:S(2)}) %collective-permute-start.7) | collective-permute-done | bytes 131104 | tf_op jit(solution)/shard_map/ppermute | solution.py:30
  102.8 4.2 %all-to-all-start.2 = ((bf16[4,64,1792]{2,1,0:T(8,128)(2,1)}), bf16[4,64,1792]{2,1,0:T(8,128)(2,1)}, u32[]{:S(2)}, u32[]{:S(2)}) async-start(bf16[4,64,1792]{2,1,0:T(8,128)(2,1)} %bitcast.194), calls=%async_computation.2 | async-start | bytes 1835008 | tf_op jit(solution)/shard_map/all_to_all | solution.py:23
  107.1 12.2 %all-to-all-done.2 = bf16[4,64,1792]{2,1,0:T(8,128)(2,1)} async-done(((bf16[4,64,1792]{2,1,0:T(8,128)(2,1)}), bf16[4,64,1792]{2,1,0:T(8,128)(2,1)}, u32[]{:S(2)}, u32[]{:S(2)}) %all-to-all-start.2) | async-done | bytes 917536 | tf_op jit(solution)/shard_map/all_to_all | solution.py:23
  121.2 36.8 %all_to_all.62 = bf16[16,8,1792]{2,1,0:T(8,128)(2,1)S(1)} all-to-all(bf16[16,8,1792]{2,1,0:T(8,128)(2,1)S(1)} %fusion.2), channel_id=1, replica_groups={{0,1,2,3,4,5,6,7,8,9,10,11,12,13,14,15},{16,17,18,19,20,21,22,23,24,25,..., dimensions={0} | all-to-all | bytes 917504 | tf_op jit(solution)/shard_map/all_to_all | solution.py:23
  158.1 5.4 %collective-permute-start.8 = (bf16[8,7168]{1,0:T(8,128)(2,1)S(1)}, bf16[8,7168]{1,0:T(8,128)(2,1)S(1)}, u32[]{:S(2)}, u32[]{:S(2)}) collective-permute-start(bf16[8,7168]{1,0:T(8,128)(2,1)S(1)} %fusion.54), channel_id=1, source_target_pairs={{0,72},{1,73},{2,74},{3,75},{4,76},{5,77},{6,78},{7,79},{8,64},{9,... | collective-permute-start | bytes 344072 | tf_op jit(solution)/shard_map/ppermute | solution.py:40
  163.5 13.6 %collective-permute-done.8 = bf16[8,7168]{1,0:T(8,128)(2,1)S(1)} collective-permute-done((bf16[8,7168]{1,0:T(8,128)(2,1)S(1)}, bf16[8,7168]{1,0:T(8,128)(2,1)S(1)}, u32[]{:S(2)}, u32[]{:S(2)}) %collective-permute-start.8) | collective-permute-done | bytes 114720 | tf_op jit(solution)/shard_map/ppermute | solution.py:40
  177.4 29.3 %all_to_all.63 = bf16[16,8,1792]{2,1,0:T(8,128)(2,1)S(1)} all-to-all(bf16[16,8,1792]{2,1,0:T(8,128)(2,1)S(1)} %pad_maximum_fusion.1), channel_id=1, replica_groups={{0,1,2,3,4,5,6,7,8,9,10,11,12,13,14,15},{16,17,18,19,20,21,22,23,24,25,..., dimensions={0} | all-to-all | bytes 917504 | tf_op jit(solution)/shard_map/all_to_all | solution.py:23
  207.3 16.6 %all_to_all.64 = bf16[4,64,1792]{2,1,0:T(8,128)(2,1)S(1)} all-to-all(bf16[4,64,1792]{2,1,0:T(8,128)(2,1)S(1)} %bitcast.196), channel_id=1, replica_groups={{0,16,32,48},{1,17,33,49},{2,18,34,50},{3,19,35,51},{4,20,36,52},{5,21,..., dimensions={0} | all-to-all | bytes 1835008 | tf_op jit(solution)/shard_map/all_to_all | solution.py:23
  232.1 3.4 %collective-permute-done.10 = f32[256,128]{0,1:T(8,128)S(1)} collective-permute-done((f32[256,128]{0,1:T(8,128)S(1)}, f32[256,128]{0,1:T(8,128)S(1)}, u32[]{:S(2)}, u32[]{:S(2)}) %collective-permute-start.10) | collective-permute-done | bytes 131104 | tf_op jit(solution)/shard_map/ppermute | solution.py:30
  235.6 3.1 collective-permute-start.11
  242.3 3.9 %collective-permute-done.12 = bf16[2,256,128]{1,2,0:T(8,128)(2,1)S(1)} collective-permute-done((bf16[2,256,128]{1,2,0:T(8,128)(2,1)S(1)}, bf16[2,256,128]{1,2,0:T(8,128)(2,1)S(1)}, u32[]{:S(2)}, u32[]{:S(2)}) %collective-permute-start.12) | collective-permute-done | bytes 131104 | tf_op jit(solution)/shard_map/ppermute | solution.py:30
  246.9 15.0 %all_to_all.65 = bf16[4,64,1792]{2,1,0:T(8,128)(2,1)S(1)} all-to-all(bf16[4,64,1792]{2,1,0:T(8,128)(2,1)S(1)} %bitcast.195), channel_id=1, replica_groups={{0,16,32,48},{1,17,33,49},{2,18,34,50},{3,19,35,51},{4,20,36,52},{5,21,..., dimensions={0} | all-to-all | bytes 1835008 | tf_op jit(solution)/shard_map/all_to_all | solution.py:23
  262.6 32.2 %all_to_all.66 = bf16[16,8,1792]{2,1,0:T(8,128)(2,1)S(1)} all-to-all(bf16[16,8,1792]{2,1,0:T(8,128)(2,1)S(1)} %bitcast.197), channel_id=1, replica_groups={{0,1,2,3,4,5,6,7,8,9,10,11,12,13,14,15},{16,17,18,19,20,21,22,23,24,25,..., dimensions={0} | all-to-all | bytes 917504 | tf_op jit(solution)/shard_map/all_to_all | solution.py:23
  294.8 5.7 %collective-permute-start.13 = (bf16[8,7168]{1,0:T(8,128)(2,1)S(1)}, bf16[8,7168]{1,0:T(8,128)(2,1)S(1)}, u32[]{:S(2)}, u32[]{:S(2)}) collective-permute-start(bf16[8,7168]{1,0:T(8,128)(2,1)S(1)} %fusion.52), channel_id=1, source_target_pairs={{0,72},{1,73},{2,74},{3,75},{4,76},{5,77},{6,78},{7,79},{8,64},{9,... | collective-permute-start | bytes 344072 | tf_op jit(solution)/shard_map/ppermute | solution.py:40
  300.5 13.3 %collective-permute-done.13 = bf16[8,7168]{1,0:T(8,128)(2,1)S(1)} collective-permute-done((bf16[8,7168]{1,0:T(8,128)(2,1)S(1)}, bf16[8,7168]{1,0:T(8,128)(2,1)S(1)}, u32[]{:S(2)}, u32[]{:S(2)}) %collective-permute-start.13) | collective-permute-done | bytes 114720 | tf_op jit(solution)/shard_map/ppermute | solution.py:40
  (99 shorter events, 57.1 us)
Async XLA Ops:
  0.0 5.7 %copy-start.5 = (f32[1,7168]{1,0:T(1,128)S(1)}, f32[1,7168]{1,0:T(1,128)}, u32[]{:S(2)}) copy-start(f32[1,7168]{1,0:T(1,128)} %param.7) | copy-start | bytes 86020
  0.0 6.4 %copy-start.3 = (bf16[1,8,7168]{2,1,0:T(8,128)(2,1)S(1)}, bf16[1,8,7168]{2,1,0:T(8,128)(2,1)}, u32[]{:S(2)}) copy-start(bf16[1,8,7168]{2,1,0:T(8,128)(2,1)} %param.6) | copy-start | bytes 344068
  0.0 6.7 %copy-start.7 = (f32[1,2,8,2]{2,3,1,0:T(2,128)S(1)}, f32[1,2,8,2]{2,3,1,0:T(2,128)}, u32[]{:S(2)}) copy-start(f32[1,2,8,2]{2,3,1,0:T(2,128)} %param.11) | copy-start | bytes 388
  0.0 6.8 %copy-start.6 = (s32[1,2,8,2]{2,3,1,0:T(2,128)S(1)}, s32[1,2,8,2]{2,3,1,0:T(2,128)}, u32[]{:S(2)}) copy-start(s32[1,2,8,2]{2,3,1,0:T(2,128)} %param.10) | copy-start | bytes 388
  2.6 20.8 %collective-permute-start = (bf16[2,1792,128]{2,1,0:T(8,128)(2,1)}, bf16[2,1792,128]{2,1,0:T(8,128)(2,1)S(1)}, u32[]{:S(2)}, u32[]{:S(2)}) collective-permute-start(bf16[2,1792,128]{2,1,0:T(8,128)(2,1)} %get-tuple-element.39), channel_id=1, source_target_pairs={{0,1},{1,0},{2,3},{3,2},{4,5},{5,4},{6,7},{7,6},{8,9},{9,8},{10,11... | collective-permute-start | bytes 2752520 | tf_op jit(solution)/shard_map/ppermute | solution.py:30
  7.7 37.7 %all-to-all-start = ((bf16[16,8,1920]{2,1,0:T(8,128)(2,1)}), bf16[16,8,1920]{2,1,0:T(8,128)(2,1)S(1)}, u32[]{:S(2)}, u32[]{:S(2)}) async-start(bf16[16,8,1920]{2,1,0:T(8,128)(2,1)} %maximum_maximum_fusion), calls=%async_computation | async-start | bytes 983040 | tf_op jit(solution)/shard_map/all_to_all | solution.py:23
  29.2 7.0 %collective-permute-start.1 = (bf16[2,128,1792]{2,1,0:T(8,128)(2,1)}, bf16[2,128,1792]{2,1,0:T(8,128)(2,1)}, u32[]{:S(2)}, u32[]{:S(2)}) collective-permute-start(bf16[2,128,1792]{2,1,0:T(8,128)(2,1)} %maximum_select_fusion.1), channel_id=1, source_target_pairs={{0,1},{1,0},{2,3},{3,2},{4,5},{5,4},{6,7},{7,6},{8,9},{9,8},{10,11... | collective-permute-start | bytes 2752520 | tf_op jit(solution)/shard_map/ppermute | solution.py:30
  31.4 26.7 %collective-permute-start.2 = (bf16[2,1792,128]{2,1,0:T(8,128)(2,1)}, bf16[2,1792,128]{2,1,0:T(8,128)(2,1)S(1)}, u32[]{:S(2)}, u32[]{:S(2)}) collective-permute-start(bf16[2,1792,128]{2,1,0:T(8,128)(2,1)} %get-tuple-element.15), channel_id=1, source_target_pairs={{0,2},{1,3},{2,0},{3,1},{4,6},{5,7},{6,4},{7,5},{8,10},{9,11},{10,... | collective-permute-start | bytes 2752520 | tf_op jit(solution)/shard_map/ppermute | solution.py:30
  38.8 39.0 %collective-permute-start.3 = (bf16[2,128,1792]{2,1,0:T(8,128)(2,1)}, bf16[2,128,1792]{2,1,0:T(8,128)(2,1)}, u32[]{:S(2)}, u32[]{:S(2)}) collective-permute-start(bf16[2,128,1792]{2,1,0:T(8,128)(2,1)} %get-tuple-element.27), channel_id=1, source_target_pairs={{0,2},{1,3},{2,0},{3,1},{4,6},{5,7},{6,4},{7,5},{8,10},{9,11},{10,... | collective-permute-start | bytes 2752520 | tf_op jit(solution)/shard_map/ppermute | solution.py:30
  47.5 18.0 %all-to-all-start.1 = ((bf16[4,64,1792]{2,1,0:T(8,128)(2,1)}), bf16[4,64,1792]{2,1,0:T(8,128)(2,1)S(1)}, u32[]{:S(2)}, u32[]{:S(2)}) async-start(bf16[4,64,1792]{2,1,0:T(8,128)(2,1)} %bitcast.25), calls=%async_computation.1 | async-start | bytes 1835008 | tf_op jit(solution)/shard_map/all_to_all | solution.py:23
  58.0 25.4 %copy-start = (bf16[2,1792,128]{2,1,0:T(8,128)(2,1)}, bf16[2,1792,128]{2,1,0:T(8,128)(2,1)S(1)}, u32[]{:S(2)}) copy-start(bf16[2,1792,128]{2,1,0:T(8,128)(2,1)S(1)} %collective-permute-done.2) | copy-start | bytes 2752516
  78.8 17.7 %copy-start.2 = (bf16[2,128,1792]{2,1,0:T(8,128)(2,1)S(1)}, bf16[2,128,1792]{2,1,0:T(8,128)(2,1)}, u32[]{:S(2)}) copy-start(bf16[2,128,1792]{2,1,0:T(8,128)(2,1)} %get-tuple-element.19) | copy-start | bytes 2752516
  78.8 4.2 %collective-permute-start.4 = (f32[2,256,128]{1,2,0:T(8,128)S(1)}, f32[2,256,128]{1,2,0:T(8,128)S(1)}, u32[]{:S(2)}, u32[]{:S(2)}) collective-permute-start(f32[2,256,128]{1,2,0:T(8,128)S(1)} %pad_maximum_fusion.4), channel_id=1, source_target_pairs={{0,1},{1,0},{2,3},{3,2},{4,5},{5,4},{6,7},{7,6},{8,9},{9,8},{10,11... | collective-permute-start | bytes 786440 | tf_op jit(solution)/shard_map/ppermute | solution.py:30
  83.4 6.6 %collective-permute-start.5 = (f32[256,128]{0,1:T(8,128)S(1)}, f32[256,128]{0,1:T(8,128)S(1)}, u32[]{:S(2)}, u32[]{:S(2)}) collective-permute-start(f32[256,128]{0,1:T(8,128)S(1)} %convolution_add_fusion), channel_id=1, source_target_pairs={{0,2},{1,3},{2,0},{3,1},{4,6},{5,7},{6,4},{7,5},{8,10},{9,11},{10,... | collective-permute-start | bytes 393224 | tf_op jit(solution)/shard_map/ppermute | solution.py:30
  90.6 4.0 %collective-permute-start.6 = (bf16[256,128]{0,1:T(8,128)(2,1)S(1)}, bf16[256,128]{0,1:T(8,128)(2,1)S(1)}, u32[]{:S(2)}, u32[]{:S(2)}) collective-permute-start(bf16[256,128]{0,1:T(8,128)(2,1)S(1)} %multiply_convert_fusion.2), channel_id=1, source_target_pairs={{0,1},{1,0},{2,3},{3,2},{4,5},{5,4},{6,7},{7,6},{8,9},{9,8},{10,11... | collective-permute-start | bytes 196616 | tf_op jit(solution)/shard_map/ppermute | solution.py:30
  94.6 6.6 %collective-permute-start.7 = (bf16[2,256,128]{1,2,0:T(8,128)(2,1)S(1)}, bf16[2,256,128]{1,2,0:T(8,128)(2,1)S(1)}, u32[]{:S(2)}, u32[]{:S(2)}) collective-permute-start(bf16[2,256,128]{1,2,0:T(8,128)(2,1)S(1)} %pad_maximum_fusion.6), channel_id=1, source_target_pairs={{0,2},{1,3},{2,0},{3,1},{4,6},{5,7},{6,4},{7,5},{8,10},{9,11},{10,... | collective-permute-start | bytes 393224 | tf_op jit(solution)/shard_map/ppermute | solution.py:30
  102.8 16.6 %all-to-all-start.2 = ((bf16[4,64,1792]{2,1,0:T(8,128)(2,1)}), bf16[4,64,1792]{2,1,0:T(8,128)(2,1)}, u32[]{:S(2)}, u32[]{:S(2)}) async-start(bf16[4,64,1792]{2,1,0:T(8,128)(2,1)} %bitcast.194), calls=%async_computation.2 | async-start | bytes 1835008 | tf_op jit(solution)/shard_map/all_to_all | solution.py:23
  158.1 19.0 %collective-permute-start.8 = (bf16[8,7168]{1,0:T(8,128)(2,1)S(1)}, bf16[8,7168]{1,0:T(8,128)(2,1)S(1)}, u32[]{:S(2)}, u32[]{:S(2)}) collective-permute-start(bf16[8,7168]{1,0:T(8,128)(2,1)S(1)} %fusion.54), channel_id=1, source_target_pairs={{0,72},{1,73},{2,74},{3,75},{4,76},{5,77},{6,78},{7,79},{8,64},{9,... | collective-permute-start | bytes 344072 | tf_op jit(solution)/shard_map/ppermute | solution.py:40
  207.3 17.1 %copy-start.1 = (bf16[2,1792,128]{2,1,0:T(8,128)(2,1)S(1)}, bf16[2,1792,128]{2,1,0:T(8,128)(2,1)}, u32[]{:S(2)}) copy-start(bf16[2,1792,128]{2,1,0:T(8,128)(2,1)} %copy-done) | copy-start | bytes 2752516
  224.8 3.7 %collective-permute-start.9 = (f32[2,256,128]{1,2,0:T(8,128)S(1)}, f32[2,256,128]{1,2,0:T(8,128)S(1)}, u32[]{:S(2)}, u32[]{:S(2)}) collective-permute-start(f32[2,256,128]{1,2,0:T(8,128)S(1)} %pad_maximum_fusion.5), channel_id=1, source_target_pairs={{0,1},{1,0},{2,3},{3,2},{4,5},{5,4},{6,7},{7,6},{8,9},{9,8},{10,11... | collective-permute-start | bytes 786440 | tf_op jit(solution)/shard_map/ppermute | solution.py:30
  228.9 6.6 %collective-permute-start.10 = (f32[256,128]{0,1:T(8,128)S(1)}, f32[256,128]{0,1:T(8,128)S(1)}, u32[]{:S(2)}, u32[]{:S(2)}) collective-permute-start(f32[256,128]{0,1:T(8,128)S(1)} %fusion.15), channel_id=1, source_target_pairs={{0,2},{1,3},{2,0},{3,1},{4,6},{5,7},{6,4},{7,5},{8,10},{9,11},{10,... | collective-permute-start | bytes 393224 | tf_op jit(solution)/shard_map/ppermute | solution.py:30
  235.6 4.0 %collective-permute-start.11 = (bf16[256,128]{0,1:T(8,128)(2,1)S(1)}, bf16[256,128]{0,1:T(8,128)(2,1)S(1)}, u32[]{:S(2)}, u32[]{:S(2)}) collective-permute-start(bf16[256,128]{0,1:T(8,128)(2,1)S(1)} %multiply_convert_fusion.1), channel_id=1, source_target_pairs={{0,1},{1,0},{2,3},{3,2},{4,5},{5,4},{6,7},{7,6},{8,9},{9,8},{10,11... | collective-permute-start | bytes 196616 | tf_op jit(solution)/shard_map/ppermute | solution.py:30
  239.6 6.6 %collective-permute-start.12 = (bf16[2,256,128]{1,2,0:T(8,128)(2,1)S(1)}, bf16[2,256,128]{1,2,0:T(8,128)(2,1)S(1)}, u32[]{:S(2)}, u32[]{:S(2)}) collective-permute-start(bf16[2,256,128]{1,2,0:T(8,128)(2,1)S(1)} %pad_maximum_fusion.7), channel_id=1, source_target_pairs={{0,2},{1,3},{2,0},{3,1},{4,6},{5,7},{6,4},{7,5},{8,10},{9,11},{10,... | collective-permute-start | bytes 393224 | tf_op jit(solution)/shard_map/ppermute | solution.py:30
  294.8 19.0 %collective-permute-start.13 = (bf16[8,7168]{1,0:T(8,128)(2,1)S(1)}, bf16[8,7168]{1,0:T(8,128)(2,1)S(1)}, u32[]{:S(2)}, u32[]{:S(2)}) collective-permute-start(bf16[8,7168]{1,0:T(8,128)(2,1)S(1)} %fusion.52), channel_id=1, source_target_pairs={{0,72},{1,73},{2,74},{3,75},{4,76},{5,77},{6,78},{7,79},{8,64},{9,... | collective-permute-start | bytes 344072 | tf_op jit(solution)/shard_map/ppermute | solution.py:40
  (1 other events, 1.0 us)
